TPU v7x, 32 devices: a whole 2x2x4 slice. The times are simulated.
32 devices in a mesh: mesh: 8 (over z, core), run: 4 (over y, x).
Axes of the slice: x: 2, y: 2, z: 4, core: 2. Of those that a mesh axis runs over, the one named last changes fastest.
Arguments:
- snapshots: bfloat16 [16384, 2048], P('mesh', 'run'), may hold values from -6 to 6
- block_cols: int32 [256, 16], P('mesh'), may hold values from 0 to 255, as said below
- mass_blocks: bfloat16 [256, 64, 1024], P('mesh'), as said below
Outputs:
- gram: float32 [2048, 2048], P('mesh', 'run')
Inputs may be any that keep to these rules, and one draw needn't show every extreme that they name: `block_cols`: block row b names 16 different block columns, the first of them b itself; all lie from 2 blocks before the first block row of shard b // 32 to 2 blocks after its last. In every shard but the first, its first block row names the block 2 before the shard; in every shard but the last, its last block row names the block 2 after it. `mass_blocks`: entry [b, i, k * 64 + j] is row i, column j of the k-th stored block of block row b, in the order of block_cols.
All inputs are finite; a program needn't handle non-finite values.
Results may differ from a plain program's by a relative error of at most 0.00056.
Values may be sent and summed in bfloat16 or wider, within the bound.
No kernel may reach another device: no remote copies, remote signals or barrier semaphores. Data moves between devices by JAX's collectives and lax.ppermute only.
A program may use at most 128 MiB of HBM per device.

v0:
```python
import jax
import jax.numpy as jnp
from jax import lax
from jax.sharding import PartitionSpec as P

BLK = 64
HB = 2


def extended(block, sides, width):
    for axis, dim in sides:
        count = lax.axis_size(axis)
        forward = [(i, i + 1) for i in range(count - 1)]
        backward = [(target, source) for source, target in forward]
        low = lax.ppermute(
            lax.slice_in_dim(block, block.shape[dim] - width, None, axis=dim), axis, forward
        )
        high = lax.ppermute(lax.slice_in_dim(block, 0, width, axis=dim), axis, backward)
        block = jnp.concatenate([low, block, high], axis=dim)
    return block


def contract_nodes(left_cols, right_cols):
    return lax.dot_general(
        left_cols, right_cols, (((0,), (0,)), ((), ())), preferred_element_type=jnp.float32
    )


def on_device(snapshots, block_cols, mass_blocks):
    node_count = snapshots.shape[0]
    column_count = snapshots.shape[1]
    blocks_here = node_count // BLK
    stored_count = block_cols.shape[1]
    rim_width = HB * BLK
    padded = extended(snapshots, (("mesh", 0),), rim_width)
    shard_index = lax.axis_index("mesh")
    local_cols = block_cols - (shard_index * blocks_here - HB)
    blocked = padded.reshape(blocks_here + 2 * HB, BLK, column_count)
    picked = blocked[local_cols].reshape(blocks_here, stored_count * BLK, column_count)
    weighted = jnp.einsum("bim,bmc->bic", mass_blocks, picked, preferred_element_type=jnp.float32)
    weighted = weighted.astype(jnp.bfloat16).reshape(node_count, column_count)
    gathered = lax.all_gather(snapshots, "run", axis=1, tiled=True)
    return lax.psum_scatter(
        contract_nodes(gathered, weighted), "mesh", scatter_dimension=0, tiled=True
    )


def solution(mesh):
    placed = (P("mesh", "run"), P("mesh", None), P("mesh", None, None))
    return jax.shard_map(
        on_device, mesh=mesh, in_specs=placed, out_specs=P("mesh", "run"), check_vma=False
    )
```

profile of v0, /device:TPU:0, one launch (start us, length us, event | category | flops | bytes accessed | tf_op | source)
XLA Modules:
  0.0 167.7 jit_solution(6542890312637564476)
XLA Ops:
  6.5 0.0 all-gather.2.cloned.1.call-start
  6.5 0.7 all-gather.2.cloned.1.call-update
  7.3 0.0 reduce-scatter.2.cloned.1.call-start
  7.3 1.0 fusion
  8.3 2.4 %collective-permute-start = (bf16[128,512]{1,0:T(8,128)(2,1)S(1)}, bf16[128,512]{1,0:T(8,128)(2,1)S(1)}, u32[]{:S(2)}, u32[]{:S(2)}) collective-permute-start(bf16[128,512]{1,0:T(8,128)(2,1)S(1)} %get-tuple-element.5), channel_id=1, source_target_pairs={{0,4},{4,8},{8,12},{12,16},{16,20},{20,24},{24,28},{1,5},{5,9},{9,... | collective-permute-start | bytes 393224 | tf_op jit(solution)/shard_map/ppermute | solution.py:15
  10.7 1.3 collective-permute-start.1
  12.0 0.7 compare_select_fusion
  12.7 0.1 copy.5
  12.8 0.1 reshape.14
  12.9 0.0 collective-permute-done
  12.9 3.2 %collective-permute-done.1 = bf16[128,512]{1,0:T(8,128)(2,1)S(1)} collective-permute-done((bf16[128,512]{1,0:T(8,128)(2,1)S(1)}, bf16[128,512]{1,0:T(8,128)(2,1)S(1)}, u32[]{:S(2)}, u32[]{:S(2)}) %collective-permute-start.1) | collective-permute-done | bytes 131104 | tf_op jit(solution)/shard_map/ppermute | solution.py:18
  16.1 1.7 %pad_maximum_fusion = bf16[2304,512]{1,0:T(8,128)(2,1)S(1)} fusion(bf16[128,512]{1,0:T(8,128)(2,1)S(1)} %collective-permute-done.1, bf16[2048,512]{1,0:T(8,128)(2,1)} %param.3, bf16[128,512]{1,0:T(8,128)(2,1)S(1)} %collective-permute-done), kind=kLoop, calls=%fused_computation.2 | loop fusion | flops 7077888 | bytes 4718592 | tf_op jit(solution)/shard_map/concatenate | solution.py:19
  17.9 16.1 %gather_fusion = bf16[512,64,512]{2,1,0:T(8,128)(2,1)} fusion(bf16[36,64,512]{2,1,0:T(8,128)(2,1)S(1)} %bitcast.11, s32[1024]{0:T(1024)S(1)} %pad_clamp_fusion), kind=kCustom, calls=%fused_computation | custom fusion | bytes 67110912 | tf_op jit(solution)/shard_map/gather | solution.py:39
  34.0 17.2 %convolution_convert_fusion = bf16[32,512,64]{1,2,0:T(8,128)(2,1)S(1)} fusion(bf16[32,64,1024]{2,1,0:T(8,128)(2,1)} %param.5, bf16[32,1024,512]{2,1,0:T(8,128)(2,1)} %bitcast.12), kind=kOutput, calls=%fused_computation.3 | convolution fusion | flops 2148532224 | bytes 39845888 | tf_op jit(solution)/shard_map/bim,bmc->bic/dot_general | solution.py:40
  51.2 48.0 %all-gather.2.cloned.1.call-done = bf16[2048,2048]{1,0:T(8,128)(2,1)} async-done(((bf16[2048,512]{1,0:T(8,128)(2,1)}), bf16[2048,2048]{1,0:T(8,128)(2,1)}) %all-gather.2.cloned.1.call-update) | async-done | bytes 8388624 | tf_op jit(solution)/shard_map/all_gather | solution.py:42
  99.3 9.4 %convolution_bitcast_fusion = f32[2048,512]{0,1:T(8,128)} fusion(bf16[2048,512]{1,0:T(8,128)(2,1)S(1)} %bitcast.13, bf16[2048,2048]{1,0:T(8,128)(2,1)} %all-gather.2.cloned.1.call-done), kind=kOutput, calls=%fused_computation.1 | convolution fusion | flops 4294967296 | bytes 14680064 | tf_op jit(solution)/shard_map/dot_general | solution.py:24
  108.7 0.0 reduce-scatter.2.cloned.1.call-update
  108.7 50.1 %reduce-scatter.2.cloned.1.call-done = f32[256,512]{0,1:T(8,128)} async-done(((f32[2048,512]{0,1:T(8,128)}), f32[256,512]{0,1:T(8,128)}) %reduce-scatter.2.cloned.1.call-update) | async-done | bytes 524304 | tf_op jit(solution)/shard_map/reduce_scatter | solution.py:43
  158.8 2.0 %copy.6 = f32[256,512]{1,0:T(8,128)} copy(f32[256,512]{0,1:T(8,128)} %reduce-scatter.2.cloned.1.call-done) | data formatting | bytes 1048576 | tf_op jit(solution)/shard_map/reduce_scatter | solution.py:43
  (1 shorter events, 0.0 us)
Async XLA Ops:
  6.5 92.7 %all-gather.2.cloned.1.call-start = ((), (), s32[]{:S(2)}) async-start(), calls=%async_computation.1 | async-start | bytes 10485760 | tf_op jit(solution)/shard_map/all_gather | solution.py:42
  7.3 151.5 %reduce-scatter.2.cloned.1.call-start = ((), (), s32[]{:S(2)}) async-start(), calls=%async_computation.2 | async-start | bytes 4718592 | tf_op jit(solution)/shard_map/reduce_scatter | solution.py:43
  8.3 4.6 %collective-permute-start = (bf16[128,512]{1,0:T(8,128)(2,1)S(1)}, bf16[128,512]{1,0:T(8,128)(2,1)S(1)}, u32[]{:S(2)}, u32[]{:S(2)}) collective-permute-start(bf16[128,512]{1,0:T(8,128)(2,1)S(1)} %get-tuple-element.5), channel_id=1, source_target_pairs={{0,4},{4,8},{8,12},{12,16},{16,20},{20,24},{24,28},{1,5},{5,9},{9,... | collective-permute-start | bytes 393224 | tf_op jit(solution)/shard_map/ppermute | solution.py:15
  10.7 5.4 %collective-permute-start.1 = (bf16[128,512]{1,0:T(8,128)(2,1)S(1)}, bf16[128,512]{1,0:T(8,128)(2,1)S(1)}, u32[]{:S(2)}, u32[]{:S(2)}) collective-permute-start(bf16[128,512]{1,0:T(8,128)(2,1)S(1)} %get-tuple-element.6), channel_id=1, source_target_pairs={{4,0},{8,4},{12,8},{16,12},{20,16},{24,20},{28,24},{5,1},{9,5},{13... | collective-permute-start | bytes 393224 | tf_op jit(solution)/shard_map/ppermute | solution.py:18
Sparse Core Ops, SparseCore 0:
  9.2 90.0 all-gather.1
  108.8 49.8 reduce-scatter.1
where the time goes:
time: 168 us
  waiting for transfers between devices  102 us (61%)
  matrix products  26.7 us (16%)
  local copies, waits for them, and re-layouts  19.3 us (11%)
  between operations  13.4 us (8%)
  starting transfers between devices  3.74 us (2%)
  other arithmetic  2.46 us (1%)
    reduce_scatter x1, waiting for transfers between devices, on_device(): lax.psum_scatter(contract_nodes(gathered, weighted), 'mesh', scatter_dime...  50.1 us
    all_gather x1, waiting for transfers between devices, on_device(): gathered = lax.all_gather(snapshots, 'run', axis=1, tiled=True)  48 us
    dot_general x1, matrix products, on_device(): jnp.einsum('bim,bmc->bic', mass_blocks, picked, preferred_element_type=jn...  17.2 us
    gather x1, local copies, waits for them, and re-layouts, on_device(): blocked[local_cols].reshape(blocks_here, stored_count * BLK, column_count)  16.1 us
    dot_general x1, matrix products, contract_nodes(): lax.dot_general(left_cols, right_cols, (((0,), (0,)), ((), ())), preferre...  9.44 us
  transfers between devices with their start and end apart: 4, of which 3 were waited for; matrix products, arithmetic and copies ran while one was open for 22% of the time, Pallas kernels for 0%

commit v1 on v0

v1 whole, which is shorter than its diff:
```python
import functools

import jax
import jax.numpy as jnp
from jax import lax
from jax.experimental import pallas as pl
from jax.experimental.pallas import tpu as pltpu
from jax.sharding import PartitionSpec as P

HB = 2


def contract_nodes(left_cols, right_cols):
    return lax.dot_general(
        left_cols, right_cols, (((0,), (0,)), ((), ())), preferred_element_type=jnp.float32
    )


def weigh_body(places, group, blk, cols_ref, mass_ref, *refs):
    count = len(places)
    pieces, out_ref, rows_ref, sems = refs[:count], refs[count], refs[count + 1], refs[count + 2]
    step = pl.program_id(0)

    @pl.when(step == 0)
    def _():
        copies = [
            pltpu.make_async_copy(
                piece, rows_ref.at[r : r + piece.shape[0], c : c + piece.shape[1]], sems.at[i]
            )
            for i, (piece, (r, c)) in enumerate(zip(pieces, places))
        ]
        for copy in copies:
            copy.start()
        for copy in copies:
            copy.wait()

    for i in range(group):
        row = step * group + i
        picked = jnp.concatenate(
            [
                rows_ref[pl.ds(pl.multiple_of(cols_ref[row, k] * blk, blk), blk), :]
                for k in range(cols_ref.shape[1])
            ],
            axis=0,
        )
        product = jnp.dot(mass_ref[i], picked, preferred_element_type=jnp.float32)
        out_ref[i * blk : (i + 1) * blk, :] = product.astype(out_ref.dtype)


def weigh(local_cols, mass_blocks, pieces, places, width):
    block_rows, blk, stored = mass_blocks.shape
    group = next(g for g in (8, 4, 2, 1) if block_rows % g == 0)
    row_count = block_rows * blk + 2 * HB * blk
    spec = pltpu.PrefetchScalarGridSpec(
        num_scalar_prefetch=1,
        grid=(block_rows // group,),
        in_specs=[pl.BlockSpec((group, blk, stored), lambda g, cols: (g, 0, 0))]
        + [pl.BlockSpec(memory_space=pl.ANY)] * len(pieces),
        out_specs=pl.BlockSpec((group * blk, width), lambda g, cols: (g, 0)),
        scratch_shapes=[
            pltpu.VMEM((row_count, width), jnp.bfloat16),
            pltpu.SemaphoreType.DMA((len(pieces),)),
        ],
    )
    return pl.pallas_call(
        functools.partial(weigh_body, places, group, blk),
        grid_spec=spec,
        out_shape=jax.ShapeDtypeStruct((block_rows * blk, width), jnp.bfloat16),
        cost_estimate=pl.CostEstimate(
            flops=8 * block_rows * blk * stored * width,
            bytes_accessed=2 * (block_rows * blk * stored + 2 * row_count * width),
            transcendentals=0,
        ),
        name="weigh",
    )(local_cols, mass_blocks, *pieces)


def product_body(steps, pick_ref, *refs):
    keep_ref, send_ref, first_ref, second_ref = refs[-4:]
    left_a, left_b, w = refs[:3]
    extra = refs[3:5] if len(refs) == 9 else None
    step = pl.program_id(0)
    own = w.shape[1]

    def add(acc_ref, left, right, lo):
        part = contract_nodes(left[...], right[...])
        hi = lo + right.shape[1]

        @pl.when(step == 0)
        def _():
            acc_ref[:, lo:hi] = part

        @pl.when(step > 0)
        def _():
            acc_ref[:, lo:hi] += part

    add(first_ref, left_a, w, 0)
    add(second_ref, left_b, w, 0)
    if extra is not None:
        add(first_ref, left_a, extra[1], own)
        add(second_ref, left_b, extra[0], own)

    @pl.when((step == steps - 1) & (pick_ref[0] == 0))
    def _():
        keep_ref[...] = first_ref[...]
        send_ref[...] = second_ref[...]

    @pl.when((step == steps - 1) & (pick_ref[0] != 0))
    def _():
        keep_ref[...] = second_ref[...]
        send_ref[...] = first_ref[...]


def products(pick, left, w, extra=None):
    nodes, own = w.shape
    steps = next(s for s in (4, 2, 1) if nodes % s == 0)
    depth = nodes // steps
    if isinstance(left, tuple):
        width = left[0].shape[1]
        operands = [left[0], left[1], w]
        specs = [pl.BlockSpec((depth, width), lambda k, p: (k, 0))] * 2
    else:
        width = left.shape[1] // 2
        operands = [left, left, w]
        specs = [
            pl.BlockSpec((depth, width), lambda k, p: (k, 0)),
            pl.BlockSpec((depth, width), lambda k, p: (k, 1)),
        ]
    specs.append(pl.BlockSpec((depth, own), lambda k, p: (k, 0)))
    total = own
    if extra is not None:
        half = extra.shape[1] // 2
        total += half
        operands += [extra, extra]
        specs += [
            pl.BlockSpec((depth, half), lambda k, p: (k, 0)),
            pl.BlockSpec((depth, half), lambda k, p: (k, 1)),
        ]
    result = jax.ShapeDtypeStruct((width, total), jnp.float32)
    whole = pl.BlockSpec((width, total), lambda k, p: (0, 0))
    return pl.pallas_call(
        functools.partial(product_body, steps),
        grid_spec=pltpu.PrefetchScalarGridSpec(
            num_scalar_prefetch=1,
            grid=(steps,),
            in_specs=specs,
            out_specs=[whole, whole],
            scratch_shapes=[pltpu.VMEM((width, total), jnp.float32)] * 2,
        ),
        out_shape=[result, result],
        cost_estimate=pl.CostEstimate(
            flops=4 * nodes * width * total,
            bytes_accessed=2 * nodes * (2 * width + total) + 8 * width * total,
            transcendentals=0,
        ),
        name="products",
    )(pick, *operands)


LINE = {
    0: (((1, 0), (3, 2)), ((2, 0),)),
    1: (((0, 1), (3, 2)), ((2, 1),)),
    2: (((3, 2), (0, 1)), ((1, 2),)),
    3: (((2, 3), (0, 1)), ((1, 3),)),
}
X, Y = 1, 2


def everywhere(chips, runs):
    return [(z, c, q) for z in range(chips) for c in range(2) for q in range(runs)]


def exchange_plan(chips, runs):
    flat = lambda z, c, q: (2 * z + c) * runs + q
    across = lambda bit: [(q, q ^ bit) for q in range(runs)]
    cores = [(m, m ^ 1) for m in range(2 * chips)]

    def line(target, round_):
        return [
            (flat(s, c, q), flat(t, c, q))
            for c in range(2)
            for q in range(runs)
            for s, t in LINE[target(c, q)][round_]
        ]

    def corner(target, bit):
        return [
            (flat(target(c, q), c, q), flat(target(c, q), c, q ^ bit(c)))
            for c in range(2)
            for q in range(runs)
        ]

    return across, cores, line, corner


def on_square(snapshots, block_cols, mass_blocks):
    node_count, column_count = snapshots.shape
    blk = mass_blocks.shape[1]
    blocks_here = node_count // blk
    rim = HB * blk
    half = column_count // 2
    runs = lax.axis_size("run")
    chips = lax.axis_size("mesh") // 2
    both = ("mesh", "run")
    across, cores, line, corner = exchange_plan(chips, runs)
    shard = lax.axis_index("mesh")
    column = lax.axis_index("run")
    core, chip = shard % 2, shard // 2
    local_cols = block_cols - (shard * blocks_here - HB)

    def over_x(v):
        return lax.ppermute(v, "run", across(X))

    def over_y(v):
        return lax.ppermute(v, "run", across(Y))

    left, right = snapshots[:, :half], snapshots[:, half:]
    a1, b2 = over_x(left), over_y(right)
    shards = 2 * chips
    low = lax.ppermute(snapshots[-rim:], "mesh", [(i, i + 1) for i in range(shards - 1)])
    high = lax.ppermute(snapshots[:rim], "mesh", [(i + 1, i) for i in range(shards - 1)])
    rims = jnp.concatenate([low, high], axis=0)
    ra, rb = over_x(rims[:, :half]), over_y(rims[:, half:])
    left, right, ra, rb = lax.optimization_barrier((left, right, ra, rb))
    a2, b1 = over_x(right), over_y(left)

    top = rim + node_count
    w = weigh(
        local_cols, mass_blocks, [low, snapshots, high], [(0, 0), (rim, 0), (top, 0)], column_count
    )

    def summed(kept, sent, target):
        total = kept + lax.ppermute(sent, "mesh", cores)
        for round_ in range(2):
            total = total + lax.ppermute(total, both, line(target, round_))
        return total

    pick = core[None].astype(jnp.int32)
    own = summed(*products(pick, snapshots, w), lambda c, q: q)

    wx = weigh(
        local_cols,
        mass_blocks,
        [ra[:rim], a1, ra[rim:], rb[:rim], b2, rb[rim:]],
        [(0, 0), (rim, 0), (top, 0), (0, half), (rim, half), (top, half)],
        column_count,
    )

    def stage(a, b, core_a):
        pick_here = (core != core_a)[None].astype(jnp.int32)
        target = lambda c, q: q ^ (X if c == core_a else Y)
        total = summed(*products(pick_here, (a, b), w, wx), target)
        moved = lax.ppermute(
            total[:, column_count:], both, corner(target, lambda c: Y if c == core_a else X)
        )
        return total[:, :column_count], moved

    near1, far1 = stage(a1, b2, 0)
    near2, far2 = stage(a2, b1, 1)
    first = core == 0
    far = jnp.concatenate([jnp.where(first, far2, far1), jnp.where(first, far1, far2)], axis=1)
    near = jnp.where((chip == (column ^ X)) == first, near1, near2)
    return jnp.where(chip == column, own, jnp.where(chip == (column ^ (X | Y)), far, near))


def on_device(snapshots, block_cols, mass_blocks):
    node_count, column_count = snapshots.shape
    blk = mass_blocks.shape[1]
    blocks_here = node_count // blk
    rim = HB * blk
    shards = lax.axis_size("mesh")
    low = lax.ppermute(snapshots[-rim:], "mesh", [(i, i + 1) for i in range(shards - 1)])
    high = lax.ppermute(snapshots[:rim], "mesh", [(i + 1, i) for i in range(shards - 1)])
    local_cols = block_cols - (lax.axis_index("mesh") * blocks_here - HB)
    weighted = weigh(
        local_cols,
        mass_blocks,
        [low, snapshots, high],
        [(0, 0), (rim, 0), (rim + node_count, 0)],
        column_count,
    )
    gathered = lax.all_gather(snapshots, "run", axis=1, tiled=True)
    return lax.psum_scatter(
        contract_nodes(gathered, weighted), "mesh", scatter_dimension=0, tiled=True
    )


def solution(mesh):
    placed = (P("mesh", "run"), P("mesh", None), P("mesh", None, None))
    square = mesh.shape["run"] == 4 and mesh.shape["mesh"] == 8
    return jax.shard_map(
        on_square if square else on_device,
        mesh=mesh,
        in_specs=placed,
        out_specs=P("mesh", "run"),
        check_vma=False,
    )
```

time: 168 us -> 150 us (0.89)
  Pallas kernels: 0 us -> 44.4 us
  waiting for transfers between devices: 102 us -> 69.6 us
  matrix products: 26.7 us -> 0 us
  starting transfers between devices: 3.74 us -> 22.3 us
  between operations: 13.4 us -> 0.28 us
  local copies, waits for them, and re-layouts: 19.3 us -> 8.11 us
  other arithmetic: 2.46 us -> 4.4 us
    ppermute x2 -> x19, waiting for transfers between devices: 3.23 us -> 69.6 us  [the longest x6 53.3 us: summed(): total = total + lax.ppermute(total, both, line(target, round_))]
    reduce_scatter x1 -> x0, waiting for transfers between devices: 50.1 us -> none  [on_device(): lax.psum_scatter(contract_nodes(gathered, weighted), 'mesh', scatter_dime...]
    all_gather x1 -> x0, waiting for transfers between devices: 48 us -> none  [on_device(): gathered = lax.all_gather(snapshots, 'run', axis=1, tiled=True)]
    pallas_call x0 -> x5, Pallas kernels: none -> 44.4 us  [the longest x3 22.3 us: products(): pl.pallas_call(functools.partial(product_body, steps), grid_spec=pltpu.Pr...]
    dot_general x2 -> x0, matrix products: 26.7 us -> none  [the longest x1 17.2 us: on_device(): jnp.einsum('bim,bmc->bic', mass_blocks, picked, preferred_element_type=jn...]
    ppermute x2 -> x19, starting transfers between devices: 3.7 us -> 22.3 us  [the longest x6 9.04 us: summed(): total = total + lax.ppermute(total, both, line(target, round_))]
    gather x1 -> x0, local copies, waits for them, and re-layouts: 16.1 us -> none  [on_device(): blocked[local_cols].reshape(blocks_here, stored_count * BLK, column_count)]
    slice x1 -> x6, local copies, waits for them, and re-layouts: 0.99 us -> 4.76 us  [the longest x1 3.02 us: on_square(): left, right = (snapshots[:, :half], snapshots[:, half:])]
  transfers between devices with their start and end apart: 4 -> 19, of which waited for: 3 -> 8; matrix products, arithmetic and copies ran while one was open for 22% -> 5% of each run, Pallas kernels for 0% -> 30%
where the time goes in v1:
time: 150 us; the launch traced here: 149 us
  waiting for transfers between devices  69.6 us (46%)
  Pallas kernels  44.4 us (30%)
  starting transfers between devices  22.3 us (15%)
  local copies, waits for them, and re-layouts  8.11 us (5%)
  other arithmetic  4.4 us (3%)
    ppermute x6, waiting for transfers between devices, summed(): total = total + lax.ppermute(total, both, line(target, round_))  53.3 us
    pallas_call x3, Pallas kernels, products(): pl.pallas_call(functools.partial(product_body, steps), grid_spec=pltpu.Pr...  22.3 us
    pallas_call x2, Pallas kernels, weigh(): pl.pallas_call(functools.partial(weigh_body, places, group, blk), grid_sp...  22 us
    ppermute x3, waiting for transfers between devices, over_x(): return lax.ppermute(v, 'run', across(X))  13.3 us
    ppermute x6, starting transfers between devices, summed(): total = total + lax.ppermute(total, both, line(target, round_))  9.04 us
    ppermute x3, starting transfers between devices, over_y(): return lax.ppermute(v, 'run', across(Y))  3.62 us
    unnamed x22, local copies, waits for them, and re-layouts  3.34 us
    slice x1, local copies, waits for them, and re-layouts, on_square(): left, right = (snapshots[:, :half], snapshots[:, half:])  3.02 us
  transfers between devices with their start and end apart: 19, of which 8 were waited for; matrix products, arithmetic and copies ran while one was open for 5% of the time, Pallas kernels for 30%

profile of v1, /device:TPU:0, one launch (start us, length us, event | category | flops | bytes accessed | tf_op | source)
XLA Modules:
  0.0 149.0 jit_solution(5506503809903075939)
XLA Ops:
  1.0 2.4 %collective-permute-start = (bf16[128,512]{1,0:T(8,128)(2,1)S(1)}, bf16[128,512]{1,0:T(8,128)(2,1)S(1)}, u32[]{:S(2)}, u32[]{:S(2)}) collective-permute-start(bf16[128,512]{1,0:T(8,128)(2,1)S(1)} %get-tuple-element.26), channel_id=1, source_target_pairs={{0,4},{4,8},{8,12},{12,16},{16,20},{20,24},{24,28},{1,5},{5,9},{9,... | collective-permute-start | bytes 393224 | tf_op jit(solution)/shard_map/ppermute | solution.py:220
  3.4 1.3 collective-permute-start.1
  4.7 3.0 %fusion.3 = (bf16[2048,256]{1,0:T(8,128)(2,1)}, bf16[2048,256]{1,0:T(8,128)(2,1)}) fusion(bf16[2048,512]{1,0:T(8,128)(2,1)} %refs_1_.3), kind=kLoop, calls=%fused_computation.9 | loop fusion | bytes 4194304 | tf_op jit(solution)/shard_map/slice | solution.py:217
  7.7 2.3 %collective-permute-start.9 = (bf16[2048,256]{1,0:T(8,128)(2,1)}, bf16[2048,256]{1,0:T(8,128)(2,1)S(1)}, u32[]{:S(2)}, u32[]{:S(2)}) collective-permute-start(bf16[2048,256]{1,0:T(8,128)(2,1)} %get-tuple-element.18), channel_id=1, source_target_pairs={{0,1},{1,0},{2,3},{3,2},{4,5},{5,4},{6,7},{7,6},{8,9},{9,8},{10,11... | collective-permute-start | bytes 3145736 | tf_op jit(solution)/shard_map/ppermute | solution.py:212
  10.0 1.5 %collective-permute-start.10 = (bf16[2048,256]{1,0:T(8,128)(2,1)}, bf16[2048,256]{1,0:T(8,128)(2,1)S(1)}, u32[]{:S(2)}, u32[]{:S(2)}) collective-permute-start(bf16[2048,256]{1,0:T(8,128)(2,1)} %get-tuple-element.17), channel_id=1, source_target_pairs={{0,2},{1,3},{2,0},{3,1},{4,6},{5,7},{6,4},{7,5},{8,10},{9,11},{10,... | collective-permute-start | bytes 3145736 | tf_op jit(solution)/shard_map/ppermute | solution.py:215
  13.0 11.0 %weigh.2.refs_2_ = bf16[2048,512]{1,0:T(8,128)(2,1)} custom-call(s32[32,16]{1,0:T(8,128)} %broadcast_subtract_fusion.cols_ref, bf16[32,64,1024]{2,1,0:T(8,128)(2,1)} %mass_ref.3, bf16[128,512]{1,0:T(8,128)(2,1)} %copy-done.7, bf16[2048,512]{1,0:T(8,128)(2,1)} %refs_1_.3, bf16[128,512]{1,0:T(8,128)(2,1)} %copy-done.8), custom_call_target="tpu_custom_call" | custom-call | flops 8589934592 | bytes 8912896 | tf_op jit(solution)/shard_map/weigh/pallas_call | solution.py:65
  24.0 11.1 %collective-permute-done.5 = bf16[256,256]{1,0:T(8,128)(2,1)S(1)} collective-permute-done((bf16[256,256]{1,0:T(8,128)(2,1)S(1)}, bf16[256,256]{1,0:T(8,128)(2,1)S(1)}, u32[]{:S(2)}, u32[]{:S(2)}) %collective-permute-start.5) | collective-permute-done | bytes 131104 | tf_op jit(solution)/shard_map/ppermute | solution.py:212
  35.1 2.8 %collective-permute-done.6 = bf16[256,256]{1,0:T(8,128)(2,1)S(1)} collective-permute-done((bf16[256,256]{1,0:T(8,128)(2,1)S(1)}, bf16[256,256]{1,0:T(8,128)(2,1)S(1)}, u32[]{:S(2)}, u32[]{:S(2)}) %collective-permute-start.6) | collective-permute-done | bytes 131104 | tf_op jit(solution)/shard_map/ppermute | solution.py:215
  37.9 2.1 %collective-permute-start.8 = (bf16[2048,256]{1,0:T(8,128)(2,1)}, bf16[2048,256]{1,0:T(8,128)(2,1)}, u32[]{:S(2)}, u32[]{:S(2)}) collective-permute-start(bf16[2048,256]{1,0:T(8,128)(2,1)} %get-tuple-element.18), channel_id=1, source_target_pairs={{0,2},{1,3},{2,0},{3,1},{4,6},{5,7},{6,4},{7,5},{8,10},{9,11},{10,... | collective-permute-start | bytes 3145736 | tf_op jit(solution)/shard_map/ppermute | solution.py:215
  42.0 11.0 %weigh.3.refs_3_.refs_4_ = bf16[2048,512]{1,0:T(8,128)(2,1)} custom-call(s32[32,16]{1,0:T(8,128)} %broadcast_subtract_fusion.cols_ref, bf16[32,64,1024]{2,1,0:T(8,128)(2,1)} %mass_ref.3, bf16[128,256]{1,0:T(8,128)(2,1)} %get-tuple-element.37.refs_0_, bf16[2048,256]{1,0:T(8,128)(2,1)} %copy-done, bf16[128,256]{1,0:T(8,128)(2,1)} %get-tuple-element.38.refs_2_, ...), custom_call_target="tpu_custom_call" | custom-call | flops 8589934592 | bytes 8912896 | tf_op jit(solution)/shard_map/weigh/pallas_call | solution.py:65
  53.1 8.2 %products.5 = (f32[256,768]{1,0:T(8,128)}, f32[256,768]{1,0:T(8,128)}) custom-call(s32[1]{0:T(128)} %bitcast.2.pick_ref, bf16[2048,256]{1,0:T(8,128)(2,1)} %copy-done, bf16[2048,256]{1,0:T(8,128)(2,1)} %copy-done.1, bf16[2048,512]{1,0:T(8,128)(2,1)} %weigh.2.refs_2_, bf16[2048,512]{1,0:T(8,128)(2,1)} %weigh.3.refs_3_.refs_4_, ...), custom_call_target="tpu_custom_call" | custom-call | flops 1610612736 | bytes 6815744 | tf_op jit(solution)/shard_map/products/pallas_call | solution.py:141
  61.8 2.2 %collective-permute-done.7.refs_0_ = bf16[2048,256]{1,0:T(8,128)(2,1)S(1)} collective-permute-done((bf16[2048,256]{1,0:T(8,128)(2,1)}, bf16[2048,256]{1,0:T(8,128)(2,1)S(1)}, u32[]{:S(2)}, u32[]{:S(2)}) %collective-permute-start.7) | collective-permute-done | bytes 1048608 | tf_op jit(solution)/shard_map/ppermute | solution.py:212
  65.0 8.4 %products.4 = (f32[256,768]{1,0:T(8,128)}, f32[256,768]{1,0:T(8,128)}) custom-call(s32[1]{0:T(128)} %bitcast.1.pick_ref, bf16[2048,256]{1,0:T(8,128)(2,1)} %copy-done.2, bf16[2048,256]{1,0:T(8,128)(2,1)} %collective-permute-done.8.refs_1_, bf16[2048,512]{1,0:T(8,128)(2,1)} %weigh.2.refs_2_, bf16[2048,512]{1,0:T(8,128)(2,1)} %weigh.3.refs_3_.refs_4_, ...), custom_call_target="tpu_custom_call" | custom-call | flops 1610612736 | bytes 6815744 | tf_op jit(solution)/shard_map/products/pallas_call | solution.py:141
  74.6 1.2 add.40
  75.8 3.7 %collective-permute-start.16 = (f32[256,768]{1,0:T(8,128)S(1)}, f32[256,768]{1,0:T(8,128)S(1)}, u32[]{:S(2)}, u32[]{:S(2)}) collective-permute-start(f32[256,768]{1,0:T(8,128)S(1)} %add.40), channel_id=1, source_target_pairs={{0,8},{24,16},{9,1},{25,17},{18,26},{2,10},{27,19},{3,11},{28,20},... | collective-permute-start | bytes 2359304 | tf_op jit(solution)/shard_map/ppermute | solution.py:235
  79.7 1.3 collective-permute-start.12
  81.0 5.8 %products.3 = (f32[256,512]{1,0:T(8,128)}, f32[256,512]{1,0:T(8,128)}) custom-call(s32[1]{0:T(128)} %bitcast.pick_ref, bf16[2048,512]{1,0:T(8,128)(2,1)} %refs_1_.3, bf16[2048,512]{1,0:T(8,128)(2,1)} %refs_1_.3, bf16[2048,512]{1,0:T(8,128)(2,1)} %weigh.2.refs_2_), custom_call_target="tpu_custom_call" | custom-call | flops 1073741824 | bytes 5242880 | tf_op jit(solution)/shard_map/products/pallas_call | solution.py:141
  87.0 10.4 %collective-permute-done.16 = f32[256,768]{1,0:T(8,128)S(1)} collective-permute-done((f32[256,768]{1,0:T(8,128)S(1)}, f32[256,768]{1,0:T(8,128)S(1)}, u32[]{:S(2)}, u32[]{:S(2)}) %collective-permute-start.16) | collective-permute-done | bytes 786464 | tf_op jit(solution)/shard_map/ppermute | solution.py:235
  98.2 15.6 %collective-permute-done.12 = f32[256,768]{1,0:T(8,128)S(1)} collective-permute-done((f32[256,768]{1,0:T(8,128)S(1)}, f32[256,768]{1,0:T(8,128)S(1)}, u32[]{:S(2)}, u32[]{:S(2)}) %collective-permute-start.12) | collective-permute-done | bytes 786464 | tf_op jit(solution)/shard_map/ppermute | solution.py:235
  114.7 1.3 collective-permute-start.3
  116.0 14.8 %collective-permute-done.3 = f32[256,512]{1,0:T(8,128)S(1)} collective-permute-done((f32[256,512]{1,0:T(8,128)S(1)}, f32[256,512]{1,0:T(8,128)S(1)}, u32[]{:S(2)}, u32[]{:S(2)}) %collective-permute-start.3) | collective-permute-done | bytes 524320 | tf_op jit(solution)/shard_map/ppermute | solution.py:235
  130.8 1.3 collective-permute-start.4
  133.1 1.4 collective-permute-start.14
  135.5 12.6 %collective-permute-done.4 = f32[256,512]{1,0:T(8,128)S(1)} collective-permute-done((f32[256,512]{1,0:T(8,128)S(1)}, f32[256,512]{1,0:T(8,128)S(1)}, u32[]{:S(2)}, u32[]{:S(2)}) %collective-permute-start.4) | collective-permute-done | bytes 524320 | tf_op jit(solution)/shard_map/ppermute | solution.py:235
  (59 shorter events, 12.1 us)
Async XLA Ops:
  1.0 11.3 %collective-permute-start = (bf16[128,512]{1,0:T(8,128)(2,1)S(1)}, bf16[128,512]{1,0:T(8,128)(2,1)S(1)}, u32[]{:S(2)}, u32[]{:S(2)}) collective-permute-start(bf16[128,512]{1,0:T(8,128)(2,1)S(1)} %get-tuple-element.26), channel_id=1, source_target_pairs={{0,4},{4,8},{8,12},{12,16},{16,20},{20,24},{24,28},{1,5},{5,9},{9,... | collective-permute-start | bytes 393224 | tf_op jit(solution)/shard_map/ppermute | solution.py:220
  3.4 8.2 %copy-start.9 = (s32[32,16]{0,1:T(8,128)S(1)}, s32[32,16]{0,1:T(8,128)}, u32[]{:S(2)}) copy-start(s32[32,16]{0,1:T(8,128)} %param.4) | copy-start | bytes 6148
  3.4 8.9 %collective-permute-start.1 = (bf16[128,512]{1,0:T(8,128)(2,1)S(1)}, bf16[128,512]{1,0:T(8,128)(2,1)S(1)}, u32[]{:S(2)}, u32[]{:S(2)}) collective-permute-start(bf16[128,512]{1,0:T(8,128)(2,1)S(1)} %get-tuple-element.25), channel_id=1, source_target_pairs={{4,0},{8,4},{12,8},{16,12},{20,16},{24,20},{28,24},{5,1},{9,5},{13... | collective-permute-start | bytes 393224 | tf_op jit(solution)/shard_map/ppermute | solution.py:221
  7.7 32.9 %collective-permute-start.9 = (bf16[2048,256]{1,0:T(8,128)(2,1)}, bf16[2048,256]{1,0:T(8,128)(2,1)S(1)}, u32[]{:S(2)}, u32[]{:S(2)}) collective-permute-start(bf16[2048,256]{1,0:T(8,128)(2,1)} %get-tuple-element.18), channel_id=1, source_target_pairs={{0,1},{1,0},{2,3},{3,2},{4,5},{5,4},{6,7},{7,6},{8,9},{9,8},{10,11... | collective-permute-start | bytes 3145736 | tf_op jit(solution)/shard_map/ppermute | solution.py:212
  10.0 30.6 %collective-permute-start.10 = (bf16[2048,256]{1,0:T(8,128)(2,1)}, bf16[2048,256]{1,0:T(8,128)(2,1)S(1)}, u32[]{:S(2)}, u32[]{:S(2)}) collective-permute-start(bf16[2048,256]{1,0:T(8,128)(2,1)} %get-tuple-element.17), channel_id=1, source_target_pairs={{0,2},{1,3},{2,0},{3,1},{4,6},{5,7},{6,4},{7,5},{8,10},{9,11},{10,... | collective-permute-start | bytes 3145736 | tf_op jit(solution)/shard_map/ppermute | solution.py:215
  12.3 22.8 %collective-permute-start.5 = (bf16[256,256]{1,0:T(8,128)(2,1)S(1)}, bf16[256,256]{1,0:T(8,128)(2,1)S(1)}, u32[]{:S(2)}, u32[]{:S(2)}) collective-permute-start(bf16[256,256]{1,0:T(8,128)(2,1)S(1)} %get-tuple-element.32), channel_id=1, source_target_pairs={{0,1},{1,0},{2,3},{3,2},{4,5},{5,4},{6,7},{7,6},{8,9},{9,8},{10,11... | collective-permute-start | bytes 393224 | tf_op jit(solution)/shard_map/ppermute | solution.py:212
  12.9 24.9 %collective-permute-start.6 = (bf16[256,256]{1,0:T(8,128)(2,1)S(1)}, bf16[256,256]{1,0:T(8,128)(2,1)S(1)}, u32[]{:S(2)}, u32[]{:S(2)}) collective-permute-start(bf16[256,256]{1,0:T(8,128)(2,1)S(1)} %get-tuple-element.31), channel_id=1, source_target_pairs={{0,2},{1,3},{2,0},{3,1},{4,6},{5,7},{6,4},{7,5},{8,10},{9,11},{10,... | collective-permute-start | bytes 393224 | tf_op jit(solution)/shard_map/ppermute | solution.py:215
  37.9 26.2 %collective-permute-start.7 = (bf16[2048,256]{1,0:T(8,128)(2,1)}, bf16[2048,256]{1,0:T(8,128)(2,1)S(1)}, u32[]{:S(2)}, u32[]{:S(2)}) collective-permute-start(bf16[2048,256]{1,0:T(8,128)(2,1)} %get-tuple-element.17), channel_id=1, source_target_pairs={{0,1},{1,0},{2,3},{3,2},{4,5},{5,4},{6,7},{7,6},{8,9},{9,8},{10,11... | collective-permute-start | bytes 3145736 | tf_op jit(solution)/shard_map/ppermute | solution.py:212
  37.9 26.3 %collective-permute-start.8 = (bf16[2048,256]{1,0:T(8,128)(2,1)}, bf16[2048,256]{1,0:T(8,128)(2,1)}, u32[]{:S(2)}, u32[]{:S(2)}) collective-permute-start(bf16[2048,256]{1,0:T(8,128)(2,1)} %get-tuple-element.18), channel_id=1, source_target_pairs={{0,2},{1,3},{2,0},{3,1},{4,6},{5,7},{6,4},{7,5},{8,10},{9,11},{10,... | collective-permute-start | bytes 3145736 | tf_op jit(solution)/shard_map/ppermute | solution.py:215
  40.6 1.4 copy-start.1
  61.3 12.4 %collective-permute-start.15 = (f32[256,768]{1,0:T(8,128)}, f32[256,768]{1,0:T(8,128)S(1)}, u32[]{:S(2)}, u32[]{:S(2)}) collective-permute-start(f32[256,768]{1,0:T(8,128)} %get-tuple-element.24), channel_id=1, source_target_pairs={{0,4},{4,0},{8,12},{12,8},{16,20},{20,16},{24,28},{28,24},{1,5},{5... | collective-permute-start | bytes 2359304 | tf_op jit(solution)/shard_map/ppermute | solution.py:233
  65.0 9.6 %copy-start.3 = (f32[256,768]{1,0:T(8,128)S(1)}, f32[256,768]{1,0:T(8,128)}, u32[]{:S(2)}) copy-start(f32[256,768]{1,0:T(8,128)} %get-tuple-element.23) | copy-start | bytes 2359300
  73.4 6.2 %copy-start.5 = (f32[256,768]{1,0:T(8,128)S(1)}, f32[256,768]{1,0:T(8,128)}, u32[]{:S(2)}) copy-start(f32[256,768]{1,0:T(8,128)} %get-tuple-element.21) | copy-start | bytes 2359300
  73.4 6.2 %collective-permute-start.11 = (f32[256,768]{1,0:T(8,128)}, f32[256,768]{1,0:T(8,128)S(1)}, u32[]{:S(2)}, u32[]{:S(2)}) collective-permute-start(f32[256,768]{1,0:T(8,128)} %get-tuple-element.22), channel_id=1, source_target_pairs={{0,4},{4,0},{8,12},{12,8},{16,20},{20,16},{24,28},{28,24},{1,5},{5... | collective-permute-start | bytes 2359304 | tf_op jit(solution)/shard_map/ppermute | solution.py:233
  75.8 21.6 %collective-permute-start.16 = (f32[256,768]{1,0:T(8,128)S(1)}, f32[256,768]{1,0:T(8,128)S(1)}, u32[]{:S(2)}, u32[]{:S(2)}) collective-permute-start(f32[256,768]{1,0:T(8,128)S(1)} %add.40), channel_id=1, source_target_pairs={{0,8},{24,16},{9,1},{25,17},{18,26},{2,10},{27,19},{3,11},{28,20},... | collective-permute-start | bytes 2359304 | tf_op jit(solution)/shard_map/ppermute | solution.py:235
  79.7 34.1 %collective-permute-start.12 = (f32[256,768]{1,0:T(8,128)S(1)}, f32[256,768]{1,0:T(8,128)S(1)}, u32[]{:S(2)}, u32[]{:S(2)}) collective-permute-start(f32[256,768]{1,0:T(8,128)S(1)} %add.37), channel_id=1, source_target_pairs={{24,16},{0,8},{17,25},{1,9},{10,2},{26,18},{3,11},{27,19},{4,12},{... | collective-permute-start | bytes 2359304 | tf_op jit(solution)/shard_map/ppermute | solution.py:235
  86.8 27.8 %copy-start.6 = (f32[256,512]{1,0:T(8,128)S(1)}, f32[256,512]{1,0:T(8,128)}, u32[]{:S(2)}) copy-start(f32[256,512]{1,0:T(8,128)} %get-tuple-element.15) | copy-start | bytes 1572868
  86.8 27.8 %collective-permute-start.2 = (f32[256,512]{1,0:T(8,128)}, f32[256,512]{1,0:T(8,128)S(1)}, u32[]{:S(2)}, u32[]{:S(2)}) collective-permute-start(f32[256,512]{1,0:T(8,128)} %get-tuple-element.16), channel_id=1, source_target_pairs={{0,4},{4,0},{8,12},{12,8},{16,20},{20,16},{24,28},{28,24},{1,5},{5... | collective-permute-start | bytes 1572872 | tf_op jit(solution)/shard_map/ppermute | solution.py:233
  97.5 34.7 %collective-permute-start.17 = (f32[256,768]{1,0:T(8,128)S(1)}, f32[256,768]{1,0:T(8,128)S(1)}, u32[]{:S(2)}, u32[]{:S(2)}) collective-permute-start(f32[256,768]{1,0:T(8,128)S(1)} %add.41), channel_id=1, source_target_pairs={{16,8},{17,1},{10,26},{11,19},{12,20},{13,29},{22,6},{23,15}} | collective-permute-start | bytes 2359304 | tf_op jit(solution)/shard_map/ppermute | solution.py:235
  113.9 19.1 %collective-permute-start.13 = (f32[256,768]{1,0:T(8,128)S(1)}, f32[256,768]{1,0:T(8,128)S(1)}, u32[]{:S(2)}, u32[]{:S(2)}) collective-permute-start(f32[256,768]{1,0:T(8,128)S(1)} %add.38), channel_id=1, source_target_pairs={{8,16},{9,25},{18,2},{19,11},{20,12},{21,5},{14,30},{15,23}} | collective-permute-start | bytes 2359304 | tf_op jit(solution)/shard_map/ppermute | solution.py:235
  114.7 16.1 %collective-permute-start.3 = (f32[256,512]{1,0:T(8,128)S(1)}, f32[256,512]{1,0:T(8,128)S(1)}, u32[]{:S(2)}, u32[]{:S(2)}) collective-permute-start(f32[256,512]{1,0:T(8,128)S(1)} %add.34), channel_id=1, source_target_pairs={{8,0},{24,16},{1,9},{25,17},{26,18},{2,10},{19,27},{3,11},{12,4},{... | collective-permute-start | bytes 1572872 | tf_op jit(solution)/shard_map/ppermute | solution.py:235
  130.8 17.2 %collective-permute-start.4 = (f32[256,512]{1,0:T(8,128)S(1)}, f32[256,512]{1,0:T(8,128)S(1)}, u32[]{:S(2)}, u32[]{:S(2)}) collective-permute-start(f32[256,512]{1,0:T(8,128)S(1)} %add.35), channel_id=1, source_target_pairs={{16,0},{17,9},{10,18},{11,27},{20,4},{21,13},{14,22},{15,31}} | collective-permute-start | bytes 1572872 | tf_op jit(solution)/shard_map/ppermute | solution.py:235
  132.3 2.2 %collective-permute-start.18 = (f32[256,256]{1,0:T(8,128)S(1)}, f32[256,256]{1,0:T(8,128)S(1)}, u32[]{:S(2)}, u32[]{:S(2)}) collective-permute-start(f32[256,256]{1,0:T(8,128)S(1)} %slice.59), channel_id=1, source_target_pairs={{8,10},{1,3},{26,24},{19,17},{20,21},{29,28},{6,7},{15,14}} | collective-permute-start | bytes 786440 | tf_op jit(solution)/shard_map/ppermute | solution.py:253
  133.1 1.4 collective-permute-start.14
  (5 other events, 4.5 us)

commit v2 on v0

v2 whole, which is shorter than its diff:
```python
import functools

import jax
import jax.numpy as jnp
from jax import lax
from jax.experimental import pallas as pl
from jax.experimental.pallas import tpu as pltpu
from jax.sharding import PartitionSpec as P


HB = 2


def contract_nodes(left_cols, right_cols):
    return lax.dot_general(
        left_cols, right_cols, (((0,), (0,)), ((), ())), preferred_element_type=jnp.float32
    )


def span(start, size):
    return slice(start, start + size)


def fused_body(plan, *refs):
    refs = list(refs)
    cols_ref, pick_ref = refs.pop(0), refs.pop(0)
    mass_hbm = refs.pop(0) if plan["weighs"] else None
    pieces = [refs.pop(0) for _ in range(plan["count"])]
    own_hbm = refs.pop(0) if plan["own"] else None
    extra_hbm = refs.pop(0) if plan["extra"] else None
    made_ref = refs.pop(0) if plan["weighs"] else None
    keep_ref, send_ref = (refs.pop(0), refs.pop(0)) if plan["multiplies"] else (None, None)
    rows_ref = refs.pop(0)
    mass_ref = refs.pop(0) if plan["weighs"] else None
    own_ref = refs.pop(0) if plan["own"] else None
    extra_ref = refs.pop(0) if plan["extra"] else None
    sems = refs.pop(0)
    blk, rim, half = plan["blk"], plan["rim"], plan["half"]

    used = iter(range(64))
    fetch = lambda source, target: pltpu.make_async_copy(source, target, sems.at[next(used)])
    rows_in = [
        fetch(pieces[p].at[span(r, n), :], rows_ref.at[span(to, n), span(lane, pieces[p].shape[1])])
        for p, r, n, to, lane in plan["places"]
    ]
    mass_in, own_in, extra_in = [], [], []
    if plan["weighs"]:
        parts = plan["parts"]
        size = mass_ref.shape[0] // parts
        mass_in = [
            fetch(mass_hbm.at[span(i * size, size)], mass_ref.at[span(i * size, size)])
            for i in range(parts)
        ]
    if plan["own"]:
        own_in = [fetch(own_hbm, own_ref)]
    if plan["extra"]:
        extra_in = [fetch(extra_hbm, extra_ref)]
    for copy in rows_in + mass_in + own_in + extra_in:
        copy.start()
    for copy in rows_in:
        copy.wait()

    if plan["weighs"]:
        for row in range(mass_ref.shape[0]):
            if row % size == 0:
                mass_in[row // size].wait()
            picked = jnp.concatenate(
                [
                    rows_ref[pl.ds(pl.multiple_of(cols_ref[row, k] * blk, blk), blk), :]
                    for k in range(cols_ref.shape[1])
                ],
                axis=0,
            )
            product = jnp.dot(mass_ref[row], picked, preferred_element_type=jnp.float32)
            made_ref[row * blk : (row + 1) * blk, :] = product.astype(made_ref.dtype)
    for copy in own_in + extra_in:
        copy.wait()

    if plan["multiplies"]:
        w_ref = own_ref if plan["own"] else made_ref
        x_ref = extra_ref if plan["extra"] else (made_ref if plan["own"] else None)
        own = w_ref.shape[1]
        nodes = w_ref.shape[0]
        lead = rim if plan["padded"] else 0
        for target, first in ((keep_ref, pick_ref[0]), (send_ref, 1 - pick_ref[0])):
            left = rows_ref[span(lead, nodes), pl.ds(pl.multiple_of(first * half, half), half)]
            target[:, :own] = contract_nodes(left, w_ref[...])
            if x_ref is not None:
                right = x_ref[:, pl.ds(pl.multiple_of((1 - first) * half, half), half)]
                target[:, own:] = contract_nodes(left, right)


def fused(local_cols, pick, mass_blocks, pieces, places, own=None, extra=None, weighs=True, multiplies=True):
    block_rows, blk, stored = mass_blocks.shape
    rim = HB * blk
    nodes = block_rows * blk
    width = max(lane + pieces[p].shape[1] for p, _, _, _, lane in places)
    half = width // 2
    row_count = max(to + n for _, _, n, to, _ in places)
    parts = 4 if block_rows % 4 == 0 else 1
    plan = dict(
        blk=blk, rim=rim, half=half, weighs=weighs, multiplies=multiplies, places=places,
        count=len(pieces), own=own is not None, extra=extra is not None,
        padded=row_count > nodes, parts=parts,
    )
    total = width + half if own is not None else width
    operands, scratch = [], [pltpu.VMEM((row_count, width), jnp.bfloat16)]
    outs, flops = [], 0
    if weighs:
        operands.append(mass_blocks)
        scratch.append(pltpu.VMEM(mass_blocks.shape, jnp.bfloat16))
        outs.append(jax.ShapeDtypeStruct((nodes, width), jnp.bfloat16))
        flops += 8 * nodes * stored * width
    operands += pieces
    for w in (own, extra):
        if w is not None:
            operands.append(w)
            scratch.append(pltpu.VMEM(w.shape, jnp.bfloat16))
    if multiplies:
        outs += [jax.ShapeDtypeStruct((half, total), jnp.float32)] * 2
        flops += 4 * nodes * half * total
    scratch.append(pltpu.SemaphoreType.DMA((len(places) + parts + 2,)))
    return pl.pallas_call(
        functools.partial(fused_body, plan),
        grid_spec=pltpu.PrefetchScalarGridSpec(
            num_scalar_prefetch=2,
            grid=(),
            in_specs=[pl.BlockSpec(memory_space=pl.ANY)] * len(operands),
            out_specs=[pl.BlockSpec(memory_space=pltpu.VMEM)] * len(outs),
            scratch_shapes=scratch,
        ),
        out_shape=outs,
        cost_estimate=pl.CostEstimate(flops=flops, bytes_accessed=8 << 20, transcendentals=0),
    )(local_cols, pick, *operands)


TOP = 32000.0
EXTRA = 16


def encoded(values):
    peak = jnp.maximum(jnp.max(jnp.abs(values), axis=0, keepdims=True), 1e-30)
    power = jnp.ceil(jnp.log2(peak))
    whole = jnp.round(values * (jnp.exp2(-power) * TOP)).astype(jnp.int32)
    return whole.astype(jnp.int16), power.astype(jnp.int32)


def put_encoded(target, values):
    rows, width = values.shape
    whole, power = encoded(values)
    target[:rows, :] = whole
    target[rows:, :] = jnp.broadcast_to(power, (EXTRA, width)).astype(jnp.int16)


def decoded(source, lo, hi):
    rows = source.shape[0] - EXTRA
    power = source[rows:, lo:hi].astype(jnp.int32).astype(jnp.float32)[:1]
    whole = source[:rows, lo:hi].astype(jnp.int32).astype(jnp.float32)
    return whole * (jnp.exp2(power) * (1.0 / TOP))


def merge_body(kept_ref, came_ref, total_ref, coded_ref):
    total = kept_ref[...] + came_ref[...]
    total_ref[...] = total
    put_encoded(coded_ref, total)


def merge(kept, came):
    rows, width = kept.shape
    return pl.pallas_call(
        merge_body,
        out_shape=[
            jax.ShapeDtypeStruct((rows, width), jnp.float32),
            jax.ShapeDtypeStruct((rows + EXTRA, width), jnp.int16),
        ],
        cost_estimate=pl.CostEstimate(
            flops=8 * rows * width, bytes_accessed=14 * rows * width, transcendentals=0
        ),
    )(kept, came)


def turn_body(own, flag_ref, total_ref, came_ref, near_ref, leg_ref, far_ref, coded_ref):
    width = total_ref.shape[1]
    total = total_ref[...] + decoded(came_ref, 0, width)
    near_ref[...] = total[:, :own]
    put_encoded(coded_ref, total)
    far_ref[...] = coded_ref[:, own:]
    half = width - own
    first = pl.multiple_of(flag_ref[0] * half, half)
    leg_ref[...] = coded_ref[:, pl.ds(first, own)]


def turn(flag, total, came, own):
    rows, width = total.shape
    coded = lambda columns: jax.ShapeDtypeStruct((rows + EXTRA, columns), jnp.int16)
    vmem = pl.BlockSpec(memory_space=pltpu.VMEM)
    return pl.pallas_call(
        functools.partial(turn_body, own),
        grid_spec=pltpu.PrefetchScalarGridSpec(
            num_scalar_prefetch=1,
            grid=(),
            in_specs=[vmem] * 2,
            out_specs=[vmem] * 3,
            scratch_shapes=[pltpu.VMEM((rows + EXTRA, width), jnp.int16)],
        ),
        out_shape=[jax.ShapeDtypeStruct((rows, own), jnp.float32), coded(own), coded(width - own)],
        cost_estimate=pl.CostEstimate(
            flops=8 * rows * width, bytes_accessed=12 * rows * width, transcendentals=0
        ),
    )(flag, total, came)


def close_body(case_ref, own, own_came, near1, leg1, far1, near2, leg2, far2, out_ref):
    width = out_ref.shape[1]
    half = width // 2
    case = case_ref[0]

    @pl.when(case == 0)
    def _():
        out_ref[...] = own[...] + own_came[...]

    for number, near, leg in ((1, near1, leg1), (2, near2, leg2)):

        @pl.when(case == number)
        def _():
            out_ref[...] = near[...] + decoded(leg, 0, width)

    first, second = (leg1, far1), (leg2, far2)
    for number, pair in ((3, (second, first)), (4, (first, second))):

        @pl.when(case == number)
        def _():
            for i, (leg, far) in enumerate(pair):
                out_ref[:, i * half : (i + 1) * half] = decoded(leg, half, width) + decoded(far, 0, half)


def close(case, *parts):
    vmem = pl.BlockSpec(memory_space=pltpu.VMEM)
    return pl.pallas_call(
        close_body,
        grid_spec=pltpu.PrefetchScalarGridSpec(
            num_scalar_prefetch=1, grid=(), in_specs=[vmem] * len(parts), out_specs=vmem
        ),
        out_shape=jax.ShapeDtypeStruct(parts[0].shape, jnp.float32),
        name="close",
    )(case, *parts)


LINE = {t: (((t ^ 1, t), (t ^ 3, t ^ 2)), ((t ^ 2, t),)) for t in range(4)}
X, Y = 1, 2


def is_traced(value):
    return not isinstance(value, int)


def exchange_plan(chips, runs):
    flat = lambda z, c, q: (2 * z + c) * runs + q
    across = lambda bit: [(q, q ^ bit) for q in range(runs)]
    cores = [(m, m ^ 1) for m in range(2 * chips)]

    def line(target, round_):
        return [
            (flat(s, c, q), flat(t, c, q))
            for c in range(2)
            for q in range(runs)
            for s, t in LINE[target(c, q)][round_]
        ]

    def corner(target, bit):
        return [
            (flat(target(c, q), c, q), flat(target(c, q), c, q ^ bit(c)))
            for c in range(2)
            for q in range(runs)
        ]

    def around(target, bit):
        return [
            (flat(s, c, q), flat(t, c, q ^ bit(c)))
            for c in range(2)
            for q in range(runs)
            for s, t in LINE[target(c, q)][1]
        ]

    return across, cores, line, corner, around


def on_square(snapshots, block_cols, mass_blocks):
    node_count, column_count = snapshots.shape
    blk = mass_blocks.shape[1]
    blocks_here = node_count // blk
    rim = HB * blk
    half = column_count // 2
    runs = lax.axis_size("run")
    chips = lax.axis_size("mesh") // 2
    both = ("mesh", "run")
    across, cores, line, corner, around = exchange_plan(chips, runs)
    shard = lax.axis_index("mesh")
    column = lax.axis_index("run")
    core, chip = shard % 2, shard // 2
    local_cols = block_cols - (shard * blocks_here - HB)

    def over_x(v):
        return lax.ppermute(v, "run", across(X))

    def over_y(v):
        return lax.ppermute(v, "run", across(Y))

    pick = core[None].astype(jnp.int32)
    shards = 2 * chips
    low = lax.ppermute(snapshots[-rim:], "mesh", [(i, i + 1) for i in range(shards - 1)])
    high = lax.ppermute(snapshots[:rim], "mesh", [(i + 1, i) for i in range(shards - 1)])
    left = snapshots[:, :half]
    a1 = over_x(left)
    right = lax.optimization_barrier((snapshots, left))[0][:, half:]
    b2 = over_y(right)
    rims = jnp.concatenate([low, high], axis=0)
    ra = over_x(rims[:, :half])
    rb = over_y(rims[:, half:])
    a2 = over_x(right)
    b1 = over_y(left)

    top = rim + node_count

    def towards(core_a):
        return lambda c, q: q ^ jnp.where(c == core_a, X, Y) if is_traced(c) else q ^ (X, Y)[c != core_a]

    def crossing(core_a):
        return lambda c: (Y, X)[c != core_a]

    w, keep0, send0 = fused(
        local_cols, pick, mass_blocks, [low, snapshots, high],
        [(0, 0, rim, 0, 0), (1, 0, node_count, rim, 0), (2, 0, rim, top, 0)],
    )
    wx, keep1, send1 = fused(
        local_cols, pick, mass_blocks, [a1, ra, b2, rb],
        [
            (0, 0, node_count, rim, 0), (1, 0, rim, 0, 0), (1, rim, rim, top, 0),
            (2, 0, node_count, rim, half), (3, 0, rim, 0, half), (3, rim, rim, top, half),
        ],
        own=w,
    )
    keep2, send2 = fused(
        local_cols, 1 - pick, mass_blocks, [a2, b1],
        [(0, 0, node_count, 0, 0), (1, 0, node_count, 0, half)],
        own=w, extra=wx, weighs=False,
    )
    own_target = lambda c, q: q
    own = keep0 + lax.ppermute(send0, "mesh", cores)
    own = own + lax.ppermute(own, both, line(own_target, 0))
    own_came = lax.ppermute(own, both, line(own_target, 1))

    def finished(kept, sent, core_a):
        target, bit = towards(core_a), crossing(core_a)
        came = lax.ppermute(sent, "mesh", cores)
        total, coded = merge(kept, came)
        came = lax.ppermute(coded, both, line(target, 0))
        at_target = (chip == target(core, column))[None].astype(jnp.int32)
        near, leg, far = turn(at_target, total, came, column_count)
        leg = lax.ppermute(leg, both, line(target, 1) + corner(target, bit))
        far = lax.ppermute(far, both, around(target, bit))
        return near, leg, far

    stage1 = finished(keep1, send1, 0)
    stage2 = finished(keep2, send2, 1)
    near = jnp.where((chip == (column ^ X)) == (core == 0), 1, 2)
    case = jnp.where(chip == column, 0, jnp.where(chip == (column ^ (X | Y)), 3 + core, near))
    return close(case[None].astype(jnp.int32), own, own_came, *stage1, *stage2)


def on_device(snapshots, block_cols, mass_blocks):
    node_count, _ = snapshots.shape
    blk = mass_blocks.shape[1]
    blocks_here = node_count // blk
    rim = HB * blk
    shards = lax.axis_size("mesh")
    low = lax.ppermute(snapshots[-rim:], "mesh", [(i, i + 1) for i in range(shards - 1)])
    high = lax.ppermute(snapshots[:rim], "mesh", [(i + 1, i) for i in range(shards - 1)])
    local_cols = block_cols - (lax.axis_index("mesh") * blocks_here - HB)
    (weighted,) = fused(
        local_cols, jnp.zeros((1,), jnp.int32), mass_blocks, [low, snapshots, high],
        [(0, 0, rim, 0, 0), (1, 0, node_count, rim, 0), (2, 0, rim, rim + node_count, 0)],
        multiplies=False,
    )
    gathered = lax.all_gather(snapshots, "run", axis=1, tiled=True)
    return lax.psum_scatter(
        contract_nodes(gathered, weighted), "mesh", scatter_dimension=0, tiled=True
    )


def solution(mesh):
    placed = (P("mesh", "run"), P("mesh", None), P("mesh", None, None))
    square = mesh.shape["run"] == 4 and mesh.shape["mesh"] == 8

    def body(*args):
        return (on_square if square else on_device)(*args)

    return jax.shard_map(
        body, mesh=mesh, in_specs=placed, out_specs=P("mesh", "run"), check_vma=False
    )
```

time: 168 us -> 149 us (0.89); the launches traced: 168 us -> 147 us
  Pallas kernels: 0 us -> 42.2 us
  waiting for transfers between devices: 102 us -> 67 us
  matrix products: 26.7 us -> 0 us
  starting transfers between devices: 3.74 us -> 25.3 us
  between operations: 13.4 us -> 0.38 us
  local copies, waits for them, and re-layouts: 19.3 us -> 10.2 us
    ppermute x2 -> x19, waiting for transfers between devices: 3.23 us -> 67 us  [the longest x3 44.6 us: over_y(): return lax.ppermute(v, 'run', across(Y))]
    reduce_scatter x1 -> x0, waiting for transfers between devices: 50.1 us -> none  [on_device(): lax.psum_scatter(contract_nodes(gathered, weighted), 'mesh', scatter_dime...]
    all_gather x1 -> x0, waiting for transfers between devices: 48 us -> none  [on_device(): gathered = lax.all_gather(snapshots, 'run', axis=1, tiled=True)]
    pallas_call x0 -> x8, Pallas kernels: none -> 42.2 us  [the longest x3 29.9 us: fused(): pl.pallas_call(functools.partial(fused_body, plan), grid_spec=pltpu.Prefe...]
    dot_general x2 -> x0, matrix products: 26.7 us -> none  [the longest x1 17.2 us: on_device(): jnp.einsum('bim,bmc->bic', mass_blocks, picked, preferred_element_type=jn...]
    ppermute x2 -> x19, starting transfers between devices: 3.7 us -> 25.3 us  [the longest x2 6.83 us: finished(): came = lax.ppermute(coded, both, line(target, 0))]
    gather x1 -> x0, local copies, waits for them, and re-layouts: 16.1 us -> none  [on_device(): blocked[local_cols].reshape(blocks_here, stored_count * BLK, column_count)]
    unnamed x0 -> x34, local copies, waits for them, and re-layouts: none -> 6 us
  transfers between devices with their start and end apart: 4 -> 19, of which waited for: 3 -> 4; matrix products, arithmetic and copies ran while one was open for 22% -> 3% of each run, Pallas kernels for 0% -> 27%
where the time goes in v2:
time: 149 us; the launch traced here: 147 us
  waiting for transfers between devices  67 us (45%)
  Pallas kernels  42.2 us (28%)
  starting transfers between devices  25.3 us (17%)
  local copies, waits for them, and re-layouts  10.2 us (7%)
  other arithmetic  1.8 us (1%)
    ppermute x3, waiting for transfers between devices, over_y(): return lax.ppermute(v, 'run', across(Y))  44.6 us
    pallas_call x3, Pallas kernels, fused(): pl.pallas_call(functools.partial(fused_body, plan), grid_spec=pltpu.Prefe...  29.9 us
    ppermute x2, waiting for transfers between devices, finished(): came = lax.ppermute(coded, both, line(target, 0))  14.8 us
    ppermute x2, starting transfers between devices, finished(): came = lax.ppermute(coded, both, line(target, 0))  6.83 us
    unnamed x34, local copies, waits for them, and re-layouts  6 us
    pallas_call x2, Pallas kernels, merge(): pl.pallas_call(merge_body, out_shape=[jax.ShapeDtypeStruct((rows, width),...  5.04 us
    pallas_call x2, Pallas kernels, turn(): pl.pallas_call(functools.partial(turn_body, own), grid_spec=pltpu.Prefetc...  4.7 us
    ppermute x3, starting transfers between devices, over_y(): return lax.ppermute(v, 'run', across(Y))  4.09 us
  transfers between devices with their start and end apart: 19, of which 4 were waited for; matrix products, arithmetic and copies ran while one was open for 3% of the time, Pallas kernels for 27%

profile of v2, /device:TPU:0, one launch (start us, length us, event | category | flops | bytes accessed | tf_op | source)
XLA Modules:
  0.0 146.8 jit_solution(12152146123391846721)
XLA Ops:
  0.0 1.8 %fusion = (bf16[128,512]{1,0:T(8,128)(2,1)S(1)}, bf16[128,512]{1,0:T(8,128)(2,1)}) fusion(bf16[2048,512]{1,0:T(8,128)(2,1)} %refs_4_.1), kind=kLoop, calls=%fused_computation.3 | loop fusion | bytes 524288 | tf_op jit(solution)/shard_map/slice | solution.py:312
  1.8 2.4 %collective-permute-start = (bf16[128,512]{1,0:T(8,128)(2,1)}, bf16[128,512]{1,0:T(8,128)(2,1)S(1)}, u32[]{:S(2)}, u32[]{:S(2)}) collective-permute-start(bf16[128,512]{1,0:T(8,128)(2,1)} %get-tuple-element.44), channel_id=1, source_target_pairs={{0,4},{4,8},{8,12},{12,16},{16,20},{20,24},{24,28},{1,5},{5,9},{9,... | collective-permute-start | bytes 393224 | tf_op jit(solution)/shard_map/ppermute | solution.py:311
  4.2 1.3 collective-permute-start.1
  5.5 1.3 slice.20
  7.9 2.3 %collective-permute-start.13 = (bf16[2048,256]{1,0:T(8,128)(2,1)}, bf16[2048,256]{1,0:T(8,128)(2,1)S(1)}, u32[]{:S(2)}, u32[]{:S(2)}) collective-permute-start(bf16[2048,256]{1,0:T(8,128)(2,1)} %slice.22), channel_id=1, source_target_pairs={{0,1},{1,0},{2,3},{3,2},{4,5},{5,4},{6,7},{7,6},{8,9},{9,8},{10,11... | collective-permute-start | bytes 3145736 | tf_op jit(solution)/shard_map/ppermute | solution.py:304
  10.2 1.5 %collective-permute-start.7 = (bf16[2048,256]{1,0:T(8,128)(2,1)}, bf16[2048,256]{1,0:T(8,128)(2,1)}, u32[]{:S(2)}, u32[]{:S(2)}) collective-permute-start(bf16[2048,256]{1,0:T(8,128)(2,1)} %slice.22), channel_id=1, source_target_pairs={{0,2},{1,3},{2,0},{3,1},{4,6},{5,7},{6,4},{7,5},{8,10},{9,11},{10,... | collective-permute-start | bytes 3145736 | tf_op jit(solution)/shard_map/ppermute | solution.py:307
  13.2 2.1 %collective-permute-start.8 = (bf16[256,256]{1,0:T(8,128)(2,1)S(1)}, bf16[256,256]{1,0:T(8,128)(2,1)S(1)}, u32[]{:S(2)}, u32[]{:S(2)}) collective-permute-start(bf16[256,256]{1,0:T(8,128)(2,1)S(1)} %get-tuple-element.45), channel_id=1, source_target_pairs={{0,2},{1,3},{2,0},{3,1},{4,6},{5,7},{6,4},{7,5},{8,10},{9,11},{10,... | collective-permute-start | bytes 393224 | tf_op jit(solution)/shard_map/ppermute | solution.py:307
  15.8 44.6 %collective-permute-done.8.refs_6_ = bf16[256,256]{1,0:T(8,128)(2,1)S(1)} collective-permute-done((bf16[256,256]{1,0:T(8,128)(2,1)S(1)}, bf16[256,256]{1,0:T(8,128)(2,1)S(1)}, u32[]{:S(2)}, u32[]{:S(2)}) %collective-permute-start.8) | collective-permute-done | bytes 131104 | tf_op jit(solution)/shard_map/ppermute | solution.py:307
  61.1 11.1 %shard_map.37 = (bf16[2048,512]{1,0:T(8,128)(2,1)}, f32[256,512]{1,0:T(8,128)}, f32[256,512]{1,0:T(8,128)}) custom-call(s32[32,16]{1,0:T(8,128)} %broadcast_subtract_fusion.refs_0_, s32[1]{0:T(128)} %bitcast.1.refs_1_, bf16[32,64,1024]{2,1,0:T(8,128)(2,1)} %refs_2_.3, bf16[128,512]{1,0:T(8,128)(2,1)} %copy-done.13, bf16[2048,512]{1,0:T(8,128)(2,1)} %refs_4_.1, ...), custom_call_target="tpu_custom_call" | custom-call | flops 9663676416 | bytes 8388608 | tf_op jit(solution)/shard_map/pallas_call | solution.py:123
  73.4 12.0 %shard_map.38 = (bf16[2048,512]{1,0:T(8,128)(2,1)}, f32[256,768]{1,0:T(8,128)}, f32[256,768]{1,0:T(8,128)}) custom-call(s32[32,16]{1,0:T(8,128)} %broadcast_subtract_fusion.refs_0_, s32[1]{0:T(128)} %bitcast.1.refs_1_, bf16[32,64,1024]{2,1,0:T(8,128)(2,1)} %refs_2_.3, bf16[2048,256]{1,0:T(8,128)(2,1)} %collective-permute-done.5.refs_3_, ...), custom_call_target="tpu_custom_call" | custom-call | flops 10200547328 | bytes 8388608 | tf_op jit(solution)/shard_map/pallas_call | solution.py:123
  86.9 6.7 %shard_map.41 = (f32[256,768]{1,0:T(8,128)}, f32[256,768]{1,0:T(8,128)}) custom-call(s32[32,16]{1,0:T(8,128)} %broadcast_subtract_fusion.refs_0_, s32[1]{0:T(128)S(6)} %sub.20.refs_1_, bf16[2048,256]{1,0:T(8,128)(2,1)} %copy-done.2, bf16[2048,256]{1,0:T(8,128)(2,1)} %copy-done.3, bf16[2048,512]{1,0:T(8,128)(2,1)} %get-tuple-element.27.refs_7_.refs_4_, ...), custom_call_target="tpu_custom_call" | custom-call | flops 1610612736 | bytes 8388608 | tf_op jit(solution)/shard_map/pallas_call | solution.py:123
  95.3 1.3 collective-permute-start.3
  96.6 2.5 %shard_map.39 = (f32[256,768]{1,0:T(8,128)}, s16[272,768]{1,0:T(8,128)(2,1)}) custom-call(f32[256,768]{1,0:T(8,128)} %get-tuple-element.28.kept_ref, f32[256,768]{1,0:T(8,128)} %collective-permute-done.9.came_ref), custom_call_target="tpu_custom_call" | custom-call | flops 1572864 | bytes 2752512 | tf_op jit(solution)/shard_map/pallas_call | solution.py:170
  99.1 5.6 %collective-permute-start.10 = (s16[272,768]{1,0:T(8,128)(2,1)}, s16[272,768]{1,0:T(8,128)(2,1)S(1)}, u32[]{:S(2)}, u32[]{:S(2)}) collective-permute-start(s16[272,768]{1,0:T(8,128)(2,1)} %get-tuple-element.31), channel_id=1, source_target_pairs={{0,8},{16,24},{9,1},{25,17},{18,26},{2,10},{27,19},{11,3},{28,20},... | collective-permute-start | bytes 1253384 | tf_op jit(solution)/shard_map/ppermute | solution.py:357
  105.6 2.5 %shard_map.42 = (f32[256,768]{1,0:T(8,128)}, s16[272,768]{1,0:T(8,128)(2,1)}) custom-call(f32[256,768]{1,0:T(8,128)} %get-tuple-element.36.kept_ref, f32[256,768]{1,0:T(8,128)} %copy-done.4), custom_call_target="tpu_custom_call" | custom-call | flops 1572864 | bytes 2752512 | tf_op jit(solution)/shard_map/pallas_call | solution.py:170
  109.4 3.6 %collective-permute-done.3 = f32[256,512]{1,0:T(8,128)S(1)} collective-permute-done((f32[256,512]{1,0:T(8,128)S(1)}, f32[256,512]{1,0:T(8,128)S(1)}, u32[]{:S(2)}, u32[]{:S(2)}) %collective-permute-start.3) | collective-permute-done | bytes 524320 | tf_op jit(solution)/shard_map/ppermute | solution.py:350
  113.0 1.3 collective-permute-start.4
  115.1 2.4 %shard_map.40 = (f32[256,512]{1,0:T(8,128)}, s16[272,512]{1,0:T(8,128)(2,1)}, s16[272,256]{1,0:T(8,128)(2,1)}) custom-call(s32[1]{0:T(128)} %bitcast.2.flag_ref, f32[256,768]{1,0:T(8,128)} %get-tuple-element.30.total_ref, s16[272,768]{1,0:T(8,128)(2,1)} %copy-done.8), custom_call_target="tpu_custom_call" | custom-call | flops 1572864 | bytes 2359296 | tf_op jit(solution)/shard_map/pallas_call | solution.py:197
  118.2 14.8 %collective-permute-done.16.came_ref = s16[272,768]{1,0:T(8,128)(2,1)S(1)} collective-permute-done((s16[272,768]{1,0:T(8,128)(2,1)}, s16[272,768]{1,0:T(8,128)(2,1)S(1)}, u32[]{:S(2)}, u32[]{:S(2)}) %collective-permute-start.16) | collective-permute-done | bytes 417824 | tf_op jit(solution)/shard_map/ppermute | solution.py:357
  133.7 2.3 %shard_map.43 = (f32[256,512]{1,0:T(8,128)}, s16[272,512]{1,0:T(8,128)(2,1)}, s16[272,256]{1,0:T(8,128)(2,1)}) custom-call(s32[1]{0:T(128)} %bitcast.3.flag_ref, f32[256,768]{1,0:T(8,128)} %get-tuple-element.38.total_ref, s16[272,768]{1,0:T(8,128)(2,1)} %copy-done.7), custom_call_target="tpu_custom_call" | custom-call | flops 1572864 | bytes 2359296 | tf_op jit(solution)/shard_map/pallas_call | solution.py:197
  136.0 1.3 collective-permute-start.17
  138.0 1.3 collective-permute-start.18
  139.4 4.0 %collective-permute-done.18.far2 = s16[272,256]{1,0:T(8,128)(2,1)S(1)} collective-permute-done((s16[272,256]{1,0:T(8,128)(2,1)}, s16[272,256]{1,0:T(8,128)(2,1)S(1)}, u32[]{:S(2)}, u32[]{:S(2)}) %collective-permute-start.18) | collective-permute-done | bytes 139296 | tf_op jit(solution)/shard_map/ppermute | solution.py:361
  144.2 2.6 %close.1 = f32[256,512]{1,0:T(8,128)} custom-call(s32[1]{0:T(128)} %bitcast.case_ref, f32[256,512]{1,0:T(8,128)} %copy-done.1, f32[256,512]{1,0:T(8,128)} %copy-done.6, f32[256,512]{1,0:T(8,128)} %get-tuple-element.32.near1, s16[272,512]{1,0:T(8,128)(2,1)} %copy-done.9, s16[272,256]{1,0:T(8,128)(2,1)} %copy-done.11, f32[256,512]{1,0:T(8,128)} %get-tuple-element.40.near2, ...), custom_call_target="tpu_custom_call" | custom-call | tf_op jit(solution)/shard_map/close/pallas_call | solution.py:239
  (64 shorter events, 13.9 us)
Async XLA Ops:
  0.0 6.8 %copy-start = (bf16[2048,512]{1,0:T(8,128)(2,1)S(1)}, bf16[2048,512]{1,0:T(8,128)(2,1)}, u32[]{:S(2)}) copy-start(bf16[2048,512]{1,0:T(8,128)(2,1)} %refs_4_.1) | copy-start | bytes 6291460
  1.8 11.2 %collective-permute-start = (bf16[128,512]{1,0:T(8,128)(2,1)}, bf16[128,512]{1,0:T(8,128)(2,1)S(1)}, u32[]{:S(2)}, u32[]{:S(2)}) collective-permute-start(bf16[128,512]{1,0:T(8,128)(2,1)} %get-tuple-element.44), channel_id=1, source_target_pairs={{0,4},{4,8},{8,12},{12,16},{16,20},{20,24},{24,28},{1,5},{5,9},{9,... | collective-permute-start | bytes 393224 | tf_op jit(solution)/shard_map/ppermute | solution.py:311
  4.2 8.9 %collective-permute-start.1 = (bf16[128,512]{1,0:T(8,128)(2,1)S(1)}, bf16[128,512]{1,0:T(8,128)(2,1)S(1)}, u32[]{:S(2)}, u32[]{:S(2)}) collective-permute-start(bf16[128,512]{1,0:T(8,128)(2,1)S(1)} %get-tuple-element.43), channel_id=1, source_target_pairs={{4,0},{8,4},{12,8},{16,12},{20,16},{24,20},{28,24},{5,1},{9,5},{13... | collective-permute-start | bytes 393224 | tf_op jit(solution)/shard_map/ppermute | solution.py:312
  7.9 77.7 %collective-permute-start.13 = (bf16[2048,256]{1,0:T(8,128)(2,1)}, bf16[2048,256]{1,0:T(8,128)(2,1)S(1)}, u32[]{:S(2)}, u32[]{:S(2)}) collective-permute-start(bf16[2048,256]{1,0:T(8,128)(2,1)} %slice.22), channel_id=1, source_target_pairs={{0,1},{1,0},{2,3},{3,2},{4,5},{5,4},{6,7},{7,6},{8,9},{9,8},{10,11... | collective-permute-start | bytes 3145736 | tf_op jit(solution)/shard_map/ppermute | solution.py:304
  10.2 63.2 %collective-permute-start.7 = (bf16[2048,256]{1,0:T(8,128)(2,1)}, bf16[2048,256]{1,0:T(8,128)(2,1)}, u32[]{:S(2)}, u32[]{:S(2)}) collective-permute-start(bf16[2048,256]{1,0:T(8,128)(2,1)} %slice.22), channel_id=1, source_target_pairs={{0,2},{1,3},{2,0},{3,1},{4,6},{5,7},{6,4},{7,5},{8,10},{9,11},{10,... | collective-permute-start | bytes 3145736 | tf_op jit(solution)/shard_map/ppermute | solution.py:307
  11.7 73.8 %collective-permute-start.14 = (bf16[2048,256]{1,0:T(8,128)(2,1)S(1)}, bf16[2048,256]{1,0:T(8,128)(2,1)S(1)}, u32[]{:S(2)}, u32[]{:S(2)}) collective-permute-start(bf16[2048,256]{1,0:T(8,128)(2,1)S(1)} %slice.20), channel_id=1, source_target_pairs={{0,2},{1,3},{2,0},{3,1},{4,6},{5,7},{6,4},{7,5},{8,10},{9,11},{10,... | collective-permute-start | bytes 3145736 | tf_op jit(solution)/shard_map/ppermute | solution.py:307
  13.0 48.1 %copy-start.13 = (bf16[128,512]{1,0:T(8,128)(2,1)}, bf16[128,512]{1,0:T(8,128)(2,1)S(1)}, u32[]{:S(2)}) copy-start(bf16[128,512]{1,0:T(8,128)(2,1)S(1)} %collective-permute-done.refs_3_) | copy-start | bytes 393220
  13.0 60.4 %collective-permute-start.5 = (bf16[2048,256]{1,0:T(8,128)(2,1)S(1)}, bf16[2048,256]{1,0:T(8,128)(2,1)}, u32[]{:S(2)}, u32[]{:S(2)}) collective-permute-start(bf16[2048,256]{1,0:T(8,128)(2,1)S(1)} %slice.20), channel_id=1, source_target_pairs={{0,1},{1,0},{2,3},{3,2},{4,5},{5,4},{6,7},{7,6},{8,9},{9,8},{10,11... | collective-permute-start | bytes 3145736 | tf_op jit(solution)/shard_map/ppermute | solution.py:304
  13.1 48.0 %copy-start.14 = (bf16[128,512]{1,0:T(8,128)(2,1)}, bf16[128,512]{1,0:T(8,128)(2,1)S(1)}, u32[]{:S(2)}) copy-start(bf16[128,512]{1,0:T(8,128)(2,1)S(1)} %collective-permute-done.1.refs_5_) | copy-start | bytes 393220
  13.2 47.3 %collective-permute-start.8 = (bf16[256,256]{1,0:T(8,128)(2,1)S(1)}, bf16[256,256]{1,0:T(8,128)(2,1)S(1)}, u32[]{:S(2)}, u32[]{:S(2)}) collective-permute-start(bf16[256,256]{1,0:T(8,128)(2,1)S(1)} %get-tuple-element.45), channel_id=1, source_target_pairs={{0,2},{1,3},{2,0},{3,1},{4,6},{5,7},{6,4},{7,5},{8,10},{9,11},{10,... | collective-permute-start | bytes 393224 | tf_op jit(solution)/shard_map/ppermute | solution.py:307
  61.1 11.1 %collective-permute-start.6 = (bf16[256,256]{1,0:T(8,128)(2,1)S(1)}, bf16[256,256]{1,0:T(8,128)(2,1)}, u32[]{:S(2)}, u32[]{:S(2)}) collective-permute-start(bf16[256,256]{1,0:T(8,128)(2,1)S(1)} %get-tuple-element.46), channel_id=1, source_target_pairs={{0,1},{1,0},{2,3},{3,2},{4,5},{5,4},{6,7},{7,6},{8,9},{9,8},{10,11... | collective-permute-start | bytes 393224 | tf_op jit(solution)/shard_map/ppermute | solution.py:304
  72.3 21.9 %collective-permute-start.2 = (f32[256,512]{1,0:T(8,128)}, f32[256,512]{1,0:T(8,128)}, u32[]{:S(2)}, u32[]{:S(2)}) collective-permute-start(f32[256,512]{1,0:T(8,128)} %get-tuple-element.25), channel_id=1, source_target_pairs={{0,4},{4,0},{8,12},{12,8},{16,20},{20,16},{24,28},{28,24},{1,5},{5... | collective-permute-start | bytes 1572872 | tf_op jit(solution)/shard_map/ppermute | solution.py:349
  85.4 11.2 %collective-permute-start.9 = (f32[256,768]{1,0:T(8,128)}, f32[256,768]{1,0:T(8,128)}, u32[]{:S(2)}, u32[]{:S(2)}) collective-permute-start(f32[256,768]{1,0:T(8,128)} %get-tuple-element.29), channel_id=1, source_target_pairs={{0,4},{4,0},{8,12},{12,8},{16,20},{20,16},{24,28},{28,24},{1,5},{5... | collective-permute-start | bytes 2359304 | tf_op jit(solution)/shard_map/ppermute | solution.py:355
  86.9 7.2 %copy-start.5 = (f32[256,512]{1,0:T(8,128)S(1)}, f32[256,512]{1,0:T(8,128)}, u32[]{:S(2)}) copy-start(f32[256,512]{1,0:T(8,128)} %get-tuple-element.24) | copy-start | bytes 1572868
  93.7 11.0 %collective-permute-start.15 = (f32[256,768]{1,0:T(8,128)}, f32[256,768]{1,0:T(8,128)S(1)}, u32[]{:S(2)}, u32[]{:S(2)}) collective-permute-start(f32[256,768]{1,0:T(8,128)} %get-tuple-element.37), channel_id=1, source_target_pairs={{0,4},{4,0},{8,12},{12,8},{16,20},{20,16},{24,28},{28,24},{1,5},{5... | collective-permute-start | bytes 2359304 | tf_op jit(solution)/shard_map/ppermute | solution.py:355
  95.3 17.7 %collective-permute-start.3 = (f32[256,512]{1,0:T(8,128)S(1)}, f32[256,512]{1,0:T(8,128)S(1)}, u32[]{:S(2)}, u32[]{:S(2)}) collective-permute-start(f32[256,512]{1,0:T(8,128)S(1)} %add.17), channel_id=1, source_target_pairs={{8,0},{24,16},{1,9},{17,25},{26,18},{10,2},{19,27},{3,11},{12,4},{... | collective-permute-start | bytes 1572872 | tf_op jit(solution)/shard_map/ppermute | solution.py:350
  99.1 15.3 %collective-permute-start.10 = (s16[272,768]{1,0:T(8,128)(2,1)}, s16[272,768]{1,0:T(8,128)(2,1)S(1)}, u32[]{:S(2)}, u32[]{:S(2)}) collective-permute-start(s16[272,768]{1,0:T(8,128)(2,1)} %get-tuple-element.31), channel_id=1, source_target_pairs={{0,8},{16,24},{9,1},{25,17},{18,26},{2,10},{27,19},{11,3},{28,20},... | collective-permute-start | bytes 1253384 | tf_op jit(solution)/shard_map/ppermute | solution.py:357
  108.1 24.8 %collective-permute-start.16 = (s16[272,768]{1,0:T(8,128)(2,1)}, s16[272,768]{1,0:T(8,128)(2,1)S(1)}, u32[]{:S(2)}, u32[]{:S(2)}) collective-permute-start(s16[272,768]{1,0:T(8,128)(2,1)} %get-tuple-element.39), channel_id=1, source_target_pairs={{24,16},{8,0},{17,25},{1,9},{10,2},{26,18},{3,11},{19,27},{4,12},{... | collective-permute-start | bytes 1253384 | tf_op jit(solution)/shard_map/ppermute | solution.py:357
  113.0 30.4 %copy-start.1 = (f32[256,512]{1,0:T(8,128)}, f32[256,512]{1,0:T(8,128)S(1)}, u32[]{:S(2)}) copy-start(f32[256,512]{1,0:T(8,128)S(1)} %add.18.own) | copy-start | bytes 1572868
  113.0 26.3 %collective-permute-start.4 = (f32[256,512]{1,0:T(8,128)S(1)}, f32[256,512]{1,0:T(8,128)S(1)}, u32[]{:S(2)}, u32[]{:S(2)}) collective-permute-start(f32[256,512]{1,0:T(8,128)S(1)} %add.18.own), channel_id=1, source_target_pairs={{16,0},{25,9},{2,18},{11,27},{20,4},{29,13},{6,22},{15,31}} | collective-permute-start | bytes 1572872 | tf_op jit(solution)/shard_map/ppermute | solution.py:351
  117.5 25.9 %collective-permute-start.11 = (s16[272,512]{1,0:T(8,128)(2,1)}, s16[272,512]{1,0:T(8,128)(2,1)S(1)}, u32[]{:S(2)}, u32[]{:S(2)}) collective-permute-start(s16[272,512]{1,0:T(8,128)(2,1)} %get-tuple-element.33), channel_id=1, source_target_pairs={{24,8},{17,1},{10,26},{3,19},{4,20},{13,29},{22,6},{31,15},{8,10},... | collective-permute-start | bytes 835592 | tf_op jit(solution)/shard_map/ppermute | solution.py:360
  136.0 7.4 %collective-permute-start.17 = (s16[272,512]{1,0:T(8,128)(2,1)}, s16[272,512]{1,0:T(8,128)(2,1)S(1)}, u32[]{:S(2)}, u32[]{:S(2)}) collective-permute-start(s16[272,512]{1,0:T(8,128)(2,1)} %get-tuple-element.41), channel_id=1, source_target_pairs={{0,16},{9,25},{18,2},{27,11},{28,12},{21,5},{14,30},{7,23},{16,17}... | collective-permute-start | bytes 835592 | tf_op jit(solution)/shard_map/ppermute | solution.py:360
  137.3 2.0 %collective-permute-start.12 = (s16[272,256]{1,0:T(8,128)(2,1)}, s16[272,256]{1,0:T(8,128)(2,1)S(1)}, u32[]{:S(2)}, u32[]{:S(2)}) collective-permute-start(s16[272,256]{1,0:T(8,128)(2,1)} %get-tuple-element.34), channel_id=1, source_target_pairs={{24,10},{17,3},{10,24},{3,17},{4,21},{13,28},{22,7},{31,14}} | collective-permute-start | bytes 417800 | tf_op jit(solution)/shard_map/ppermute | solution.py:361
  138.0 5.4 %collective-permute-start.18 = (s16[272,256]{1,0:T(8,128)(2,1)}, s16[272,256]{1,0:T(8,128)(2,1)S(1)}, u32[]{:S(2)}, u32[]{:S(2)}) collective-permute-start(s16[272,256]{1,0:T(8,128)(2,1)} %get-tuple-element.42), channel_id=1, source_target_pairs={{0,17},{9,24},{18,3},{27,10},{28,14},{21,7},{14,28},{7,21}} | collective-permute-start | bytes 417800 | tf_op jit(solution)/shard_map/ppermute | solution.py:361
  (11 other events, 15.8 us)

commit v3 on v2

--- a/solution.py
+++ b/solution.py
@@ -24,16 +24,13 @@
 def fused_body(plan, *refs):
     refs = list(refs)
     cols_ref, pick_ref = refs.pop(0), refs.pop(0)
-    mass_hbm = refs.pop(0) if plan["weighs"] else None
+    mass_hbm = refs.pop(0)
     pieces = [refs.pop(0) for _ in range(plan["count"])]
-    own_hbm = refs.pop(0) if plan["own"] else None
-    extra_hbm = refs.pop(0) if plan["extra"] else None
-    made_ref = refs.pop(0) if plan["weighs"] else None
+    own_ref = refs.pop(0) if plan["own"] else None
+    made_ref = refs.pop(0)
     keep_ref, send_ref = (refs.pop(0), refs.pop(0)) if plan["multiplies"] else (None, None)
     rows_ref = refs.pop(0)
-    mass_ref = refs.pop(0) if plan["weighs"] else None
-    own_ref = refs.pop(0) if plan["own"] else None
-    extra_ref = refs.pop(0) if plan["extra"] else None
+    mass_ref = refs.pop(0)
     sems = refs.pop(0)
     blk, rim, half = plan["blk"], plan["rim"], plan["half"]
 
@@ -43,54 +40,84 @@
         fetch(pieces[p].at[span(r, n), :], rows_ref.at[span(to, n), span(lane, pieces[p].shape[1])])
         for p, r, n, to, lane in plan["places"]
     ]
-    mass_in, own_in, extra_in = [], [], []
-    if plan["weighs"]:
-        parts = plan["parts"]
-        size = mass_ref.shape[0] // parts
-        mass_in = [
-            fetch(mass_hbm.at[span(i * size, size)], mass_ref.at[span(i * size, size)])
-            for i in range(parts)
-        ]
-    if plan["own"]:
-        own_in = [fetch(own_hbm, own_ref)]
-    if plan["extra"]:
-        extra_in = [fetch(extra_hbm, extra_ref)]
-    for copy in rows_in + mass_in + own_in + extra_in:
+    mass_in, parts = [], plan["parts"]
+    size = mass_ref.shape[0] // parts
+    for i in range(parts):
+        part = span(i * size, size)
+        mass_in.append(fetch(mass_hbm.at[part], mass_ref.at[part]))
+    for copy in rows_in + mass_in:
         copy.start()
     for copy in rows_in:
         copy.wait()
 
-    if plan["weighs"]:
-        for row in range(mass_ref.shape[0]):
-            if row % size == 0:
-                mass_in[row // size].wait()
-            picked = jnp.concatenate(
-                [
-                    rows_ref[pl.ds(pl.multiple_of(cols_ref[row, k] * blk, blk), blk), :]
-                    for k in range(cols_ref.shape[1])
-                ],
-                axis=0,
-            )
-            product = jnp.dot(mass_ref[row], picked, preferred_element_type=jnp.float32)
-            made_ref[row * blk : (row + 1) * blk, :] = product.astype(made_ref.dtype)
-    for copy in own_in + extra_in:
-        copy.wait()
+    for row in range(mass_ref.shape[0]):
+        if row % size == 0:
+            mass_in[row // size].wait()
+        picked = jnp.concatenate(
+            [
+                rows_ref[pl.ds(pl.multiple_of(cols_ref[row, k] * blk, blk), blk), :]
+                for k in range(cols_ref.shape[1])
+            ],
+            axis=0,
+        )
+        product = jnp.dot(mass_ref[row], picked, preferred_element_type=jnp.float32)
+        made_ref[row * blk : (row + 1) * blk, :] = product.astype(made_ref.dtype)
 
     if plan["multiplies"]:
         w_ref = own_ref if plan["own"] else made_ref
-        x_ref = extra_ref if plan["extra"] else (made_ref if plan["own"] else None)
-        own = w_ref.shape[1]
-        nodes = w_ref.shape[0]
-        lead = rim if plan["padded"] else 0
+        own, nodes = w_ref.shape[1], w_ref.shape[0]
         for target, first in ((keep_ref, pick_ref[0]), (send_ref, 1 - pick_ref[0])):
-            left = rows_ref[span(lead, nodes), pl.ds(pl.multiple_of(first * half, half), half)]
+            left = rows_ref[span(rim, nodes), pl.ds(pl.multiple_of(first * half, half), half)]
             target[:, :own] = contract_nodes(left, w_ref[...])
-            if x_ref is not None:
-                right = x_ref[:, pl.ds(pl.multiple_of((1 - first) * half, half), half)]
+            if plan["own"]:
+                right = made_ref[:, pl.ds(pl.multiple_of((1 - first) * half, half), half)]
                 target[:, own:] = contract_nodes(left, right)
 
 
-def fused(local_cols, pick, mass_blocks, pieces, places, own=None, extra=None, weighs=True, multiplies=True):
+def in_hbm(array):
+    return pltpu.with_memory_space_constraint(array, pltpu.HBM)
+
+
+def parts_body(source, *refs):
+    targets, sems = refs[:-1], refs[-1]
+    nodes, width = source.shape
+    rim = targets[-1].shape[0]
+    half = width // 2
+    pieces = [
+        source.at[:, :half],
+        source.at[:, half:],
+        source.at[span(nodes - rim, rim), :],
+        source.at[span(0, rim), :],
+    ]
+    copies = [
+        pltpu.make_async_copy(piece, target, sems.at[i])
+        for i, (piece, target) in enumerate(zip(pieces, targets))
+    ]
+    for copy in copies:
+        copy.start()
+    for copy in copies:
+        copy.wait()
+
+
+def parts_of(snapshots, rim):
+    nodes, width = snapshots.shape
+    shapes = [(nodes, width // 2)] * 2 + [(rim, width)] * 2
+    return pl.pallas_call(
+        parts_body,
+        in_specs=[pl.BlockSpec(memory_space=pl.ANY)],
+        out_specs=[pl.BlockSpec(memory_space=pltpu.VMEM)] * 4,
+        out_shape=[pltpu.VMEM(shape, snapshots.dtype) for shape in shapes],
+        scratch_shapes=[pltpu.SemaphoreType.DMA((4,))],
+        compiler_params=pltpu.CompilerParams(vmem_limit_bytes=4 << 20),
+        name="parts",
+    )(in_hbm(snapshots))
+
+
+def in_vmem(array):
+    return pltpu.with_memory_space_constraint(array, pltpu.VMEM)
+
+
+def fused(local_cols, pick, mass_blocks, pieces, places, own=None, multiplies=True):
     block_rows, blk, stored = mass_blocks.shape
     rim = HB * blk
     nodes = block_rows * blk
@@ -99,39 +126,72 @@
     row_count = max(to + n for _, _, n, to, _ in places)
     parts = 4 if block_rows % 4 == 0 else 1
     plan = dict(
-        blk=blk, rim=rim, half=half, weighs=weighs, multiplies=multiplies, places=places,
-        count=len(pieces), own=own is not None, extra=extra is not None,
-        padded=row_count > nodes, parts=parts,
+        blk=blk, rim=rim, half=half, multiplies=multiplies, places=places, count=len(pieces),
+        own=own is not None, parts=parts,
     )
     total = width + half if own is not None else width
-    operands, scratch = [], [pltpu.VMEM((row_count, width), jnp.bfloat16)]
-    outs, flops = [], 0
-    if weighs:
-        operands.append(mass_blocks)
-        scratch.append(pltpu.VMEM(mass_blocks.shape, jnp.bfloat16))
-        outs.append(jax.ShapeDtypeStruct((nodes, width), jnp.bfloat16))
-        flops += 8 * nodes * stored * width
-    operands += pieces
-    for w in (own, extra):
-        if w is not None:
-            operands.append(w)
-            scratch.append(pltpu.VMEM(w.shape, jnp.bfloat16))
+    operands = [in_hbm(mass_blocks), *pieces]
+    specs = [pl.BlockSpec(memory_space=pl.ANY)] * len(operands)
+    if own is not None:
+        operands.append(in_vmem(own))
+        specs.append(pl.BlockSpec(memory_space=pltpu.VMEM))
+    outs = [pltpu.VMEM((nodes, width), jnp.bfloat16)]
+    flops = 8 * nodes * stored * width
     if multiplies:
-        outs += [jax.ShapeDtypeStruct((half, total), jnp.float32)] * 2
+        outs += [pltpu.VMEM((half, total), jnp.float32)] * 2
         flops += 4 * nodes * half * total
-    scratch.append(pltpu.SemaphoreType.DMA((len(places) + parts + 2,)))
     return pl.pallas_call(
         functools.partial(fused_body, plan),
         grid_spec=pltpu.PrefetchScalarGridSpec(
             num_scalar_prefetch=2,
             grid=(),
-            in_specs=[pl.BlockSpec(memory_space=pl.ANY)] * len(operands),
+            in_specs=specs,
             out_specs=[pl.BlockSpec(memory_space=pltpu.VMEM)] * len(outs),
-            scratch_shapes=scratch,
+            scratch_shapes=[
+                pltpu.VMEM((row_count, width), jnp.bfloat16),
+                pltpu.VMEM(mass_blocks.shape, jnp.bfloat16),
+                pltpu.SemaphoreType.DMA((len(places) + parts,)),
+            ],
         ),
         out_shape=outs,
         cost_estimate=pl.CostEstimate(flops=flops, bytes_accessed=8 << 20, transcendentals=0),
+        compiler_params=pltpu.CompilerParams(vmem_limit_bytes=24 << 20),
     )(local_cols, pick, *operands)
+
+
+def products_body(pick_ref, left_a, left_b, w_ref, x_ref, keep_ref, send_ref):
+    own, half = w_ref.shape[1], x_ref.shape[1] // 2
+
+    def multiply(target, left, lo):
+        target[:, :own] = contract_nodes(left[...], w_ref[...])
+        target[:, own:] = contract_nodes(left[...], x_ref[:, lo : lo + half])
+
+    @pl.when(pick_ref[0] == 0)
+    def _():
+        multiply(keep_ref, left_a, half)
+        multiply(send_ref, left_b, 0)
+
+    @pl.when(pick_ref[0] != 0)
+    def _():
+        multiply(keep_ref, left_b, 0)
+        multiply(send_ref, left_a, half)
+
+
+def products(pick, left_a, left_b, w, x):
+    nodes, own = w.shape
+    rows, total = left_a.shape[1], own + x.shape[1] // 2
+    vmem = pl.BlockSpec(memory_space=pltpu.VMEM)
+    return pl.pallas_call(
+        products_body,
+        grid_spec=pltpu.PrefetchScalarGridSpec(
+            num_scalar_prefetch=1, grid=(), in_specs=[vmem] * 4, out_specs=[vmem] * 2
+        ),
+        out_shape=[pltpu.VMEM((rows, total), jnp.float32)] * 2,
+        cost_estimate=pl.CostEstimate(
+            flops=4 * nodes * rows * total, bytes_accessed=8 << 20, transcendentals=0
+        ),
+        compiler_params=pltpu.CompilerParams(vmem_limit_bytes=16 << 20),
+    )(pick, *(in_vmem(array) for array in (left_a, left_b, w, x)))
 
 
 TOP = 32000.0
@@ -165,18 +225,28 @@
     put_encoded(coded_ref, total)
 
 
-def merge(kept, came):
+def merge(kept, came, body=merge_body):
     rows, width = kept.shape
-    return pl.pallas_call(
-        merge_body,
+    vmem = pl.BlockSpec(memory_space=pltpu.VMEM)
+    return pl.pallas_call(
+        body,
+        in_specs=[vmem] * 2,
+        out_specs=[vmem] * 2,
         out_shape=[
-            jax.ShapeDtypeStruct((rows, width), jnp.float32),
-            jax.ShapeDtypeStruct((rows + EXTRA, width), jnp.int16),
+            pltpu.VMEM((rows, width), jnp.float32),
+            pltpu.VMEM((rows + EXTRA, width), jnp.int16),
         ],
         cost_estimate=pl.CostEstimate(
             flops=8 * rows * width, bytes_accessed=14 * rows * width, transcendentals=0
         ),
-    )(kept, came)
+        compiler_params=pltpu.CompilerParams(vmem_limit_bytes=16 << 20),
+    )(in_vmem(kept), in_vmem(came))
+
+
+def step_body(total_ref, came_ref, next_ref, coded_ref):
+    total = total_ref[...] + decoded(came_ref, 0, total_ref.shape[1])
+    next_ref[...] = total
+    put_encoded(coded_ref, total)
 
 
 def turn_body(own, flag_ref, total_ref, came_ref, near_ref, leg_ref, far_ref, coded_ref):
@@ -192,7 +262,7 @@
 
 def turn(flag, total, came, own):
     rows, width = total.shape
-    coded = lambda columns: jax.ShapeDtypeStruct((rows + EXTRA, columns), jnp.int16)
+    coded = lambda columns: pltpu.VMEM((rows + EXTRA, columns), jnp.int16)
     vmem = pl.BlockSpec(memory_space=pltpu.VMEM)
     return pl.pallas_call(
         functools.partial(turn_body, own),
@@ -203,11 +273,12 @@
             out_specs=[vmem] * 3,
             scratch_shapes=[pltpu.VMEM((rows + EXTRA, width), jnp.int16)],
         ),
-        out_shape=[jax.ShapeDtypeStruct((rows, own), jnp.float32), coded(own), coded(width - own)],
+        out_shape=[pltpu.VMEM((rows, own), jnp.float32), coded(own), coded(width - own)],
         cost_estimate=pl.CostEstimate(
             flops=8 * rows * width, bytes_accessed=12 * rows * width, transcendentals=0
         ),
-    )(flag, total, came)
+        compiler_params=pltpu.CompilerParams(vmem_limit_bytes=16 << 20),
+    )(flag, in_vmem(total), in_vmem(came))
 
 
 def close_body(case_ref, own, own_came, near1, leg1, far1, near2, leg2, far2, out_ref):
@@ -217,7 +288,7 @@
 
     @pl.when(case == 0)
     def _():
-        out_ref[...] = own[...] + own_came[...]
+        out_ref[...] = own[...] + decoded(own_came, 0, width)
 
     for number, near, leg in ((1, near1, leg1), (2, near2, leg2)):
 
@@ -242,8 +313,9 @@
             num_scalar_prefetch=1, grid=(), in_specs=[vmem] * len(parts), out_specs=vmem
         ),
         out_shape=jax.ShapeDtypeStruct(parts[0].shape, jnp.float32),
+        compiler_params=pltpu.CompilerParams(vmem_limit_bytes=16 << 20),
         name="close",
-    )(case, *parts)
+    )(case, *(in_vmem(part) for part in parts))
 
 
 LINE = {t: (((t ^ 1, t), (t ^ 3, t ^ 2)), ((t ^ 2, t),)) for t in range(4)}
@@ -308,12 +380,11 @@
 
     pick = core[None].astype(jnp.int32)
     shards = 2 * chips
-    low = lax.ppermute(snapshots[-rim:], "mesh", [(i, i + 1) for i in range(shards - 1)])
-    high = lax.ppermute(snapshots[:rim], "mesh", [(i + 1, i) for i in range(shards - 1)])
-    left = snapshots[:, :half]
+    left, right, last_rows, first_rows = parts_of(snapshots, rim)
     a1 = over_x(left)
-    right = lax.optimization_barrier((snapshots, left))[0][:, half:]
     b2 = over_y(right)
+    low = lax.ppermute(last_rows, "mesh", [(i, i + 1) for i in range(shards - 1)])
+    high = lax.ppermute(first_rows, "mesh", [(i + 1, i) for i in range(shards - 1)])
     rims = jnp.concatenate([low, high], axis=0)
     ra = over_x(rims[:, :half])
     rb = over_y(rims[:, half:])
@@ -329,7 +400,7 @@
         return lambda c: (Y, X)[c != core_a]
 
     w, keep0, send0 = fused(
-        local_cols, pick, mass_blocks, [low, snapshots, high],
+        local_cols, pick, mass_blocks, [low, in_hbm(snapshots), high],
         [(0, 0, rim, 0, 0), (1, 0, node_count, rim, 0), (2, 0, rim, top, 0)],
     )
     wx, keep1, send1 = fused(
@@ -340,15 +411,13 @@
         ],
         own=w,
     )
-    keep2, send2 = fused(
-        local_cols, 1 - pick, mass_blocks, [a2, b1],
-        [(0, 0, node_count, 0, 0), (1, 0, node_count, 0, half)],
-        own=w, extra=wx, weighs=False,
-    )
+    keep2, send2 = products(1 - pick, a2, b1, w, wx)
     own_target = lambda c, q: q
-    own = keep0 + lax.ppermute(send0, "mesh", cores)
-    own = own + lax.ppermute(own, both, line(own_target, 0))
-    own_came = lax.ppermute(own, both, line(own_target, 1))
+    came = lax.ppermute(send0, "mesh", cores)
+    own, coded = merge(keep0, came)
+    came = lax.ppermute(coded, both, line(own_target, 0))
+    own, coded = merge(own, came, step_body)
+    own_came = lax.ppermute(coded, both, line(own_target, 1))
 
     def finished(kept, sent, core_a):
         target, bit = towards(core_a), crossing(core_a)

time: 149 us -> 130 us (0.87); the launches traced: 147 us -> 130 us
  starting transfers between devices: 25.3 us -> 35.5 us
  Pallas kernels: 42.2 us -> 32.6 us
  waiting for transfers between devices: 67 us -> 58.9 us
  local copies, waits for them, and re-layouts: 10.2 us -> 2.46 us
  other arithmetic: 1.8 us -> 0.01 us
    ppermute x2, waiting for transfers between devices: 14.8 us -> 0.01 us  [finished(): came = lax.ppermute(coded, both, line(target, 0))]
    ppermute x5, waiting for transfers between devices: 3.57 us -> 16.3 us  [the longest x1 12.6 us: on_square(): came = lax.ppermute(coded, both, line(own_target, 0))]
    pallas_call x3 -> x2, Pallas kernels: 29.9 us -> 20.7 us  [fused(): pl.pallas_call(functools.partial(fused_body, plan), grid_spec=pltpu.Prefe...]
    ppermute x2, starting transfers between devices: 1.96 us -> 6.8 us  [finished(): leg = lax.ppermute(leg, both, line(target, 1) + corner(target, bit))]
    slice x3 -> x0, local copies, waits for them, and re-layouts: 4.15 us -> none  [the longest x1 1.79 us: on_square(): snapshots[:rim]]
    ppermute x2, waiting for transfers between devices: 4 us -> 0.01 us  [finished(): far = lax.ppermute(far, both, around(target, bit))]
    unnamed x34 -> x6, local copies, waits for them, and re-layouts: 6 us -> 2.43 us
    pallas_call x2 -> x6, Pallas kernels: 5.04 us -> 8.11 us  [the longest x4 3.68 us: merge(): pl.pallas_call(body, in_specs=[vmem] * 2, out_specs=[vmem] * 2, out_shape...]
  transfers between devices with their start and end apart: 19 -> 19, of which waited for: 4 -> 3; matrix products, arithmetic and copies ran while one was open for 3% -> 1% of each run, Pallas kernels for 27% -> 22%
where the time goes in v3:
time: 130 us
  waiting for transfers between devices  58.9 us (45%)
  starting transfers between devices  35.5 us (27%)
  Pallas kernels  32.6 us (25%)
  local copies, waits for them, and re-layouts  2.46 us (2%)
    ppermute x3, waiting for transfers between devices, over_y(): return lax.ppermute(v, 'run', across(Y))  42.6 us
    pallas_call x2, Pallas kernels, fused(): pl.pallas_call(functools.partial(fused_body, plan), grid_spec=pltpu.Prefe...  20.7 us
    ppermute x1, waiting for transfers between devices, on_square(): came = lax.ppermute(coded, both, line(own_target, 0))  12.6 us
    ppermute x2, starting transfers between devices, finished(): came = lax.ppermute(coded, both, line(target, 0))  7.02 us
    ppermute x2, starting transfers between devices, finished(): leg = lax.ppermute(leg, both, line(target, 1) + corner(target, bit))  6.8 us
    ppermute x2, starting transfers between devices, finished(): far = lax.ppermute(far, both, around(target, bit))  4.77 us
    ppermute x3, starting transfers between devices, over_y(): return lax.ppermute(v, 'run', across(Y))  4.51 us
    ppermute x3, starting transfers between devices, over_x(): return lax.ppermute(v, 'run', across(X))  4.48 us
  transfers between devices with their start and end apart: 19, of which 3 were waited for; matrix products, arithmetic and copies ran while one was open for 1% of the time, Pallas kernels for 22%

profile of v3, /device:TPU:0, one launch (start us, length us, event | category | flops | bytes accessed | tf_op | source)
XLA Modules:
  0.0 129.8 jit_solution(849417409580869023)
XLA Ops:
  0.0 2.6 %parts.1 = (bf16[2048,256]{1,0:T(8,128)(2,1)}, bf16[2048,256]{1,0:T(8,128)(2,1)S(1)}, bf16[128,512]{1,0:T(8,128)(2,1)}, bf16[128,512]{1,0:T(8,128)(2,1)S(1)}) custom-call(bf16[2048,512]{1,0:T(8,128)(2,1)} %refs_4_.1), custom_call_target="tpu_custom_call" | custom-call | tf_op jit(solution)/shard_map/parts/pallas_call | solution.py:105
  2.6 2.4 %collective-permute-start = (bf16[128,512]{1,0:T(8,128)(2,1)}, bf16[128,512]{1,0:T(8,128)(2,1)S(1)}, u32[]{:S(2)}, u32[]{:S(2)}) collective-permute-start(bf16[128,512]{1,0:T(8,128)(2,1)} %get-tuple-element.31), channel_id=1, source_target_pairs={{0,4},{4,8},{8,12},{12,16},{16,20},{20,24},{24,28},{1,5},{5,9},{9,... | collective-permute-start | bytes 393224 | tf_op jit(solution)/shard_map/ppermute | solution.py:386
  5.0 1.3 collective-permute-start.1
  6.3 2.4 %collective-permute-start.14 = (bf16[2048,256]{1,0:T(8,128)(2,1)}, bf16[2048,256]{1,0:T(8,128)(2,1)S(1)}, u32[]{:S(2)}, u32[]{:S(2)}) collective-permute-start(bf16[2048,256]{1,0:T(8,128)(2,1)} %get-tuple-element.39), channel_id=1, source_target_pairs={{0,2},{1,3},{2,0},{3,1},{4,6},{5,7},{6,4},{7,5},{8,10},{9,11},{10,... | collective-permute-start | bytes 3145736 | tf_op jit(solution)/shard_map/ppermute | solution.py:379
  8.7 1.5 %collective-permute-start.5 = (bf16[2048,256]{1,0:T(8,128)(2,1)}, bf16[2048,256]{1,0:T(8,128)(2,1)}, u32[]{:S(2)}, u32[]{:S(2)}) collective-permute-start(bf16[2048,256]{1,0:T(8,128)(2,1)} %get-tuple-element.39), channel_id=1, source_target_pairs={{0,1},{1,0},{2,3},{3,2},{4,5},{5,4},{6,7},{7,6},{8,9},{9,8},{10,11... | collective-permute-start | bytes 3145736 | tf_op jit(solution)/shard_map/ppermute | solution.py:376
  11.7 2.0 %collective-permute-start.8 = (bf16[256,256]{1,0:T(8,128)(2,1)S(1)}, bf16[256,256]{1,0:T(8,128)(2,1)S(1)}, u32[]{:S(2)}, u32[]{:S(2)}) collective-permute-start(bf16[256,256]{1,0:T(8,128)(2,1)S(1)} %get-tuple-element.57), channel_id=1, source_target_pairs={{0,2},{1,3},{2,0},{3,1},{4,6},{5,7},{6,4},{7,5},{8,10},{9,11},{10,... | collective-permute-start | bytes 393224 | tf_op jit(solution)/shard_map/ppermute | solution.py:379
  13.7 42.5 %collective-permute-done.8.refs_6_ = bf16[256,256]{1,0:T(8,128)(2,1)S(1)} collective-permute-done((bf16[256,256]{1,0:T(8,128)(2,1)S(1)}, bf16[256,256]{1,0:T(8,128)(2,1)S(1)}, u32[]{:S(2)}, u32[]{:S(2)}) %collective-permute-start.8) | collective-permute-done | bytes 131104 | tf_op jit(solution)/shard_map/ppermute | solution.py:379
  56.3 2.5 %collective-permute-start.6 = (bf16[256,256]{1,0:T(8,128)(2,1)S(1)}, bf16[256,256]{1,0:T(8,128)(2,1)S(1)}, u32[]{:S(2)}, u32[]{:S(2)}) collective-permute-start(bf16[256,256]{1,0:T(8,128)(2,1)S(1)} %get-tuple-element.58), channel_id=1, source_target_pairs={{0,1},{1,0},{2,3},{3,2},{4,5},{5,4},{6,7},{7,6},{8,9},{9,8},{10,11... | collective-permute-start | bytes 393224 | tf_op jit(solution)/shard_map/ppermute | solution.py:376
  58.7 10.3 %shard_map.37 = (bf16[2048,512]{1,0:T(8,128)(2,1)S(1)}, f32[256,512]{1,0:T(8,128)S(1)}, f32[256,512]{1,0:T(8,128)S(1)}) custom-call(s32[32,16]{1,0:T(8,128)S(1)} %broadcast_subtract_fusion.refs_0_, s32[1]{0:T(128)} %bitcast.1.refs_1_, bf16[32,64,1024]{2,1,0:T(8,128)(2,1)} %refs_2_.3, bf16[128,512]{1,0:T(8,128)(2,1)S(1)} %collective-permute-done.refs_3_, ...), custom_call_target="tpu_custom_call" | custom-call | flops 9663676416 | bytes 8388608 | tf_op jit(solution)/shard_map/pallas_call | solution.py:143
  69.0 10.4 %shard_map.40 = (bf16[2048,512]{1,0:T(8,128)(2,1)S(1)}, f32[256,768]{1,0:T(8,128)S(1)}, f32[256,768]{1,0:T(8,128)S(1)}) custom-call(s32[32,16]{1,0:T(8,128)S(1)} %broadcast_subtract_fusion.refs_0_, s32[1]{0:T(128)} %bitcast.1.refs_1_, bf16[32,64,1024]{2,1,0:T(8,128)(2,1)} %refs_2_.3, bf16[2048,256]{1,0:T(8,128)(2,1)} %collective-permute-done.5.refs_3_, ...), custom_call_target="tpu_custom_call" | custom-call | flops 10200547328 | bytes 8388608 | tf_op jit(solution)/shard_map/pallas_call | solution.py:143
  79.4 1.1 collective-permute-start.9
  80.6 1.8 %shard_map.43 = (f32[256,768]{1,0:T(8,128)S(1)}, f32[256,768]{1,0:T(8,128)S(1)}) custom-call(s32[1]{0:T(128)S(6)} %sub.20.pick_ref, bf16[2048,256]{1,0:T(8,128)(2,1)S(1)} %collective-permute-done.13.left_a, bf16[2048,256]{1,0:T(8,128)(2,1)S(1)} %collective-permute-done.14.left_b, bf16[2048,512]{1,0:T(8,128)(2,1)S(1)} %get-tuple-element.41.refs_7_.w_ref, ...), custom_call_target="tpu_custom_call" | custom-call | flops 1610612736 | bytes 8388608 | tf_op jit(solution)/shard_map/pallas_call | solution.py:184
  83.0 1.0 shard_map.41
  84.0 5.7 %collective-permute-start.10 = (s16[272,768]{1,0:T(8,128)(2,1)}, s16[272,768]{1,0:T(8,128)(2,1)S(1)}, u32[]{:S(2)}, u32[]{:S(2)}) collective-permute-start(s16[272,768]{1,0:T(8,128)(2,1)} %get-tuple-element.45), channel_id=1, source_target_pairs={{0,8},{16,24},{9,1},{25,17},{18,26},{2,10},{27,19},{11,3},{28,20},... | collective-permute-start | bytes 1253384 | tf_op jit(solution)/shard_map/ppermute | solution.py:426
  89.7 1.0 shard_map.44
  90.7 1.3 collective-permute-start.16
  92.8 1.3 collective-permute-start.3
  94.1 12.6 %collective-permute-done.3.came_ref = s16[272,512]{1,0:T(8,128)(2,1)S(1)} collective-permute-done((s16[272,512]{1,0:T(8,128)(2,1)}, s16[272,512]{1,0:T(8,128)(2,1)S(1)}, u32[]{:S(2)}, u32[]{:S(2)}) %collective-permute-start.3) | collective-permute-done | bytes 278560 | tf_op jit(solution)/shard_map/ppermute | solution.py:418
  109.3 1.3 collective-permute-start.4
  110.6 1.0 shard_map.42
  113.3 6.1 %collective-permute-start.17 = (s16[272,512]{1,0:T(8,128)(2,1)}, s16[272,512]{1,0:T(8,128)(2,1)S(1)}, u32[]{:S(2)}, u32[]{:S(2)}) collective-permute-start(s16[272,512]{1,0:T(8,128)(2,1)} %get-tuple-element.55), channel_id=1, source_target_pairs={{0,16},{9,25},{18,2},{27,11},{28,12},{21,5},{14,30},{7,23},{16,17}... | collective-permute-start | bytes 835592 | tf_op jit(solution)/shard_map/ppermute | solution.py:429
  120.1 4.1 %collective-permute-start.18 = (s16[272,256]{1,0:T(8,128)(2,1)S(1)}, s16[272,256]{1,0:T(8,128)(2,1)S(1)}, u32[]{:S(2)}, u32[]{:S(2)}) collective-permute-start(s16[272,256]{1,0:T(8,128)(2,1)S(1)} %get-tuple-element.56), channel_id=1, source_target_pairs={{0,17},{9,24},{18,3},{27,10},{28,14},{21,7},{14,28},{7,21}} | collective-permute-start | bytes 417800 | tf_op jit(solution)/shard_map/ppermute | solution.py:430
  124.2 3.7 %collective-permute-done.4.own_came = s16[272,512]{1,0:T(8,128)(2,1)} collective-permute-done((s16[272,512]{1,0:T(8,128)(2,1)}, s16[272,512]{1,0:T(8,128)(2,1)}, u32[]{:S(2)}, u32[]{:S(2)}) %collective-permute-start.4) | collective-permute-done | bytes 278560 | tf_op jit(solution)/shard_map/ppermute | solution.py:420
  128.0 1.8 %close.1 = f32[256,512]{1,0:T(8,128)} custom-call(s32[1]{0:T(128)} %bitcast.case_ref, f32[256,512]{1,0:T(8,128)S(1)} %get-tuple-element.37.own, s16[272,512]{1,0:T(8,128)(2,1)} %collective-permute-done.4.own_came, f32[256,512]{1,0:T(8,128)S(1)} %get-tuple-element.46.near1, s16[272,512]{1,0:T(8,128)(2,1)S(1)} %collective-permute-done.11.leg1, ...), custom_call_target="tpu_custom_call" | custom-call | tf_op jit(solution)/shard_map/close/pallas_call | solution.py:310
  (34 shorter events, 7.8 us)
Async XLA Ops:
  2.6 8.9 %collective-permute-start = (bf16[128,512]{1,0:T(8,128)(2,1)}, bf16[128,512]{1,0:T(8,128)(2,1)S(1)}, u32[]{:S(2)}, u32[]{:S(2)}) collective-permute-start(bf16[128,512]{1,0:T(8,128)(2,1)} %get-tuple-element.31), channel_id=1, source_target_pairs={{0,4},{4,8},{8,12},{12,16},{16,20},{20,24},{24,28},{1,5},{5,9},{9,... | collective-permute-start | bytes 393224 | tf_op jit(solution)/shard_map/ppermute | solution.py:386
  5.0 6.6 %collective-permute-start.1 = (bf16[128,512]{1,0:T(8,128)(2,1)S(1)}, bf16[128,512]{1,0:T(8,128)(2,1)S(1)}, u32[]{:S(2)}, u32[]{:S(2)}) collective-permute-start(bf16[128,512]{1,0:T(8,128)(2,1)S(1)} %get-tuple-element.32), channel_id=1, source_target_pairs={{4,0},{8,4},{12,8},{16,12},{20,16},{24,20},{28,24},{5,1},{9,5},{13... | collective-permute-start | bytes 393224 | tf_op jit(solution)/shard_map/ppermute | solution.py:387
  6.3 74.2 %collective-permute-start.14 = (bf16[2048,256]{1,0:T(8,128)(2,1)}, bf16[2048,256]{1,0:T(8,128)(2,1)S(1)}, u32[]{:S(2)}, u32[]{:S(2)}) collective-permute-start(bf16[2048,256]{1,0:T(8,128)(2,1)} %get-tuple-element.39), channel_id=1, source_target_pairs={{0,2},{1,3},{2,0},{3,1},{4,6},{5,7},{6,4},{7,5},{8,10},{9,11},{10,... | collective-permute-start | bytes 3145736 | tf_op jit(solution)/shard_map/ppermute | solution.py:379
  8.7 60.3 %collective-permute-start.5 = (bf16[2048,256]{1,0:T(8,128)(2,1)}, bf16[2048,256]{1,0:T(8,128)(2,1)}, u32[]{:S(2)}, u32[]{:S(2)}) collective-permute-start(bf16[2048,256]{1,0:T(8,128)(2,1)} %get-tuple-element.39), channel_id=1, source_target_pairs={{0,1},{1,0},{2,3},{3,2},{4,5},{5,4},{6,7},{7,6},{8,9},{9,8},{10,11... | collective-permute-start | bytes 3145736 | tf_op jit(solution)/shard_map/ppermute | solution.py:376
  10.2 70.3 %collective-permute-start.13 = (bf16[2048,256]{1,0:T(8,128)(2,1)S(1)}, bf16[2048,256]{1,0:T(8,128)(2,1)S(1)}, u32[]{:S(2)}, u32[]{:S(2)}) collective-permute-start(bf16[2048,256]{1,0:T(8,128)(2,1)S(1)} %get-tuple-element.40), channel_id=1, source_target_pairs={{0,1},{1,0},{2,3},{3,2},{4,5},{5,4},{6,7},{7,6},{8,9},{9,8},{10,11... | collective-permute-start | bytes 3145736 | tf_op jit(solution)/shard_map/ppermute | solution.py:376
  11.5 57.5 %collective-permute-start.7 = (bf16[2048,256]{1,0:T(8,128)(2,1)S(1)}, bf16[2048,256]{1,0:T(8,128)(2,1)S(1)}, u32[]{:S(2)}, u32[]{:S(2)}) collective-permute-start(bf16[2048,256]{1,0:T(8,128)(2,1)S(1)} %get-tuple-element.40), channel_id=1, source_target_pairs={{0,2},{1,3},{2,0},{3,1},{4,6},{5,7},{6,4},{7,5},{8,10},{9,11},{10,... | collective-permute-start | bytes 3145736 | tf_op jit(solution)/shard_map/ppermute | solution.py:379
  11.7 44.6 %collective-permute-start.8 = (bf16[256,256]{1,0:T(8,128)(2,1)S(1)}, bf16[256,256]{1,0:T(8,128)(2,1)S(1)}, u32[]{:S(2)}, u32[]{:S(2)}) collective-permute-start(bf16[256,256]{1,0:T(8,128)(2,1)S(1)} %get-tuple-element.57), channel_id=1, source_target_pairs={{0,2},{1,3},{2,0},{3,1},{4,6},{5,7},{6,4},{7,5},{8,10},{9,11},{10,... | collective-permute-start | bytes 393224 | tf_op jit(solution)/shard_map/ppermute | solution.py:379
  56.3 12.7 %collective-permute-start.6 = (bf16[256,256]{1,0:T(8,128)(2,1)S(1)}, bf16[256,256]{1,0:T(8,128)(2,1)S(1)}, u32[]{:S(2)}, u32[]{:S(2)}) collective-permute-start(bf16[256,256]{1,0:T(8,128)(2,1)S(1)} %get-tuple-element.58), channel_id=1, source_target_pairs={{0,1},{1,0},{2,3},{3,2},{4,5},{5,4},{6,7},{7,6},{8,9},{9,8},{10,11... | collective-permute-start | bytes 393224 | tf_op jit(solution)/shard_map/ppermute | solution.py:376
  79.4 3.5 %collective-permute-start.9 = (f32[256,768]{1,0:T(8,128)S(1)}, f32[256,768]{1,0:T(8,128)S(1)}, u32[]{:S(2)}, u32[]{:S(2)}) collective-permute-start(f32[256,768]{1,0:T(8,128)S(1)} %get-tuple-element.43), channel_id=1, source_target_pairs={{0,4},{4,0},{8,12},{12,8},{16,20},{20,16},{24,28},{28,24},{1,5},{5... | collective-permute-start | bytes 2359304 | tf_op jit(solution)/shard_map/ppermute | solution.py:424
  82.4 7.3 %collective-permute-start.15 = (f32[256,768]{1,0:T(8,128)S(1)}, f32[256,768]{1,0:T(8,128)S(1)}, u32[]{:S(2)}, u32[]{:S(2)}) collective-permute-start(f32[256,768]{1,0:T(8,128)S(1)} %get-tuple-element.51), channel_id=1, source_target_pairs={{0,4},{4,0},{8,12},{12,8},{16,20},{20,16},{24,28},{28,24},{1,5},{5... | collective-permute-start | bytes 2359304 | tf_op jit(solution)/shard_map/ppermute | solution.py:424
  82.7 9.3 %collective-permute-start.2 = (f32[256,512]{1,0:T(8,128)S(1)}, f32[256,512]{1,0:T(8,128)S(1)}, u32[]{:S(2)}, u32[]{:S(2)}) collective-permute-start(f32[256,512]{1,0:T(8,128)S(1)} %get-tuple-element.34), channel_id=1, source_target_pairs={{0,4},{4,0},{8,12},{12,8},{16,20},{20,16},{24,28},{28,24},{1,5},{5... | collective-permute-start | bytes 1572872 | tf_op jit(solution)/shard_map/ppermute | solution.py:416
  84.0 26.7 %collective-permute-start.10 = (s16[272,768]{1,0:T(8,128)(2,1)}, s16[272,768]{1,0:T(8,128)(2,1)S(1)}, u32[]{:S(2)}, u32[]{:S(2)}) collective-permute-start(s16[272,768]{1,0:T(8,128)(2,1)} %get-tuple-element.45), channel_id=1, source_target_pairs={{0,8},{16,24},{9,1},{25,17},{18,26},{2,10},{27,19},{11,3},{28,20},... | collective-permute-start | bytes 1253384 | tf_op jit(solution)/shard_map/ppermute | solution.py:426
  90.7 21.6 %collective-permute-start.16 = (s16[272,768]{1,0:T(8,128)(2,1)}, s16[272,768]{1,0:T(8,128)(2,1)S(1)}, u32[]{:S(2)}, u32[]{:S(2)}) collective-permute-start(s16[272,768]{1,0:T(8,128)(2,1)} %get-tuple-element.53), channel_id=1, source_target_pairs={{24,16},{8,0},{17,25},{1,9},{10,2},{26,18},{3,11},{19,27},{4,12},{... | collective-permute-start | bytes 1253384 | tf_op jit(solution)/shard_map/ppermute | solution.py:426
  92.8 14.0 %collective-permute-start.3 = (s16[272,512]{1,0:T(8,128)(2,1)}, s16[272,512]{1,0:T(8,128)(2,1)S(1)}, u32[]{:S(2)}, u32[]{:S(2)}) collective-permute-start(s16[272,512]{1,0:T(8,128)(2,1)} %get-tuple-element.36), channel_id=1, source_target_pairs={{8,0},{24,16},{1,9},{17,25},{26,18},{10,2},{19,27},{3,11},{12,4},{... | collective-permute-start | bytes 835592 | tf_op jit(solution)/shard_map/ppermute | solution.py:418
  106.8 0.7 copy-start
  107.5 1.0 copy-start.1
  109.3 18.6 %collective-permute-start.4 = (s16[272,512]{1,0:T(8,128)(2,1)}, s16[272,512]{1,0:T(8,128)(2,1)}, u32[]{:S(2)}, u32[]{:S(2)}) collective-permute-start(s16[272,512]{1,0:T(8,128)(2,1)} %get-tuple-element.38), channel_id=1, source_target_pairs={{16,0},{25,9},{2,18},{11,27},{20,4},{29,13},{6,22},{15,31}} | collective-permute-start | bytes 835592 | tf_op jit(solution)/shard_map/ppermute | solution.py:420
  111.6 16.3 %collective-permute-start.11 = (s16[272,512]{1,0:T(8,128)(2,1)}, s16[272,512]{1,0:T(8,128)(2,1)S(1)}, u32[]{:S(2)}, u32[]{:S(2)}) collective-permute-start(s16[272,512]{1,0:T(8,128)(2,1)} %get-tuple-element.47), channel_id=1, source_target_pairs={{24,8},{17,1},{10,26},{3,19},{4,20},{13,29},{22,6},{31,15},{8,10},... | collective-permute-start | bytes 835592 | tf_op jit(solution)/shard_map/ppermute | solution.py:429
  113.3 14.7 %collective-permute-start.17 = (s16[272,512]{1,0:T(8,128)(2,1)}, s16[272,512]{1,0:T(8,128)(2,1)S(1)}, u32[]{:S(2)}, u32[]{:S(2)}) collective-permute-start(s16[272,512]{1,0:T(8,128)(2,1)} %get-tuple-element.55), channel_id=1, source_target_pairs={{0,16},{9,25},{18,2},{27,11},{28,12},{21,5},{14,30},{7,23},{16,17}... | collective-permute-start | bytes 835592 | tf_op jit(solution)/shard_map/ppermute | solution.py:429
  119.4 8.5 %collective-permute-start.12 = (s16[272,256]{1,0:T(8,128)(2,1)}, s16[272,256]{1,0:T(8,128)(2,1)S(1)}, u32[]{:S(2)}, u32[]{:S(2)}) collective-permute-start(s16[272,256]{1,0:T(8,128)(2,1)} %get-tuple-element.48), channel_id=1, source_target_pairs={{24,10},{17,3},{10,24},{3,17},{4,21},{13,28},{22,7},{31,14}} | collective-permute-start | bytes 417800 | tf_op jit(solution)/shard_map/ppermute | solution.py:430
  120.1 7.8 %collective-permute-start.18 = (s16[272,256]{1,0:T(8,128)(2,1)S(1)}, s16[272,256]{1,0:T(8,128)(2,1)S(1)}, u32[]{:S(2)}, u32[]{:S(2)}) collective-permute-start(s16[272,256]{1,0:T(8,128)(2,1)S(1)} %get-tuple-element.56), channel_id=1, source_target_pairs={{0,17},{9,24},{18,3},{27,10},{28,14},{21,7},{14,28},{7,21}} | collective-permute-start | bytes 417800 | tf_op jit(solution)/shard_map/ppermute | solution.py:430

commit v4 on v3

--- a/solution.py
+++ b/solution.py
@@ -26,7 +26,6 @@
     cols_ref, pick_ref = refs.pop(0), refs.pop(0)
     mass_hbm = refs.pop(0)
     pieces = [refs.pop(0) for _ in range(plan["count"])]
-    own_ref = refs.pop(0) if plan["own"] else None
     made_ref = refs.pop(0)
     keep_ref, send_ref = (refs.pop(0), refs.pop(0)) if plan["multiplies"] else (None, None)
     rows_ref = refs.pop(0)
@@ -37,8 +36,8 @@
     used = iter(range(64))
     fetch = lambda source, target: pltpu.make_async_copy(source, target, sems.at[next(used)])
     rows_in = [
-        fetch(pieces[p].at[span(r, n), :], rows_ref.at[span(to, n), span(lane, pieces[p].shape[1])])
-        for p, r, n, to, lane in plan["places"]
+        fetch(pieces[p].at[span(r, n), span(c, w)], rows_ref.at[span(to, n), span(lane, w)])
+        for p, (r, n), (c, w), to, lane in plan["places"]
     ]
     mass_in, parts = [], plan["parts"]
     size = mass_ref.shape[0] // parts
@@ -64,82 +63,97 @@
         made_ref[row * blk : (row + 1) * blk, :] = product.astype(made_ref.dtype)
 
     if plan["multiplies"]:
-        w_ref = own_ref if plan["own"] else made_ref
-        own, nodes = w_ref.shape[1], w_ref.shape[0]
+        own, nodes = made_ref.shape[1], made_ref.shape[0]
         for target, first in ((keep_ref, pick_ref[0]), (send_ref, 1 - pick_ref[0])):
             left = rows_ref[span(rim, nodes), pl.ds(pl.multiple_of(first * half, half), half)]
-            target[:, :own] = contract_nodes(left, w_ref[...])
-            if plan["own"]:
-                right = made_ref[:, pl.ds(pl.multiple_of((1 - first) * half, half), half)]
-                target[:, own:] = contract_nodes(left, right)
+            target[:, :own] = contract_nodes(left, made_ref[...])
 
 
 def in_hbm(array):
     return pltpu.with_memory_space_constraint(array, pltpu.HBM)
 
 
-def parts_body(source, *refs):
+def parts_body(cuts, source, *refs):
     targets, sems = refs[:-1], refs[-1]
-    nodes, width = source.shape
-    rim = targets[-1].shape[0]
-    half = width // 2
-    pieces = [
-        source.at[:, :half],
-        source.at[:, half:],
-        source.at[span(nodes - rim, rim), :],
-        source.at[span(0, rim), :],
-    ]
-    copies = [
-        pltpu.make_async_copy(piece, target, sems.at[i])
-        for i, (piece, target) in enumerate(zip(pieces, targets))
-    ]
+    copies = []
+    for pieces, target in zip(cuts, targets):
+        done = 0
+        for (r, n), (c, w) in pieces:
+            copies.append(
+                pltpu.make_async_copy(
+                    source.at[span(r, n), span(c, w)],
+                    target.at[span(done, n), :],
+                    sems.at[len(copies)],
+                )
+            )
+            done += n
     for copy in copies:
         copy.start()
     for copy in copies:
         copy.wait()
 
 
-def parts_of(snapshots, rim):
-    nodes, width = snapshots.shape
-    shapes = [(nodes, width // 2)] * 2 + [(rim, width)] * 2
-    return pl.pallas_call(
-        parts_body,
+def parts_of(array, *cuts):
+    shapes = [(sum(n for (_, n), _ in pieces), pieces[0][1][1]) for pieces in cuts]
+    return pl.pallas_call(
+        functools.partial(parts_body, cuts),
         in_specs=[pl.BlockSpec(memory_space=pl.ANY)],
-        out_specs=[pl.BlockSpec(memory_space=pltpu.VMEM)] * 4,
-        out_shape=[pltpu.VMEM(shape, snapshots.dtype) for shape in shapes],
-        scratch_shapes=[pltpu.SemaphoreType.DMA((4,))],
+        out_specs=[pl.BlockSpec(memory_space=pltpu.VMEM)] * len(cuts),
+        out_shape=[pltpu.VMEM(shape, array.dtype) for shape in shapes],
+        scratch_shapes=[pltpu.SemaphoreType.DMA((sum(len(pieces) for pieces in cuts),))],
         compiler_params=pltpu.CompilerParams(vmem_limit_bytes=4 << 20),
-        name="parts",
-    )(in_hbm(snapshots))
+    )(in_hbm(array))
+
+
+def rims_body(*refs):
+    edges, (last_ref, first_ref) = refs[:-2], refs[-2:]
+    rim = last_ref.shape[0]
+    lane = 0
+    for edge in edges:
+        place = span(lane, edge.shape[1])
+        first_ref[:, place] = edge[:rim, :]
+        last_ref[:, place] = edge[rim:, :]
+        lane += edge.shape[1]
+
+
+def rims_of(*edges):
+    vmem = pl.BlockSpec(memory_space=pltpu.VMEM)
+    shape = (edges[0].shape[0] // 2, sum(edge.shape[1] for edge in edges))
+    return pl.pallas_call(
+        rims_body,
+        in_specs=[vmem] * len(edges),
+        out_specs=[vmem] * 2,
+        out_shape=[pltpu.VMEM(shape, edges[0].dtype)] * 2,
+        compiler_params=pltpu.CompilerParams(vmem_limit_bytes=4 << 20),
+        name="rims",
+    )(*(in_vmem(edge) for edge in edges))
 
 
 def in_vmem(array):
     return pltpu.with_memory_space_constraint(array, pltpu.VMEM)
 
 
-def fused(local_cols, pick, mass_blocks, pieces, places, own=None, multiplies=True):
+def fused(local_cols, pick, mass_blocks, pieces, places, multiplies=True, hands_out=False):
     block_rows, blk, stored = mass_blocks.shape
     rim = HB * blk
     nodes = block_rows * blk
-    width = max(lane + pieces[p].shape[1] for p, _, _, _, lane in places)
+    width = max(lane + w for _, _, (_, w), _, lane in places)
     half = width // 2
-    row_count = max(to + n for _, _, n, to, _ in places)
+    row_count = max(to + n for _, (_, n), _, to, _ in places)
     parts = 4 if block_rows % 4 == 0 else 1
     plan = dict(
         blk=blk, rim=rim, half=half, multiplies=multiplies, places=places, count=len(pieces),
-        own=own is not None, parts=parts,
-    )
-    total = width + half if own is not None else width
+        parts=parts,
+    )
     operands = [in_hbm(mass_blocks), *pieces]
     specs = [pl.BlockSpec(memory_space=pl.ANY)] * len(operands)
-    if own is not None:
-        operands.append(in_vmem(own))
-        specs.append(pl.BlockSpec(memory_space=pltpu.VMEM))
     outs = [pltpu.VMEM((nodes, width), jnp.bfloat16)]
     flops = 8 * nodes * stored * width
     if multiplies:
-        outs += [pltpu.VMEM((half, total), jnp.float32)] * 2
-        flops += 4 * nodes * half * total
+        outs += [pltpu.VMEM((half, width), jnp.float32)] * 2
+        flops += 4 * nodes * half * width
+    rows = [pltpu.VMEM((row_count, width), jnp.bfloat16)]
+    outs, scratch = (outs + rows, []) if hands_out else (outs, rows)
     return pl.pallas_call(
         functools.partial(fused_body, plan),
         grid_spec=pltpu.PrefetchScalarGridSpec(
@@ -148,7 +162,7 @@
             in_specs=specs,
             out_specs=[pl.BlockSpec(memory_space=pltpu.VMEM)] * len(outs),
             scratch_shapes=[
-                pltpu.VMEM((row_count, width), jnp.bfloat16),
+                *scratch,
                 pltpu.VMEM(mass_blocks.shape, jnp.bfloat16),
                 pltpu.SemaphoreType.DMA((len(places) + parts,)),
             ],
@@ -175,6 +189,32 @@
     def _():
         multiply(keep_ref, left_b, 0)
         multiply(send_ref, left_a, half)
+
+
+def products_of_rows_body(rim, pick_ref, rows_ref, w_ref, x_ref, keep_ref, send_ref):
+    own, nodes, half = w_ref.shape[1], w_ref.shape[0], x_ref.shape[1] // 2
+    for target, first in ((keep_ref, pick_ref[0]), (send_ref, 1 - pick_ref[0])):
+        left = rows_ref[span(rim, nodes), pl.ds(pl.multiple_of(first * half, half), half)]
+        target[:, :own] = contract_nodes(left, w_ref[...])
+        right = x_ref[:, pl.ds(pl.multiple_of((1 - first) * half, half), half)]
+        target[:, own:] = contract_nodes(left, right)
+
+
+def products_of_rows(pick, rows, rim, w, x):
+    nodes, own = w.shape
+    half = x.shape[1] // 2
+    vmem = pl.BlockSpec(memory_space=pltpu.VMEM)
+    return pl.pallas_call(
+        functools.partial(products_of_rows_body, rim),
+        grid_spec=pltpu.PrefetchScalarGridSpec(
+            num_scalar_prefetch=1, grid=(), in_specs=[vmem] * 3, out_specs=[vmem] * 2
+        ),
+        out_shape=[pltpu.VMEM((half, own + half), jnp.float32)] * 2,
+        cost_estimate=pl.CostEstimate(
+            flops=4 * nodes * half * (own + half), bytes_accessed=8 << 20, transcendentals=0
+        ),
+        compiler_params=pltpu.CompilerParams(vmem_limit_bytes=16 << 20),
+    )(pick, *(in_vmem(array) for array in (rows, w, x)))
 
 
 def products(pick, left_a, left_b, w, x):
@@ -380,18 +420,26 @@
 
     pick = core[None].astype(jnp.int32)
     shards = 2 * chips
-    left, right, last_rows, first_rows = parts_of(snapshots, rim)
-    a1 = over_x(left)
-    b2 = over_y(right)
+    west, east = (0, half), (half, half)
+    middle = (rim, node_count - 2 * rim)
+    ends = (0, rim), (node_count - rim, rim)
+    left_edge, right_edge = parts_of(
+        snapshots, *(tuple((end, side) for end in ends) for side in (west, east))
+    )
+    a_edge = over_x(left_edge)
+    b_edge = over_y(right_edge)
+    left_middle, right_middle = parts_of(snapshots, ((middle, west),), ((middle, east),))
+    a1 = over_x(left_middle)
+    b2 = over_y(right_middle)
+    last_rows, first_rows = rims_of(left_edge, right_edge, a_edge, b_edge)
     low = lax.ppermute(last_rows, "mesh", [(i, i + 1) for i in range(shards - 1)])
     high = lax.ppermute(first_rows, "mesh", [(i + 1, i) for i in range(shards - 1)])
-    rims = jnp.concatenate([low, high], axis=0)
-    ra = over_x(rims[:, :half])
-    rb = over_y(rims[:, half:])
+    left, right = parts_of(snapshots, (((0, node_count), west),), (((0, node_count), east),))
     a2 = over_x(right)
     b1 = over_y(left)
 
     top = rim + node_count
+    all_rows, every = (0, rim), (0, column_count)
 
     def towards(core_a):
         return lambda c, q: q ^ jnp.where(c == core_a, X, Y) if is_traced(c) else q ^ (X, Y)[c != core_a]
@@ -401,16 +449,27 @@
 
     w, keep0, send0 = fused(
         local_cols, pick, mass_blocks, [low, in_hbm(snapshots), high],
-        [(0, 0, rim, 0, 0), (1, 0, node_count, rim, 0), (2, 0, rim, top, 0)],
-    )
-    wx, keep1, send1 = fused(
-        local_cols, pick, mass_blocks, [a1, ra, b2, rb],
         [
-            (0, 0, node_count, rim, 0), (1, 0, rim, 0, 0), (1, rim, rim, top, 0),
-            (2, 0, node_count, rim, half), (3, 0, rim, 0, half), (3, rim, rim, top, half),
+            (0, all_rows, every, 0, 0), (1, (0, node_count), every, rim, 0),
+            (2, all_rows, every, top, 0),
         ],
-        own=w,
-    )
+    )
+    beyond = (column_count, column_count)
+    near_rows = [
+        (piece, rows, (0, half), rim + to, lane)
+        for edge, inner, lane in ((2, 3, 0), (4, 5, half))
+        for piece, rows, to in (
+            (edge, (0, rim), 0),
+            (inner, (0, node_count - 2 * rim), rim),
+            (edge, (rim, rim), node_count - rim),
+        )
+    ]
+    wx, rows = fused(
+        local_cols, pick, mass_blocks, [low, high, a_edge, a1, b_edge, b2],
+        [(0, all_rows, beyond, 0, 0), (1, all_rows, beyond, top, 0), *near_rows],
+        multiplies=False, hands_out=True,
+    )
+    keep1, send1 = products_of_rows(pick, rows, rim, w, wx)
     keep2, send2 = products(1 - pick, a2, b1, w, wx)
     own_target = lambda c, q: q
     came = lax.ppermute(send0, "mesh", cores)
@@ -438,7 +497,7 @@
 
 
 def on_device(snapshots, block_cols, mass_blocks):
-    node_count, _ = snapshots.shape
+    node_count, column_count = snapshots.shape
     blk = mass_blocks.shape[1]
     blocks_here = node_count // blk
     rim = HB * blk
@@ -448,7 +507,11 @@
     local_cols = block_cols - (lax.axis_index("mesh") * blocks_here - HB)
     (weighted,) = fused(
         local_cols, jnp.zeros((1,), jnp.int32), mass_blocks, [low, snapshots, high],
-        [(0, 0, rim, 0, 0), (1, 0, node_count, rim, 0), (2, 0, rim, rim + node_count, 0)],
+        [
+            (0, (0, rim), (0, column_count), 0, 0),
+            (1, (0, node_count), (0, column_count), rim, 0),
+            (2, (0, rim), (0, column_count), rim + node_count, 0),
+        ],
         multiplies=False,
     )
     gathered = lax.all_gather(snapshots, "run", axis=1, tiled=True)

time: 130 us -> 111 us (0.85)
  waiting for transfers between devices: 58.9 us -> 34.6 us
  Pallas kernels: 32.6 us -> 36.7 us
  starting transfers between devices: 35.5 us -> 37.1 us
    ppermute x3, waiting for transfers between devices: 42.6 us -> 2.34 us  [over_y(): return lax.ppermute(v, 'run', across(Y))]
    ppermute x3, waiting for transfers between devices: 0.01 us -> 16.9 us  [over_x(): return lax.ppermute(v, 'run', across(X))]
    pallas_call x1 -> x5, Pallas kernels: 2.61 us -> 7.9 us  [the longest x3 5.22 us: parts_of(): pl.pallas_call(functools.partial(parts_body, cuts), in_specs=[pl.BlockSpe...]
    ppermute x2, starting transfers between devices: 1.4 us -> 3.44 us  [finished(): came = lax.ppermute(sent, 'mesh', cores)]
  transfers between devices with their start and end apart: 19 -> 19, of which waited for: 3 -> 8; matrix products, arithmetic and copies ran while one was open for 1% -> 0% of each run, Pallas kernels for 22% -> 30%
where the time goes in v4:
time: 111 us; the launch traced here: 110 us
  starting transfers between devices  37.1 us (33%)
  Pallas kernels  36.7 us (33%)
  waiting for transfers between devices  34.6 us (31%)
  local copies, waits for them, and re-layouts  1.76 us (2%)
    pallas_call x2, Pallas kernels, fused(): pl.pallas_call(functools.partial(fused_body, plan), grid_spec=pltpu.Prefe...  19.4 us
    ppermute x3, waiting for transfers between devices, over_x(): return lax.ppermute(v, 'run', across(X))  16.9 us
    ppermute x1, waiting for transfers between devices, on_square(): came = lax.ppermute(coded, both, line(own_target, 0))  12.6 us
    ppermute x2, starting transfers between devices, finished(): leg = lax.ppermute(leg, both, line(target, 1) + corner(target, bit))  6.83 us
    ppermute x2, starting transfers between devices, finished(): came = lax.ppermute(coded, both, line(target, 0))  6.26 us
    ppermute x2, starting transfers between devices, finished(): far = lax.ppermute(far, both, around(target, bit))  5.72 us
    pallas_call x3, Pallas kernels, parts_of(): pl.pallas_call(functools.partial(parts_body, cuts), in_specs=[pl.BlockSpe...  5.22 us
    ppermute x3, starting transfers between devices, over_x(): return lax.ppermute(v, 'run', across(X))  5 us
  transfers between devices with their start and end apart: 19, of which 8 were waited for; matrix products, arithmetic and copies ran while one was open for 0% of the time, Pallas kernels for 30%

profile of v4, /device:TPU:0, one launch (start us, length us, event | category | flops | bytes accessed | tf_op | source)
XLA Modules:
  0.0 110.3 jit_solution(3788219161935239836)
XLA Ops:
  1.0 3.0 %collective-permute-start = (bf16[256,256]{1,0:T(8,128)(2,1)S(1)}, bf16[256,256]{1,0:T(8,128)(2,1)S(1)}, u32[]{:S(2)}, u32[]{:S(2)}) collective-permute-start(bf16[256,256]{1,0:T(8,128)(2,1)S(1)} %get-tuple-element.36.refs_0_), channel_id=1, source_target_pairs={{0,1},{1,0},{2,3},{3,2},{4,5},{5,4},{6,7},{7,6},{8,9},{9,8},{10,11... | collective-permute-start | bytes 393224 | tf_op jit(solution)/shard_map/ppermute | solution.py:416
  4.0 1.5 %collective-permute-start.1 = (bf16[256,256]{1,0:T(8,128)(2,1)S(1)}, bf16[256,256]{1,0:T(8,128)(2,1)S(1)}, u32[]{:S(2)}, u32[]{:S(2)}) collective-permute-start(bf16[256,256]{1,0:T(8,128)(2,1)S(1)} %get-tuple-element.37.refs_1_), channel_id=1, source_target_pairs={{0,2},{1,3},{2,0},{3,1},{4,6},{5,7},{6,4},{7,5},{8,10},{9,11},{10,... | collective-permute-start | bytes 393224 | tf_op jit(solution)/shard_map/ppermute | solution.py:419
  5.5 2.0 %collective-permute-done.refs_2_.refs_5_ = bf16[256,256]{1,0:T(8,128)(2,1)S(1)} collective-permute-done((bf16[256,256]{1,0:T(8,128)(2,1)S(1)}, bf16[256,256]{1,0:T(8,128)(2,1)S(1)}, u32[]{:S(2)}, u32[]{:S(2)}) %collective-permute-start) | collective-permute-done | bytes 131104 | tf_op jit(solution)/shard_map/ppermute | solution.py:416
  7.5 1.5 %collective-permute-done.1.refs_3_.refs_7_ = bf16[256,256]{1,0:T(8,128)(2,1)S(1)} collective-permute-done((bf16[256,256]{1,0:T(8,128)(2,1)S(1)}, bf16[256,256]{1,0:T(8,128)(2,1)S(1)}, u32[]{:S(2)}, u32[]{:S(2)}) %collective-permute-start.1) | collective-permute-done | bytes 131104 | tf_op jit(solution)/shard_map/ppermute | solution.py:419
  9.8 2.0 %collective-permute-start.2 = (bf16[128,1024]{1,0:T(8,128)(2,1)}, bf16[128,1024]{1,0:T(8,128)(2,1)}, u32[]{:S(2)}, u32[]{:S(2)}) collective-permute-start(bf16[128,1024]{1,0:T(8,128)(2,1)} %get-tuple-element.38), channel_id=1, source_target_pairs={{0,4},{4,8},{8,12},{12,16},{16,20},{20,24},{24,28},{1,5},{5,9},{9,... | collective-permute-start | bytes 786440 | tf_op jit(solution)/shard_map/ppermute | solution.py:435
  11.8 1.4 %collective-permute-start.3 = (bf16[128,1024]{1,0:T(8,128)(2,1)}, bf16[128,1024]{1,0:T(8,128)(2,1)}, u32[]{:S(2)}, u32[]{:S(2)}) collective-permute-start(bf16[128,1024]{1,0:T(8,128)(2,1)} %get-tuple-element.39), channel_id=1, source_target_pairs={{4,0},{8,4},{12,8},{16,12},{20,16},{24,20},{28,24},{5,1},{9,5},{13... | collective-permute-start | bytes 786440 | tf_op jit(solution)/shard_map/ppermute | solution.py:436
  13.2 2.7 %shard_map.41 = (bf16[1792,256]{1,0:T(8,128)(2,1)}, bf16[1792,256]{1,0:T(8,128)(2,1)}) custom-call(bf16[2048,512]{1,0:T(8,128)(2,1)} %source.5), custom_call_target="tpu_custom_call" | custom-call | tf_op jit(solution)/shard_map/pallas_call | solution.py:98
  16.4 1.7 %collective-permute-start.8 = (bf16[1792,256]{1,0:T(8,128)(2,1)}, bf16[1792,256]{1,0:T(8,128)(2,1)}, u32[]{:S(2)}, u32[]{:S(2)}) collective-permute-start(bf16[1792,256]{1,0:T(8,128)(2,1)} %get-tuple-element.47), channel_id=1, source_target_pairs={{0,2},{1,3},{2,0},{3,1},{4,6},{5,7},{6,4},{7,5},{8,10},{9,11},{10,... | collective-permute-start | bytes 2752520 | tf_op jit(solution)/shard_map/ppermute | solution.py:419
  18.1 1.6 %shard_map.46 = (bf16[2048,256]{1,0:T(8,128)(2,1)S(1)}, bf16[2048,256]{1,0:T(8,128)(2,1)S(1)}) custom-call(bf16[2048,512]{1,0:T(8,128)(2,1)} %source.5), custom_call_target="tpu_custom_call" | custom-call | tf_op jit(solution)/shard_map/pallas_call | solution.py:98
  19.6 1.6 %collective-permute-start.13 = (bf16[2048,256]{1,0:T(8,128)(2,1)S(1)}, bf16[2048,256]{1,0:T(8,128)(2,1)S(1)}, u32[]{:S(2)}, u32[]{:S(2)}) collective-permute-start(bf16[2048,256]{1,0:T(8,128)(2,1)S(1)} %get-tuple-element.58), channel_id=1, source_target_pairs={{0,1},{1,0},{2,3},{3,2},{4,5},{5,4},{6,7},{7,6},{8,9},{9,8},{10,11... | collective-permute-start | bytes 3145736 | tf_op jit(solution)/shard_map/ppermute | solution.py:416
  21.8 10.2 %shard_map.38 = (bf16[2048,512]{1,0:T(8,128)(2,1)S(1)}, f32[256,512]{1,0:T(8,128)S(1)}, f32[256,512]{1,0:T(8,128)S(1)}) custom-call(s32[32,16]{1,0:T(8,128)S(1)} %broadcast_subtract_fusion.refs_0_, s32[1]{0:T(128)} %bitcast.1.refs_1_.pick_ref, bf16[32,64,1024]{2,1,0:T(8,128)(2,1)} %refs_2_.3, bf16[128,1024]{1,0:T(8,128)(2,1)} %collective-permute-done.2.refs_3_, ...), custom_call_target="tpu_custom_call" | custom-call | flops 9663676416 | bytes 8388608 | tf_op jit(solution)/shard_map/pallas_call | solution.py:157
  32.1 6.3 %collective-permute-done.7.refs_6_ = bf16[1792,256]{1,0:T(8,128)(2,1)} collective-permute-done((bf16[1792,256]{1,0:T(8,128)(2,1)}, bf16[1792,256]{1,0:T(8,128)(2,1)}, u32[]{:S(2)}, u32[]{:S(2)}) %collective-permute-start.7) | collective-permute-done | bytes 917536 | tf_op jit(solution)/shard_map/ppermute | solution.py:416
  38.8 9.2 %shard_map.42 = (bf16[2048,512]{1,0:T(8,128)(2,1)S(1)}, bf16[2304,512]{1,0:T(8,128)(2,1)S(1)}) custom-call(s32[32,16]{1,0:T(8,128)S(1)} %broadcast_subtract_fusion.refs_0_, s32[1]{0:T(128)} %bitcast.1.refs_1_.pick_ref, bf16[32,64,1024]{2,1,0:T(8,128)(2,1)} %refs_2_.3, bf16[128,1024]{1,0:T(8,128)(2,1)} %collective-permute-done.2.refs_3_, ...), custom_call_target="tpu_custom_call" | custom-call | flops 8589934592 | bytes 8388608 | tf_op jit(solution)/shard_map/pallas_call | solution.py:157
  48.1 1.8 %shard_map.43 = (f32[256,768]{1,0:T(8,128)S(1)}, f32[256,768]{1,0:T(8,128)S(1)}) custom-call(s32[1]{0:T(128)} %bitcast.1.refs_1_.pick_ref, bf16[2304,512]{1,0:T(8,128)(2,1)S(1)} %get-tuple-element.48.rows_ref, bf16[2048,512]{1,0:T(8,128)(2,1)S(1)} %get-tuple-element.49.w_ref, bf16[2048,512]{1,0:T(8,128)(2,1)S(1)} %get-tuple-element.50.x_ref), custom_call_target="tpu_custom_call" | custom-call | flops 1610612736 | bytes 8388608 | tf_op jit(solution)/shard_map/pallas_call | solution.py:207
  49.9 2.3 %collective-permute-start.9 = (f32[256,768]{1,0:T(8,128)S(1)}, f32[256,768]{1,0:T(8,128)S(1)}, u32[]{:S(2)}, u32[]{:S(2)}) collective-permute-start(f32[256,768]{1,0:T(8,128)S(1)} %get-tuple-element.52), channel_id=1, source_target_pairs={{0,4},{4,0},{8,12},{12,8},{16,20},{20,16},{24,28},{28,24},{1,5},{5... | collective-permute-start | bytes 2359304 | tf_op jit(solution)/shard_map/ppermute | solution.py:483
  52.2 8.6 %collective-permute-done.13.left_a = bf16[2048,256]{1,0:T(8,128)(2,1)S(1)} collective-permute-done((bf16[2048,256]{1,0:T(8,128)(2,1)S(1)}, bf16[2048,256]{1,0:T(8,128)(2,1)S(1)}, u32[]{:S(2)}, u32[]{:S(2)}) %collective-permute-start.13) | collective-permute-done | bytes 1048608 | tf_op jit(solution)/shard_map/ppermute | solution.py:416
  61.2 1.8 %shard_map.47 = (f32[256,768]{1,0:T(8,128)S(1)}, f32[256,768]{1,0:T(8,128)S(1)}) custom-call(s32[1]{0:T(128)S(6)} %sub.20.pick_ref, bf16[2048,256]{1,0:T(8,128)(2,1)S(1)} %collective-permute-done.13.left_a, bf16[2048,256]{1,0:T(8,128)(2,1)S(1)} %collective-permute-done.14.left_b, bf16[2048,512]{1,0:T(8,128)(2,1)S(1)} %get-tuple-element.49.w_ref, ...), custom_call_target="tpu_custom_call" | custom-call | flops 1610612736 | bytes 8388608 | tf_op jit(solution)/shard_map/pallas_call | solution.py:224
  65.2 5.0 %collective-permute-start.10 = (s16[272,768]{1,0:T(8,128)(2,1)}, s16[272,768]{1,0:T(8,128)(2,1)S(1)}, u32[]{:S(2)}, u32[]{:S(2)}) collective-permute-start(s16[272,768]{1,0:T(8,128)(2,1)} %get-tuple-element.54), channel_id=1, source_target_pairs={{0,8},{16,24},{9,1},{25,17},{18,26},{2,10},{27,19},{11,3},{28,20},... | collective-permute-start | bytes 1253384 | tf_op jit(solution)/shard_map/ppermute | solution.py:485
  71.2 1.3 %collective-permute-start.16 = (s16[272,768]{1,0:T(8,128)(2,1)}, s16[272,768]{1,0:T(8,128)(2,1)S(1)}, u32[]{:S(2)}, u32[]{:S(2)}) collective-permute-start(s16[272,768]{1,0:T(8,128)(2,1)} %get-tuple-element.63), channel_id=1, source_target_pairs={{24,16},{8,0},{17,25},{1,9},{10,2},{26,18},{3,11},{19,27},{4,12},{... | collective-permute-start | bytes 1253384 | tf_op jit(solution)/shard_map/ppermute | solution.py:485
  74.7 12.6 %collective-permute-done.5.came_ref = s16[272,512]{1,0:T(8,128)(2,1)S(1)} collective-permute-done((s16[272,512]{1,0:T(8,128)(2,1)}, s16[272,512]{1,0:T(8,128)(2,1)S(1)}, u32[]{:S(2)}, u32[]{:S(2)}) %collective-permute-start.5) | collective-permute-done | bytes 278560 | tf_op jit(solution)/shard_map/ppermute | solution.py:477
  93.8 6.2 %collective-permute-start.17 = (s16[272,512]{1,0:T(8,128)(2,1)}, s16[272,512]{1,0:T(8,128)(2,1)S(1)}, u32[]{:S(2)}, u32[]{:S(2)}) collective-permute-start(s16[272,512]{1,0:T(8,128)(2,1)} %get-tuple-element.65), channel_id=1, source_target_pairs={{0,16},{9,25},{18,2},{27,11},{28,12},{21,5},{14,30},{7,23},{16,17}... | collective-permute-start | bytes 835592 | tf_op jit(solution)/shard_map/ppermute | solution.py:488
  100.7 5.1 %collective-permute-start.18 = (s16[272,256]{1,0:T(8,128)(2,1)S(1)}, s16[272,256]{1,0:T(8,128)(2,1)S(1)}, u32[]{:S(2)}, u32[]{:S(2)}) collective-permute-start(s16[272,256]{1,0:T(8,128)(2,1)S(1)} %get-tuple-element.66), channel_id=1, source_target_pairs={{0,17},{9,24},{18,3},{27,10},{28,14},{21,7},{14,28},{7,21}} | collective-permute-start | bytes 417800 | tf_op jit(solution)/shard_map/ppermute | solution.py:489
  105.8 2.7 %collective-permute-done.6.own_came = s16[272,512]{1,0:T(8,128)(2,1)} collective-permute-done((s16[272,512]{1,0:T(8,128)(2,1)}, s16[272,512]{1,0:T(8,128)(2,1)}, u32[]{:S(2)}, u32[]{:S(2)}) %collective-permute-start.6) | collective-permute-done | bytes 278560 | tf_op jit(solution)/shard_map/ppermute | solution.py:479
  108.5 1.8 %close.1 = f32[256,512]{1,0:T(8,128)} custom-call(s32[1]{0:T(128)} %bitcast.case_ref, f32[256,512]{1,0:T(8,128)S(1)} %get-tuple-element.44.own, s16[272,512]{1,0:T(8,128)(2,1)} %collective-permute-done.6.own_came, f32[256,512]{1,0:T(8,128)S(1)} %get-tuple-element.55.near1, s16[272,512]{1,0:T(8,128)(2,1)S(1)} %collective-permute-done.11.leg1, ...), custom_call_target="tpu_custom_call" | custom-call | tf_op jit(solution)/shard_map/close/pallas_call | solution.py:350
  (37 shorter events, 16.3 us)
Async XLA Ops:
  1.0 6.5 %collective-permute-start = (bf16[256,256]{1,0:T(8,128)(2,1)S(1)}, bf16[256,256]{1,0:T(8,128)(2,1)S(1)}, u32[]{:S(2)}, u32[]{:S(2)}) collective-permute-start(bf16[256,256]{1,0:T(8,128)(2,1)S(1)} %get-tuple-element.36.refs_0_), channel_id=1, source_target_pairs={{0,1},{1,0},{2,3},{3,2},{4,5},{5,4},{6,7},{7,6},{8,9},{9,8},{10,11... | collective-permute-start | bytes 393224 | tf_op jit(solution)/shard_map/ppermute | solution.py:416
  4.0 5.0 %collective-permute-start.1 = (bf16[256,256]{1,0:T(8,128)(2,1)S(1)}, bf16[256,256]{1,0:T(8,128)(2,1)S(1)}, u32[]{:S(2)}, u32[]{:S(2)}) collective-permute-start(bf16[256,256]{1,0:T(8,128)(2,1)S(1)} %get-tuple-element.37.refs_1_), channel_id=1, source_target_pairs={{0,2},{1,3},{2,0},{3,1},{4,6},{5,7},{6,4},{7,5},{8,10},{9,11},{10,... | collective-permute-start | bytes 393224 | tf_op jit(solution)/shard_map/ppermute | solution.py:419
  9.8 11.4 %collective-permute-start.2 = (bf16[128,1024]{1,0:T(8,128)(2,1)}, bf16[128,1024]{1,0:T(8,128)(2,1)}, u32[]{:S(2)}, u32[]{:S(2)}) collective-permute-start(bf16[128,1024]{1,0:T(8,128)(2,1)} %get-tuple-element.38), channel_id=1, source_target_pairs={{0,4},{4,8},{8,12},{12,16},{16,20},{20,24},{24,28},{1,5},{5,9},{9,... | collective-permute-start | bytes 786440 | tf_op jit(solution)/shard_map/ppermute | solution.py:435
  11.8 9.4 %copy-start.2 = (s32[32,16]{0,1:T(8,128)S(1)}, s32[32,16]{0,1:T(8,128)}, u32[]{:S(2)}) copy-start(s32[32,16]{0,1:T(8,128)} %param.4) | copy-start | bytes 6148
  11.8 10.0 %collective-permute-start.3 = (bf16[128,1024]{1,0:T(8,128)(2,1)}, bf16[128,1024]{1,0:T(8,128)(2,1)}, u32[]{:S(2)}, u32[]{:S(2)}) collective-permute-start(bf16[128,1024]{1,0:T(8,128)(2,1)} %get-tuple-element.39), channel_id=1, source_target_pairs={{4,0},{8,4},{12,8},{16,12},{20,16},{24,20},{28,24},{5,1},{9,5},{13... | collective-permute-start | bytes 786440 | tf_op jit(solution)/shard_map/ppermute | solution.py:436
  15.9 22.4 %collective-permute-start.7 = (bf16[1792,256]{1,0:T(8,128)(2,1)}, bf16[1792,256]{1,0:T(8,128)(2,1)}, u32[]{:S(2)}, u32[]{:S(2)}) collective-permute-start(bf16[1792,256]{1,0:T(8,128)(2,1)} %get-tuple-element.46), channel_id=1, source_target_pairs={{0,1},{1,0},{2,3},{3,2},{4,5},{5,4},{6,7},{7,6},{8,9},{9,8},{10,11... | collective-permute-start | bytes 2752520 | tf_op jit(solution)/shard_map/ppermute | solution.py:416
  16.4 22.5 %collective-permute-start.8 = (bf16[1792,256]{1,0:T(8,128)(2,1)}, bf16[1792,256]{1,0:T(8,128)(2,1)}, u32[]{:S(2)}, u32[]{:S(2)}) collective-permute-start(bf16[1792,256]{1,0:T(8,128)(2,1)} %get-tuple-element.47), channel_id=1, source_target_pairs={{0,2},{1,3},{2,0},{3,1},{4,6},{5,7},{6,4},{7,5},{8,10},{9,11},{10,... | collective-permute-start | bytes 2752520 | tf_op jit(solution)/shard_map/ppermute | solution.py:419
  19.6 41.1 %collective-permute-start.13 = (bf16[2048,256]{1,0:T(8,128)(2,1)S(1)}, bf16[2048,256]{1,0:T(8,128)(2,1)S(1)}, u32[]{:S(2)}, u32[]{:S(2)}) collective-permute-start(bf16[2048,256]{1,0:T(8,128)(2,1)S(1)} %get-tuple-element.58), channel_id=1, source_target_pairs={{0,1},{1,0},{2,3},{3,2},{4,5},{5,4},{6,7},{7,6},{8,9},{9,8},{10,11... | collective-permute-start | bytes 3145736 | tf_op jit(solution)/shard_map/ppermute | solution.py:416
  21.3 39.9 %collective-permute-start.14 = (bf16[2048,256]{1,0:T(8,128)(2,1)S(1)}, bf16[2048,256]{1,0:T(8,128)(2,1)S(1)}, u32[]{:S(2)}, u32[]{:S(2)}) collective-permute-start(bf16[2048,256]{1,0:T(8,128)(2,1)S(1)} %get-tuple-element.59), channel_id=1, source_target_pairs={{0,2},{1,3},{2,0},{3,1},{4,6},{5,7},{6,4},{7,5},{8,10},{9,11},{10,... | collective-permute-start | bytes 3145736 | tf_op jit(solution)/shard_map/ppermute | solution.py:419
  49.9 14.4 %collective-permute-start.9 = (f32[256,768]{1,0:T(8,128)S(1)}, f32[256,768]{1,0:T(8,128)S(1)}, u32[]{:S(2)}, u32[]{:S(2)}) collective-permute-start(f32[256,768]{1,0:T(8,128)S(1)} %get-tuple-element.52), channel_id=1, source_target_pairs={{0,4},{4,0},{8,12},{12,8},{16,20},{20,16},{24,28},{28,24},{1,5},{5... | collective-permute-start | bytes 2359304 | tf_op jit(solution)/shard_map/ppermute | solution.py:483
  63.0 7.2 %collective-permute-start.15 = (f32[256,768]{1,0:T(8,128)S(1)}, f32[256,768]{1,0:T(8,128)S(1)}, u32[]{:S(2)}, u32[]{:S(2)}) collective-permute-start(f32[256,768]{1,0:T(8,128)S(1)} %get-tuple-element.61), channel_id=1, source_target_pairs={{0,4},{4,0},{8,12},{12,8},{16,20},{20,16},{24,28},{28,24},{1,5},{5... | collective-permute-start | bytes 2359304 | tf_op jit(solution)/shard_map/ppermute | solution.py:483
  64.2 8.3 %collective-permute-start.4 = (f32[256,512]{1,0:T(8,128)S(1)}, f32[256,512]{1,0:T(8,128)S(1)}, u32[]{:S(2)}, u32[]{:S(2)}) collective-permute-start(f32[256,512]{1,0:T(8,128)S(1)} %get-tuple-element.41), channel_id=1, source_target_pairs={{0,4},{4,0},{8,12},{12,8},{16,20},{20,16},{24,28},{28,24},{1,5},{5... | collective-permute-start | bytes 1572872 | tf_op jit(solution)/shard_map/ppermute | solution.py:475
  65.2 25.9 %collective-permute-start.10 = (s16[272,768]{1,0:T(8,128)(2,1)}, s16[272,768]{1,0:T(8,128)(2,1)S(1)}, u32[]{:S(2)}, u32[]{:S(2)}) collective-permute-start(s16[272,768]{1,0:T(8,128)(2,1)} %get-tuple-element.54), channel_id=1, source_target_pairs={{0,8},{16,24},{9,1},{25,17},{18,26},{2,10},{27,19},{11,3},{28,20},... | collective-permute-start | bytes 1253384 | tf_op jit(solution)/shard_map/ppermute | solution.py:485
  71.2 21.7 %collective-permute-start.16 = (s16[272,768]{1,0:T(8,128)(2,1)}, s16[272,768]{1,0:T(8,128)(2,1)S(1)}, u32[]{:S(2)}, u32[]{:S(2)}) collective-permute-start(s16[272,768]{1,0:T(8,128)(2,1)} %get-tuple-element.63), channel_id=1, source_target_pairs={{24,16},{8,0},{17,25},{1,9},{10,2},{26,18},{3,11},{19,27},{4,12},{... | collective-permute-start | bytes 1253384 | tf_op jit(solution)/shard_map/ppermute | solution.py:485
  73.4 13.9 %collective-permute-start.5 = (s16[272,512]{1,0:T(8,128)(2,1)}, s16[272,512]{1,0:T(8,128)(2,1)S(1)}, u32[]{:S(2)}, u32[]{:S(2)}) collective-permute-start(s16[272,512]{1,0:T(8,128)(2,1)} %get-tuple-element.43), channel_id=1, source_target_pairs={{8,0},{24,16},{1,9},{17,25},{26,18},{10,2},{19,27},{3,11},{12,4},{... | collective-permute-start | bytes 835592 | tf_op jit(solution)/shard_map/ppermute | solution.py:477
  87.3 0.7 copy-start
  88.0 1.0 copy-start.1
  89.9 18.6 %collective-permute-start.6 = (s16[272,512]{1,0:T(8,128)(2,1)}, s16[272,512]{1,0:T(8,128)(2,1)}, u32[]{:S(2)}, u32[]{:S(2)}) collective-permute-start(s16[272,512]{1,0:T(8,128)(2,1)} %get-tuple-element.45), channel_id=1, source_target_pairs={{16,0},{25,9},{2,18},{11,27},{20,4},{29,13},{6,22},{15,31}} | collective-permute-start | bytes 835592 | tf_op jit(solution)/shard_map/ppermute | solution.py:479
  92.2 16.3 %collective-permute-start.11 = (s16[272,512]{1,0:T(8,128)(2,1)}, s16[272,512]{1,0:T(8,128)(2,1)S(1)}, u32[]{:S(2)}, u32[]{:S(2)}) collective-permute-start(s16[272,512]{1,0:T(8,128)(2,1)} %get-tuple-element.56), channel_id=1, source_target_pairs={{24,8},{17,1},{10,26},{3,19},{4,20},{13,29},{22,6},{31,15},{8,10},... | collective-permute-start | bytes 835592 | tf_op jit(solution)/shard_map/ppermute | solution.py:488
  93.8 14.7 %collective-permute-start.17 = (s16[272,512]{1,0:T(8,128)(2,1)}, s16[272,512]{1,0:T(8,128)(2,1)S(1)}, u32[]{:S(2)}, u32[]{:S(2)}) collective-permute-start(s16[272,512]{1,0:T(8,128)(2,1)} %get-tuple-element.65), channel_id=1, source_target_pairs={{0,16},{9,25},{18,2},{27,11},{28,12},{21,5},{14,30},{7,23},{16,17}... | collective-permute-start | bytes 835592 | tf_op jit(solution)/shard_map/ppermute | solution.py:488
  100.0 8.5 %collective-permute-start.12 = (s16[272,256]{1,0:T(8,128)(2,1)}, s16[272,256]{1,0:T(8,128)(2,1)S(1)}, u32[]{:S(2)}, u32[]{:S(2)}) collective-permute-start(s16[272,256]{1,0:T(8,128)(2,1)} %get-tuple-element.57), channel_id=1, source_target_pairs={{24,10},{17,3},{10,24},{3,17},{4,21},{13,28},{22,7},{31,14}} | collective-permute-start | bytes 417800 | tf_op jit(solution)/shard_map/ppermute | solution.py:489
  100.7 7.8 %collective-permute-start.18 = (s16[272,256]{1,0:T(8,128)(2,1)S(1)}, s16[272,256]{1,0:T(8,128)(2,1)S(1)}, u32[]{:S(2)}, u32[]{:S(2)}) collective-permute-start(s16[272,256]{1,0:T(8,128)(2,1)S(1)} %get-tuple-element.66), channel_id=1, source_target_pairs={{0,17},{9,24},{18,3},{27,10},{28,14},{21,7},{14,28},{7,21}} | collective-permute-start | bytes 417800 | tf_op jit(solution)/shard_map/ppermute | solution.py:489

commit v5 on v4

--- a/solution.py
+++ b/solution.py
@@ -28,6 +28,7 @@
     pieces = [refs.pop(0) for _ in range(plan["count"])]
     made_ref = refs.pop(0)
     keep_ref, send_ref = (refs.pop(0), refs.pop(0)) if plan["multiplies"] else (None, None)
+    side_ref = refs.pop(0) if plan["hands_out"] else None
     rows_ref = refs.pop(0)
     mass_ref = refs.pop(0)
     sems = refs.pop(0)
@@ -62,6 +63,8 @@
         product = jnp.dot(mass_ref[row], picked, preferred_element_type=jnp.float32)
         made_ref[row * blk : (row + 1) * blk, :] = product.astype(made_ref.dtype)
 
+    if plan["hands_out"]:
+        side_ref[...] = made_ref[:, pl.ds(pl.multiple_of((1 - pick_ref[0]) * half, half), half)]
     if plan["multiplies"]:
         own, nodes = made_ref.shape[1], made_ref.shape[0]
         for target, first in ((keep_ref, pick_ref[0]), (send_ref, 1 - pick_ref[0])):
@@ -105,6 +108,34 @@
     )(in_hbm(array))
 
 
+def sides_body(pick_ref, source, first_ref, second_ref, sems):
+    half = first_ref.shape[1]
+    copies = []
+    for target, side in ((first_ref, pick_ref[0]), (second_ref, 1 - pick_ref[0])):
+        piece = source.at[:, pl.ds(pl.multiple_of(side * half, half), half)]
+        copies.append(pltpu.make_async_copy(piece, target, sems.at[len(copies)]))
+    for copy in copies:
+        copy.start()
+    for copy in copies:
+        copy.wait()
+
+
+def sides_of(pick, array):
+    nodes, width = array.shape
+    return pl.pallas_call(
+        sides_body,
+        grid_spec=pltpu.PrefetchScalarGridSpec(
+            num_scalar_prefetch=1,
+            grid=(),
+            in_specs=[pl.BlockSpec(memory_space=pl.ANY)],
+            out_specs=[pl.BlockSpec(memory_space=pltpu.VMEM)] * 2,
+            scratch_shapes=[pltpu.SemaphoreType.DMA((2,))],
+        ),
+        out_shape=[pltpu.VMEM((nodes, width // 2), array.dtype)] * 2,
+        compiler_params=pltpu.CompilerParams(vmem_limit_bytes=4 << 20),
+    )(pick, in_hbm(array))
+
+
 def rims_body(*refs):
     edges, (last_ref, first_ref) = refs[:-2], refs[-2:]
     rim = last_ref.shape[0]
@@ -143,7 +174,7 @@
     parts = 4 if block_rows % 4 == 0 else 1
     plan = dict(
         blk=blk, rim=rim, half=half, multiplies=multiplies, places=places, count=len(pieces),
-        parts=parts,
+        parts=parts, hands_out=hands_out,
     )
     operands = [in_hbm(mass_blocks), *pieces]
     specs = [pl.BlockSpec(memory_space=pl.ANY)] * len(operands)
@@ -153,7 +184,8 @@
         outs += [pltpu.VMEM((half, width), jnp.float32)] * 2
         flops += 4 * nodes * half * width
     rows = [pltpu.VMEM((row_count, width), jnp.bfloat16)]
-    outs, scratch = (outs + rows, []) if hands_out else (outs, rows)
+    side = [pltpu.VMEM((nodes, half), jnp.bfloat16)]
+    outs, scratch = (outs + side + rows, []) if hands_out else (outs, rows)
     return pl.pallas_call(
         functools.partial(fused_body, plan),
         grid_spec=pltpu.PrefetchScalarGridSpec(
@@ -173,24 +205,6 @@
     )(local_cols, pick, *operands)
 
 
-def products_body(pick_ref, left_a, left_b, w_ref, x_ref, keep_ref, send_ref):
-    own, half = w_ref.shape[1], x_ref.shape[1] // 2
-
-    def multiply(target, left, lo):
-        target[:, :own] = contract_nodes(left[...], w_ref[...])
-        target[:, own:] = contract_nodes(left[...], x_ref[:, lo : lo + half])
-
-    @pl.when(pick_ref[0] == 0)
-    def _():
-        multiply(keep_ref, left_a, half)
-        multiply(send_ref, left_b, 0)
-
-    @pl.when(pick_ref[0] != 0)
-    def _():
-        multiply(keep_ref, left_b, 0)
-        multiply(send_ref, left_a, half)
-
-
 def products_of_rows_body(rim, pick_ref, rows_ref, w_ref, x_ref, keep_ref, send_ref):
     own, nodes, half = w_ref.shape[1], w_ref.shape[0], x_ref.shape[1] // 2
     for target, first in ((keep_ref, pick_ref[0]), (send_ref, 1 - pick_ref[0])):
@@ -215,23 +229,6 @@
         ),
         compiler_params=pltpu.CompilerParams(vmem_limit_bytes=16 << 20),
     )(pick, *(in_vmem(array) for array in (rows, w, x)))
-
-
-def products(pick, left_a, left_b, w, x):
-    nodes, own = w.shape
-    rows, total = left_a.shape[1], own + x.shape[1] // 2
-    vmem = pl.BlockSpec(memory_space=pltpu.VMEM)
-    return pl.pallas_call(
-        products_body,
-        grid_spec=pltpu.PrefetchScalarGridSpec(
-            num_scalar_prefetch=1, grid=(), in_specs=[vmem] * 4, out_specs=[vmem] * 2
-        ),
-        out_shape=[pltpu.VMEM((rows, total), jnp.float32)] * 2,
-        cost_estimate=pl.CostEstimate(
-            flops=4 * nodes * rows * total, bytes_accessed=8 << 20, transcendentals=0
-        ),
-        compiler_params=pltpu.CompilerParams(vmem_limit_bytes=16 << 20),
-    )(pick, *(in_vmem(array) for array in (left_a, left_b, w, x)))
 
 
 TOP = 32000.0
@@ -289,6 +286,36 @@
     put_encoded(coded_ref, total)
 
 
+def chip_body(pick_ref, left, left_too, w, w_too, x, x_too, total_ref, coded_ref):
+    own, half = w.shape[1], x_too.shape[1]
+    side = x[:, pl.ds(pl.multiple_of(pick_ref[0] * half, half), half)]
+    near = contract_nodes(left[...], w[...]) + contract_nodes(left_too[...], w_too[...])
+    total_ref[:, :own] = near
+    total_ref[:, own:] = contract_nodes(left[...], side) + contract_nodes(left_too[...], x_too[...])
+    put_encoded(coded_ref, total_ref[...])
+
+
+def chip_products(pick, *operands):
+    left, _, w, _, _, x_too = operands
+    nodes, rows = left.shape
+    total = w.shape[1] + x_too.shape[1]
+    vmem = pl.BlockSpec(memory_space=pltpu.VMEM)
+    return pl.pallas_call(
+        chip_body,
+        grid_spec=pltpu.PrefetchScalarGridSpec(
+            num_scalar_prefetch=1, grid=(), in_specs=[vmem] * 6, out_specs=[vmem] * 2
+        ),
+        out_shape=[
+            pltpu.VMEM((rows, total), jnp.float32),
+            pltpu.VMEM((rows + EXTRA, total), jnp.int16),
+        ],
+        cost_estimate=pl.CostEstimate(
+            flops=4 * nodes * rows * total, bytes_accessed=8 << 20, transcendentals=0
+        ),
+        compiler_params=pltpu.CompilerParams(vmem_limit_bytes=16 << 20),
+    )(pick, *(in_vmem(operand) for operand in operands))
+
+
 def turn_body(own, flag_ref, total_ref, came_ref, near_ref, leg_ref, far_ref, coded_ref):
     width = total_ref.shape[1]
     total = total_ref[...] + decoded(came_ref, 0, width)
@@ -394,7 +421,11 @@
             for s, t in LINE[target(c, q)][1]
         ]
 
-    return across, cores, line, corner, around
+    step = lambda z, c, q: flat(z, c, q ^ (Y, X)[c])
+    devices = [(z, c, q) for z in range(chips) for c in range(2) for q in range(runs)]
+    straight = [(flat(z, c, q), step(z, c, q)) for z, c, q in devices]
+    crosswise = [(flat(z, c, q), step(z, 1 - c, q)) for z, c, q in devices]
+    return across, cores, line, corner, around, straight, crosswise
 
 
 def on_square(snapshots, block_cols, mass_blocks):
@@ -406,7 +437,7 @@
     runs = lax.axis_size("run")
     chips = lax.axis_size("mesh") // 2
     both = ("mesh", "run")
-    across, cores, line, corner, around = exchange_plan(chips, runs)
+    across, cores, line, corner, around, straight, crosswise = exchange_plan(chips, runs)
     shard = lax.axis_index("mesh")
     column = lax.axis_index("run")
     core, chip = shard % 2, shard // 2
@@ -434,9 +465,9 @@
     last_rows, first_rows = rims_of(left_edge, right_edge, a_edge, b_edge)
     low = lax.ppermute(last_rows, "mesh", [(i, i + 1) for i in range(shards - 1)])
     high = lax.ppermute(first_rows, "mesh", [(i + 1, i) for i in range(shards - 1)])
-    left, right = parts_of(snapshots, (((0, node_count), west),), (((0, node_count), east),))
-    a2 = over_x(right)
-    b1 = over_y(left)
+    mine, others = sides_of(pick, snapshots)
+    got = lax.ppermute(mine, both, straight)
+    got_too = lax.ppermute(others, both, crosswise)
 
     top = rim + node_count
     all_rows, every = (0, rim), (0, column_count)
@@ -464,13 +495,15 @@
             (edge, (rim, rim), node_count - rim),
         )
     ]
-    wx, rows = fused(
+    wx, wx_side, rows = fused(
         local_cols, pick, mass_blocks, [low, high, a_edge, a1, b_edge, b2],
         [(0, all_rows, beyond, 0, 0), (1, all_rows, beyond, top, 0), *near_rows],
         multiplies=False, hands_out=True,
     )
     keep1, send1 = products_of_rows(pick, rows, rim, w, wx)
-    keep2, send2 = products(1 - pick, a2, b1, w, wx)
+    w_too = lax.ppermute(w, "mesh", cores)
+    wx_too = lax.ppermute(wx_side, "mesh", cores)
+    total2, coded2 = chip_products(pick, got, got_too, w, w_too, wx, wx_too)
     own_target = lambda c, q: q
     came = lax.ppermute(send0, "mesh", cores)
     own, coded = merge(keep0, came)
@@ -478,10 +511,12 @@
     own, coded = merge(own, came, step_body)
     own_came = lax.ppermute(coded, both, line(own_target, 1))
 
-    def finished(kept, sent, core_a):
+    def added(kept, sent):
+        came = lax.ppermute(sent, "mesh", cores)
+        return merge(kept, came)
+
+    def finished(total, coded, core_a):
         target, bit = towards(core_a), crossing(core_a)
-        came = lax.ppermute(sent, "mesh", cores)
-        total, coded = merge(kept, came)
         came = lax.ppermute(coded, both, line(target, 0))
         at_target = (chip == target(core, column))[None].astype(jnp.int32)
         near, leg, far = turn(at_target, total, came, column_count)
@@ -489,8 +524,8 @@
         far = lax.ppermute(far, both, around(target, bit))
         return near, leg, far
 
-    stage1 = finished(keep1, send1, 0)
-    stage2 = finished(keep2, send2, 1)
+    stage1 = finished(*added(keep1, send1), 0)
+    stage2 = finished(total2, coded2, 1)
     near = jnp.where((chip == (column ^ X)) == (core == 0), 1, 2)
     case = jnp.where(chip == column, 0, jnp.where(chip == (column ^ (X | Y)), 3 + core, near))
     return close(case[None].astype(jnp.int32), own, own_came, *stage1, *stage2)

time: 111 us -> 108 us (0.973)
  waiting for transfers between devices: 34.6 us -> 27.6 us
  starting transfers between devices: 37.1 us -> 42 us
  Pallas kernels: 36.7 us -> 35.5 us
    ppermute x3 -> x2, waiting for transfers between devices: 16.9 us -> 3.84 us  [over_x(): return lax.ppermute(v, 'run', across(X))]
    ppermute x2 -> x5, waiting for transfers between devices: 0.01 us -> 6.48 us  [the longest x1 4.27 us: on_square(): got = lax.ppermute(mine, both, straight)]
    ppermute x2 -> x5, starting transfers between devices: 3.44 us -> 9.72 us  [the longest x1 4.19 us: on_square(): w_too = lax.ppermute(w, 'mesh', cores)]
    pallas_call x1 -> x2, Pallas kernels: 1.82 us -> 4.3 us  [the longest x1 2.75 us: chip_products(): pl.pallas_call(chip_body, grid_spec=pltpu.PrefetchScalarGridSpec(num_scal...]
    ppermute x2, starting transfers between devices: 6.26 us -> 8.68 us  [finished(): came = lax.ppermute(coded, both, line(target, 0))]
    ppermute x3 -> x2, starting transfers between devices: 5 us -> 3.44 us  [over_x(): return lax.ppermute(v, 'run', across(X))]
    pallas_call x3 -> x2, Pallas kernels: 5.22 us -> 3.71 us  [parts_of(): pl.pallas_call(functools.partial(parts_body, cuts), in_specs=[pl.BlockSpe...]
    pallas_call x4 -> x3, Pallas kernels: 3.7 us -> 2.73 us  [merge(): pl.pallas_call(body, in_specs=[vmem] * 2, out_specs=[vmem] * 2, out_shape...]
  transfers between devices with their start and end apart: 19 -> 20, of which waited for: 8 -> 8; matrix products, arithmetic and copies ran while one was open for 0% -> 0% of each run, Pallas kernels for 30% -> 31%
where the time goes in v5:
time: 108 us; the launch traced here: 107 us
  starting transfers between devices  42 us (39%)
  Pallas kernels  35.5 us (33%)
  waiting for transfers between devices  27.6 us (26%)
  local copies, waits for them, and re-layouts  1.76 us (2%)
    pallas_call x2, Pallas kernels, fused(): pl.pallas_call(functools.partial(fused_body, plan), grid_spec=pltpu.Prefe...  19.1 us
    ppermute x1, waiting for transfers between devices, on_square(): came = lax.ppermute(coded, both, line(own_target, 0))  12.4 us
    ppermute x2, starting transfers between devices, finished(): came = lax.ppermute(coded, both, line(target, 0))  8.68 us
    ppermute x2, starting transfers between devices, finished(): leg = lax.ppermute(leg, both, line(target, 1) + corner(target, bit))  6.83 us
    ppermute x2, starting transfers between devices, finished(): far = lax.ppermute(far, both, around(target, bit))  4.77 us
    ppermute x1, waiting for transfers between devices, on_square(): got = lax.ppermute(mine, both, straight)  4.27 us
    ppermute x1, starting transfers between devices, on_square(): w_too = lax.ppermute(w, 'mesh', cores)  4.19 us
    ppermute x2, waiting for transfers between devices, over_x(): return lax.ppermute(v, 'run', across(X))  3.84 us
  transfers between devices with their start and end apart: 20, of which 8 were waited for; matrix products, arithmetic and copies ran while one was open for 0% of the time, Pallas kernels for 31%

profile of v5, /device:TPU:0, one launch (start us, length us, event | category | flops | bytes accessed | tf_op | source)
XLA Modules:
  0.0 107.1 jit_solution(5745744821884581140)
XLA Ops:
  1.0 3.0 %collective-permute-start = (bf16[256,256]{1,0:T(8,128)(2,1)S(1)}, bf16[256,256]{1,0:T(8,128)(2,1)S(1)}, u32[]{:S(2)}, u32[]{:S(2)}) collective-permute-start(bf16[256,256]{1,0:T(8,128)(2,1)S(1)} %get-tuple-element.35.refs_0_), channel_id=1, source_target_pairs={{0,1},{1,0},{2,3},{3,2},{4,5},{5,4},{6,7},{7,6},{8,9},{9,8},{10,11... | collective-permute-start | bytes 393224 | tf_op jit(solution)/shard_map/ppermute | solution.py:447
  4.0 1.5 %collective-permute-start.1 = (bf16[256,256]{1,0:T(8,128)(2,1)S(1)}, bf16[256,256]{1,0:T(8,128)(2,1)S(1)}, u32[]{:S(2)}, u32[]{:S(2)}) collective-permute-start(bf16[256,256]{1,0:T(8,128)(2,1)S(1)} %get-tuple-element.36.refs_1_), channel_id=1, source_target_pairs={{0,2},{1,3},{2,0},{3,1},{4,6},{5,7},{6,4},{7,5},{8,10},{9,11},{10,... | collective-permute-start | bytes 393224 | tf_op jit(solution)/shard_map/ppermute | solution.py:450
  5.5 2.0 %collective-permute-done.refs_2_.refs_5_ = bf16[256,256]{1,0:T(8,128)(2,1)S(1)} collective-permute-done((bf16[256,256]{1,0:T(8,128)(2,1)S(1)}, bf16[256,256]{1,0:T(8,128)(2,1)S(1)}, u32[]{:S(2)}, u32[]{:S(2)}) %collective-permute-start) | collective-permute-done | bytes 131104 | tf_op jit(solution)/shard_map/ppermute | solution.py:447
  7.5 1.5 %collective-permute-done.1.refs_3_.refs_7_ = bf16[256,256]{1,0:T(8,128)(2,1)S(1)} collective-permute-done((bf16[256,256]{1,0:T(8,128)(2,1)S(1)}, bf16[256,256]{1,0:T(8,128)(2,1)S(1)}, u32[]{:S(2)}, u32[]{:S(2)}) %collective-permute-start.1) | collective-permute-done | bytes 131104 | tf_op jit(solution)/shard_map/ppermute | solution.py:450
  9.1 1.3 %collective-permute-start.2 = (bf16[128,1024]{1,0:T(8,128)(2,1)S(1)}, bf16[128,1024]{1,0:T(8,128)(2,1)S(1)}, u32[]{:S(2)}, u32[]{:S(2)}) collective-permute-start(bf16[128,1024]{1,0:T(8,128)(2,1)S(1)} %get-tuple-element.37), channel_id=1, source_target_pairs={{0,4},{4,8},{8,12},{12,16},{16,20},{20,24},{24,28},{1,5},{5,9},{9,... | collective-permute-start | bytes 786440 | tf_op jit(solution)/shard_map/ppermute | solution.py:466
  11.7 2.7 %shard_map.41 = (bf16[1792,256]{1,0:T(8,128)(2,1)}, bf16[1792,256]{1,0:T(8,128)(2,1)}) custom-call(bf16[2048,512]{1,0:T(8,128)(2,1)} %source.5), custom_call_target="tpu_custom_call" | custom-call | tf_op jit(solution)/shard_map/pallas_call | solution.py:101
  14.8 1.7 %collective-permute-start.8 = (bf16[1792,256]{1,0:T(8,128)(2,1)}, bf16[1792,256]{1,0:T(8,128)(2,1)}, u32[]{:S(2)}, u32[]{:S(2)}) collective-permute-start(bf16[1792,256]{1,0:T(8,128)(2,1)} %get-tuple-element.46), channel_id=1, source_target_pairs={{0,2},{1,3},{2,0},{3,1},{4,6},{5,7},{6,4},{7,5},{8,10},{9,11},{10,... | collective-permute-start | bytes 2752520 | tf_op jit(solution)/shard_map/ppermute | solution.py:450
  16.6 10.1 %shard_map.38 = (bf16[2048,512]{1,0:T(8,128)(2,1)S(1)}, f32[256,512]{1,0:T(8,128)S(1)}, f32[256,512]{1,0:T(8,128)S(1)}) custom-call(s32[32,16]{1,0:T(8,128)S(1)} %broadcast_subtract_fusion.refs_0_, s32[1]{0:T(128)} %bitcast.1.refs_1_.pick_ref, bf16[32,64,1024]{2,1,0:T(8,128)(2,1)} %refs_2_.3, bf16[128,1024]{1,0:T(8,128)(2,1)S(1)} %collective-permute-done.2.refs_3_, ...), custom_call_target="tpu_custom_call" | custom-call | flops 9663676416 | bytes 8388608 | tf_op jit(solution)/shard_map/pallas_call | solution.py:189
  26.7 4.2 %collective-permute-start.15 = (bf16[2048,512]{1,0:T(8,128)(2,1)S(1)}, bf16[2048,512]{1,0:T(8,128)(2,1)S(1)}, u32[]{:S(2)}, u32[]{:S(2)}) collective-permute-start(bf16[2048,512]{1,0:T(8,128)(2,1)S(1)} %get-tuple-element.48.w_ref.w), channel_id=1, source_target_pairs={{0,4},{4,0},{8,12},{12,8},{16,20},{20,16},{24,28},{28,24},{1,5},{5... | collective-permute-start | bytes 6291464 | tf_op jit(solution)/shard_map/ppermute | solution.py:504
  30.9 1.6 %shard_map.46 = (bf16[2048,256]{1,0:T(8,128)(2,1)S(1)}, bf16[2048,256]{1,0:T(8,128)(2,1)S(1)}) custom-call(s32[1]{0:T(128)} %bitcast.1.refs_1_.pick_ref, bf16[2048,512]{1,0:T(8,128)(2,1)} %source.5), custom_call_target="tpu_custom_call" | custom-call | tf_op jit(solution)/shard_map/pallas_call | solution.py:125
  32.5 1.6 %collective-permute-start.13 = (bf16[2048,256]{1,0:T(8,128)(2,1)S(1)}, bf16[2048,256]{1,0:T(8,128)(2,1)S(1)}, u32[]{:S(2)}, u32[]{:S(2)}) collective-permute-start(bf16[2048,256]{1,0:T(8,128)(2,1)S(1)} %get-tuple-element.57), channel_id=1, source_target_pairs={{0,2},{1,3},{2,0},{3,1},{4,5},{5,4},{6,7},{7,6},{8,10},{9,11},{10,... | collective-permute-start | bytes 3145736 | tf_op jit(solution)/shard_map/ppermute | solution.py:469
  34.1 1.9 %collective-permute-done.7.refs_6_ = bf16[1792,256]{1,0:T(8,128)(2,1)S(1)} collective-permute-done((bf16[1792,256]{1,0:T(8,128)(2,1)}, bf16[1792,256]{1,0:T(8,128)(2,1)S(1)}, u32[]{:S(2)}, u32[]{:S(2)}) %collective-permute-start.7) | collective-permute-done | bytes 917536 | tf_op jit(solution)/shard_map/ppermute | solution.py:447
  36.5 9.0 %shard_map.42 = (bf16[2048,512]{1,0:T(8,128)(2,1)S(1)}, bf16[2048,256]{1,0:T(8,128)(2,1)S(1)}, bf16[2304,512]{1,0:T(8,128)(2,1)S(1)}) custom-call(s32[32,16]{1,0:T(8,128)S(1)} %broadcast_subtract_fusion.refs_0_, s32[1]{0:T(128)} %bitcast.1.refs_1_.pick_ref, bf16[32,64,1024]{2,1,0:T(8,128)(2,1)} %refs_2_.3, ...), custom_call_target="tpu_custom_call" | custom-call | flops 8589934592 | bytes 8388608 | tf_op jit(solution)/shard_map/pallas_call | solution.py:189
  45.5 3.8 %collective-permute-start.16 = (bf16[2048,256]{1,0:T(8,128)(2,1)S(1)}, bf16[2048,256]{1,0:T(8,128)(2,1)S(1)}, u32[]{:S(2)}, u32[]{:S(2)}) collective-permute-start(bf16[2048,256]{1,0:T(8,128)(2,1)S(1)} %get-tuple-element.59), channel_id=1, source_target_pairs={{0,4},{4,0},{8,12},{12,8},{16,20},{20,16},{24,28},{28,24},{1,5},{5... | collective-permute-start | bytes 3145736 | tf_op jit(solution)/shard_map/ppermute | solution.py:505
  49.3 1.8 %shard_map.43 = (f32[256,768]{1,0:T(8,128)S(1)}, f32[256,768]{1,0:T(8,128)S(1)}) custom-call(s32[1]{0:T(128)} %bitcast.1.refs_1_.pick_ref, bf16[2304,512]{1,0:T(8,128)(2,1)S(1)} %get-tuple-element.47.rows_ref, bf16[2048,512]{1,0:T(8,128)(2,1)S(1)} %get-tuple-element.48.w_ref.w, bf16[2048,512]{1,0:T(8,128)(2,1)S(1)} %get-tuple-element.49.x_ref.x), custom_call_target="tpu_custom_call" | custom-call | flops 1610612736 | bytes 8388608 | tf_op jit(solution)/shard_map/pallas_call | solution.py:221
  51.3 2.2 %collective-permute-done.9.came_ref = f32[256,768]{1,0:T(8,128)S(1)} collective-permute-done((f32[256,768]{1,0:T(8,128)S(1)}, f32[256,768]{1,0:T(8,128)S(1)}, u32[]{:S(2)}, u32[]{:S(2)}) %collective-permute-start.9) | collective-permute-done | bytes 786464 | tf_op jit(solution)/shard_map/ppermute | solution.py:515
  54.6 4.3 %collective-permute-done.13.left = bf16[2048,256]{1,0:T(8,128)(2,1)S(1)} collective-permute-done((bf16[2048,256]{1,0:T(8,128)(2,1)S(1)}, bf16[2048,256]{1,0:T(8,128)(2,1)S(1)}, u32[]{:S(2)}, u32[]{:S(2)}) %collective-permute-start.13) | collective-permute-done | bytes 1048608 | tf_op jit(solution)/shard_map/ppermute | solution.py:469
  58.9 7.4 %collective-permute-start.10 = (s16[272,768]{1,0:T(8,128)(2,1)}, s16[272,768]{1,0:T(8,128)(2,1)S(1)}, u32[]{:S(2)}, u32[]{:S(2)}) collective-permute-start(s16[272,768]{1,0:T(8,128)(2,1)} %get-tuple-element.53), channel_id=1, source_target_pairs={{0,8},{16,24},{9,1},{25,17},{18,26},{2,10},{27,19},{11,3},{28,20},... | collective-permute-start | bytes 1253384 | tf_op jit(solution)/shard_map/ppermute | solution.py:520
  66.3 2.7 %shard_map.47 = (f32[256,768]{1,0:T(8,128)S(1)}, s16[272,768]{1,0:T(8,128)(2,1)}) custom-call(s32[1]{0:T(128)} %bitcast.1.refs_1_.pick_ref, bf16[2048,256]{1,0:T(8,128)(2,1)S(1)} %collective-permute-done.13.left, bf16[2048,256]{1,0:T(8,128)(2,1)S(1)} %collective-permute-done.14.left_too, bf16[2048,512]{1,0:T(8,128)(2,1)S(1)} %get-tuple-element.48.w_ref.w, ...), custom_call_target="tpu_custom_call" | custom-call | flops 1610612736 | bytes 8388608 | tf_op jit(solution)/shard_map/pallas_call | solution.py:303
  72.5 12.4 %collective-permute-done.5.came_ref = s16[272,512]{1,0:T(8,128)(2,1)S(1)} collective-permute-done((s16[272,512]{1,0:T(8,128)(2,1)}, s16[272,512]{1,0:T(8,128)(2,1)S(1)}, u32[]{:S(2)}, u32[]{:S(2)}) %collective-permute-start.5) | collective-permute-done | bytes 278560 | tf_op jit(solution)/shard_map/ppermute | solution.py:510
  91.5 6.2 %collective-permute-start.18 = (s16[272,512]{1,0:T(8,128)(2,1)}, s16[272,512]{1,0:T(8,128)(2,1)S(1)}, u32[]{:S(2)}, u32[]{:S(2)}) collective-permute-start(s16[272,512]{1,0:T(8,128)(2,1)} %get-tuple-element.63), channel_id=1, source_target_pairs={{0,16},{9,25},{18,2},{27,11},{28,12},{21,5},{14,30},{7,23},{16,17}... | collective-permute-start | bytes 835592 | tf_op jit(solution)/shard_map/ppermute | solution.py:523
  98.3 4.1 %collective-permute-start.19 = (s16[272,256]{1,0:T(8,128)(2,1)S(1)}, s16[272,256]{1,0:T(8,128)(2,1)S(1)}, u32[]{:S(2)}, u32[]{:S(2)}) collective-permute-start(s16[272,256]{1,0:T(8,128)(2,1)S(1)} %get-tuple-element.64), channel_id=1, source_target_pairs={{0,17},{9,24},{18,3},{27,10},{28,14},{21,7},{14,28},{7,21}} | collective-permute-start | bytes 417800 | tf_op jit(solution)/shard_map/ppermute | solution.py:524
  102.4 2.8 %collective-permute-done.6.own_came = s16[272,512]{1,0:T(8,128)(2,1)} collective-permute-done((s16[272,512]{1,0:T(8,128)(2,1)}, s16[272,512]{1,0:T(8,128)(2,1)}, u32[]{:S(2)}, u32[]{:S(2)}) %collective-permute-start.6) | collective-permute-done | bytes 278560 | tf_op jit(solution)/shard_map/ppermute | solution.py:512
  105.3 1.8 %close.1 = f32[256,512]{1,0:T(8,128)} custom-call(s32[1]{0:T(128)} %bitcast.case_ref, f32[256,512]{1,0:T(8,128)S(1)} %get-tuple-element.43.own, s16[272,512]{1,0:T(8,128)(2,1)} %collective-permute-done.6.own_came, f32[256,512]{1,0:T(8,128)S(1)} %get-tuple-element.54.near1, s16[272,512]{1,0:T(8,128)(2,1)S(1)} %collective-permute-done.11.leg1, ...), custom_call_target="tpu_custom_call" | custom-call | tf_op jit(solution)/shard_map/close/pallas_call | solution.py:377
  (38 shorter events, 15.2 us)
Async XLA Ops:
  0.0 16.5 %copy-start.2 = (s32[32,16]{0,1:T(8,128)S(1)}, s32[32,16]{0,1:T(8,128)}, u32[]{:S(2)}) copy-start(s32[32,16]{0,1:T(8,128)} %param.4) | copy-start | bytes 6148
  1.0 6.5 %collective-permute-start = (bf16[256,256]{1,0:T(8,128)(2,1)S(1)}, bf16[256,256]{1,0:T(8,128)(2,1)S(1)}, u32[]{:S(2)}, u32[]{:S(2)}) collective-permute-start(bf16[256,256]{1,0:T(8,128)(2,1)S(1)} %get-tuple-element.35.refs_0_), channel_id=1, source_target_pairs={{0,1},{1,0},{2,3},{3,2},{4,5},{5,4},{6,7},{7,6},{8,9},{9,8},{10,11... | collective-permute-start | bytes 393224 | tf_op jit(solution)/shard_map/ppermute | solution.py:447
  4.0 5.0 %collective-permute-start.1 = (bf16[256,256]{1,0:T(8,128)(2,1)S(1)}, bf16[256,256]{1,0:T(8,128)(2,1)S(1)}, u32[]{:S(2)}, u32[]{:S(2)}) collective-permute-start(bf16[256,256]{1,0:T(8,128)(2,1)S(1)} %get-tuple-element.36.refs_1_), channel_id=1, source_target_pairs={{0,2},{1,3},{2,0},{3,1},{4,6},{5,7},{6,4},{7,5},{8,10},{9,11},{10,... | collective-permute-start | bytes 393224 | tf_op jit(solution)/shard_map/ppermute | solution.py:450
  9.1 7.6 %collective-permute-start.2 = (bf16[128,1024]{1,0:T(8,128)(2,1)S(1)}, bf16[128,1024]{1,0:T(8,128)(2,1)S(1)}, u32[]{:S(2)}, u32[]{:S(2)}) collective-permute-start(bf16[128,1024]{1,0:T(8,128)(2,1)S(1)} %get-tuple-element.37), channel_id=1, source_target_pairs={{0,4},{4,8},{8,12},{12,16},{16,20},{20,24},{24,28},{1,5},{5,9},{9,... | collective-permute-start | bytes 786440 | tf_op jit(solution)/shard_map/ppermute | solution.py:466
  10.4 6.2 %collective-permute-start.3 = (bf16[128,1024]{1,0:T(8,128)(2,1)S(1)}, bf16[128,1024]{1,0:T(8,128)(2,1)S(1)}, u32[]{:S(2)}, u32[]{:S(2)}) collective-permute-start(bf16[128,1024]{1,0:T(8,128)(2,1)S(1)} %get-tuple-element.38), channel_id=1, source_target_pairs={{4,0},{8,4},{12,8},{16,12},{20,16},{24,20},{28,24},{5,1},{9,5},{13... | collective-permute-start | bytes 786440 | tf_op jit(solution)/shard_map/ppermute | solution.py:467
  14.4 21.5 %collective-permute-start.7 = (bf16[1792,256]{1,0:T(8,128)(2,1)}, bf16[1792,256]{1,0:T(8,128)(2,1)S(1)}, u32[]{:S(2)}, u32[]{:S(2)}) collective-permute-start(bf16[1792,256]{1,0:T(8,128)(2,1)} %get-tuple-element.45), channel_id=1, source_target_pairs={{0,1},{1,0},{2,3},{3,2},{4,5},{5,4},{6,7},{7,6},{8,9},{9,8},{10,11... | collective-permute-start | bytes 2752520 | tf_op jit(solution)/shard_map/ppermute | solution.py:447
  14.8 21.7 %collective-permute-start.8 = (bf16[1792,256]{1,0:T(8,128)(2,1)}, bf16[1792,256]{1,0:T(8,128)(2,1)}, u32[]{:S(2)}, u32[]{:S(2)}) collective-permute-start(bf16[1792,256]{1,0:T(8,128)(2,1)} %get-tuple-element.46), channel_id=1, source_target_pairs={{0,2},{1,3},{2,0},{3,1},{4,6},{5,7},{6,4},{7,5},{8,10},{9,11},{10,... | collective-permute-start | bytes 2752520 | tf_op jit(solution)/shard_map/ppermute | solution.py:450
  26.7 39.6 %collective-permute-start.15 = (bf16[2048,512]{1,0:T(8,128)(2,1)S(1)}, bf16[2048,512]{1,0:T(8,128)(2,1)S(1)}, u32[]{:S(2)}, u32[]{:S(2)}) collective-permute-start(bf16[2048,512]{1,0:T(8,128)(2,1)S(1)} %get-tuple-element.48.w_ref.w), channel_id=1, source_target_pairs={{0,4},{4,0},{8,12},{12,8},{16,20},{20,16},{24,28},{28,24},{1,5},{5... | collective-permute-start | bytes 6291464 | tf_op jit(solution)/shard_map/ppermute | solution.py:504
  32.5 26.4 %collective-permute-start.13 = (bf16[2048,256]{1,0:T(8,128)(2,1)S(1)}, bf16[2048,256]{1,0:T(8,128)(2,1)S(1)}, u32[]{:S(2)}, u32[]{:S(2)}) collective-permute-start(bf16[2048,256]{1,0:T(8,128)(2,1)S(1)} %get-tuple-element.57), channel_id=1, source_target_pairs={{0,2},{1,3},{2,0},{3,1},{4,5},{5,4},{6,7},{7,6},{8,10},{9,11},{10,... | collective-permute-start | bytes 3145736 | tf_op jit(solution)/shard_map/ppermute | solution.py:469
  34.1 32.2 %collective-permute-start.14 = (bf16[2048,256]{1,0:T(8,128)(2,1)S(1)}, bf16[2048,256]{1,0:T(8,128)(2,1)S(1)}, u32[]{:S(2)}, u32[]{:S(2)}) collective-permute-start(bf16[2048,256]{1,0:T(8,128)(2,1)S(1)} %get-tuple-element.58), channel_id=1, source_target_pairs={{0,5},{1,4},{2,7},{3,6},{4,2},{5,3},{6,0},{7,1},{8,13},{9,12},{10,... | collective-permute-start | bytes 3145736 | tf_op jit(solution)/shard_map/ppermute | solution.py:470
  45.5 20.8 %collective-permute-start.16 = (bf16[2048,256]{1,0:T(8,128)(2,1)S(1)}, bf16[2048,256]{1,0:T(8,128)(2,1)S(1)}, u32[]{:S(2)}, u32[]{:S(2)}) collective-permute-start(bf16[2048,256]{1,0:T(8,128)(2,1)S(1)} %get-tuple-element.59), channel_id=1, source_target_pairs={{0,4},{4,0},{8,12},{12,8},{16,20},{20,16},{24,28},{28,24},{1,5},{5... | collective-permute-start | bytes 3145736 | tf_op jit(solution)/shard_map/ppermute | solution.py:505
  51.1 2.4 %collective-permute-start.9 = (f32[256,768]{1,0:T(8,128)S(1)}, f32[256,768]{1,0:T(8,128)S(1)}, u32[]{:S(2)}, u32[]{:S(2)}) collective-permute-start(f32[256,768]{1,0:T(8,128)S(1)} %get-tuple-element.51), channel_id=1, source_target_pairs={{0,4},{4,0},{8,12},{12,8},{16,20},{20,16},{24,28},{28,24},{1,5},{5... | collective-permute-start | bytes 2359304 | tf_op jit(solution)/shard_map/ppermute | solution.py:515
  53.5 16.8 %collective-permute-start.4 = (f32[256,512]{1,0:T(8,128)S(1)}, f32[256,512]{1,0:T(8,128)S(1)}, u32[]{:S(2)}, u32[]{:S(2)}) collective-permute-start(f32[256,512]{1,0:T(8,128)S(1)} %get-tuple-element.40), channel_id=1, source_target_pairs={{0,4},{4,0},{8,12},{12,8},{16,20},{20,16},{24,28},{28,24},{1,5},{5... | collective-permute-start | bytes 1572872 | tf_op jit(solution)/shard_map/ppermute | solution.py:508
  58.9 29.9 %collective-permute-start.10 = (s16[272,768]{1,0:T(8,128)(2,1)}, s16[272,768]{1,0:T(8,128)(2,1)S(1)}, u32[]{:S(2)}, u32[]{:S(2)}) collective-permute-start(s16[272,768]{1,0:T(8,128)(2,1)} %get-tuple-element.53), channel_id=1, source_target_pairs={{0,8},{16,24},{9,1},{25,17},{18,26},{2,10},{27,19},{11,3},{28,20},... | collective-permute-start | bytes 1253384 | tf_op jit(solution)/shard_map/ppermute | solution.py:520
  69.0 21.4 %collective-permute-start.17 = (s16[272,768]{1,0:T(8,128)(2,1)}, s16[272,768]{1,0:T(8,128)(2,1)S(1)}, u32[]{:S(2)}, u32[]{:S(2)}) collective-permute-start(s16[272,768]{1,0:T(8,128)(2,1)} %get-tuple-element.61), channel_id=1, source_target_pairs={{24,16},{8,0},{17,25},{1,9},{10,2},{26,18},{3,11},{19,27},{4,12},{... | collective-permute-start | bytes 1253384 | tf_op jit(solution)/shard_map/ppermute | solution.py:520
  71.2 13.7 %collective-permute-start.5 = (s16[272,512]{1,0:T(8,128)(2,1)}, s16[272,512]{1,0:T(8,128)(2,1)S(1)}, u32[]{:S(2)}, u32[]{:S(2)}) collective-permute-start(s16[272,512]{1,0:T(8,128)(2,1)} %get-tuple-element.42), channel_id=1, source_target_pairs={{8,0},{24,16},{1,9},{17,25},{26,18},{10,2},{19,27},{3,11},{12,4},{... | collective-permute-start | bytes 835592 | tf_op jit(solution)/shard_map/ppermute | solution.py:510
  84.9 0.7 copy-start
  85.7 1.0 copy-start.1
  87.5 17.7 %collective-permute-start.6 = (s16[272,512]{1,0:T(8,128)(2,1)}, s16[272,512]{1,0:T(8,128)(2,1)}, u32[]{:S(2)}, u32[]{:S(2)}) collective-permute-start(s16[272,512]{1,0:T(8,128)(2,1)} %get-tuple-element.44), channel_id=1, source_target_pairs={{16,0},{25,9},{2,18},{11,27},{20,4},{29,13},{6,22},{15,31}} | collective-permute-start | bytes 835592 | tf_op jit(solution)/shard_map/ppermute | solution.py:512
  89.8 15.5 %collective-permute-start.11 = (s16[272,512]{1,0:T(8,128)(2,1)}, s16[272,512]{1,0:T(8,128)(2,1)S(1)}, u32[]{:S(2)}, u32[]{:S(2)}) collective-permute-start(s16[272,512]{1,0:T(8,128)(2,1)} %get-tuple-element.55), channel_id=1, source_target_pairs={{24,8},{17,1},{10,26},{3,19},{4,20},{13,29},{22,6},{31,15},{8,10},... | collective-permute-start | bytes 835592 | tf_op jit(solution)/shard_map/ppermute | solution.py:523
  91.5 13.8 %collective-permute-start.18 = (s16[272,512]{1,0:T(8,128)(2,1)}, s16[272,512]{1,0:T(8,128)(2,1)S(1)}, u32[]{:S(2)}, u32[]{:S(2)}) collective-permute-start(s16[272,512]{1,0:T(8,128)(2,1)} %get-tuple-element.63), channel_id=1, source_target_pairs={{0,16},{9,25},{18,2},{27,11},{28,12},{21,5},{14,30},{7,23},{16,17}... | collective-permute-start | bytes 835592 | tf_op jit(solution)/shard_map/ppermute | solution.py:523
  97.6 7.6 %collective-permute-start.12 = (s16[272,256]{1,0:T(8,128)(2,1)}, s16[272,256]{1,0:T(8,128)(2,1)S(1)}, u32[]{:S(2)}, u32[]{:S(2)}) collective-permute-start(s16[272,256]{1,0:T(8,128)(2,1)} %get-tuple-element.56), channel_id=1, source_target_pairs={{24,10},{17,3},{10,24},{3,17},{4,21},{13,28},{22,7},{31,14}} | collective-permute-start | bytes 417800 | tf_op jit(solution)/shard_map/ppermute | solution.py:524
  98.3 7.0 %collective-permute-start.19 = (s16[272,256]{1,0:T(8,128)(2,1)S(1)}, s16[272,256]{1,0:T(8,128)(2,1)S(1)}, u32[]{:S(2)}, u32[]{:S(2)}) collective-permute-start(s16[272,256]{1,0:T(8,128)(2,1)S(1)} %get-tuple-element.64), channel_id=1, source_target_pairs={{0,17},{9,24},{18,3},{27,10},{28,14},{21,7},{14,28},{7,21}} | collective-permute-start | bytes 417800 | tf_op jit(solution)/shard_map/ppermute | solution.py:524

commit v6 on v5

--- a/solution.py
+++ b/solution.py
@@ -36,8 +36,14 @@
 
     used = iter(range(64))
     fetch = lambda source, target: pltpu.make_async_copy(source, target, sems.at[next(used)])
+
+    def place(to, size):
+        if isinstance(to, int):
+            return span(to, size)
+        return pl.ds(pl.multiple_of(to[0] + pick_ref[0] * (to[1] - to[0]), size), size)
+
     rows_in = [
-        fetch(pieces[p].at[span(r, n), span(c, w)], rows_ref.at[span(to, n), span(lane, w)])
+        fetch(pieces[p].at[span(r, n), span(c, w)], rows_ref.at[place(to, n), span(lane, w)])
         for p, (r, n), (c, w), to, lane in plan["places"]
     ]
     mass_in, parts = [], plan["parts"]
@@ -55,8 +61,8 @@
             mass_in[row // size].wait()
         picked = jnp.concatenate(
             [
-                rows_ref[pl.ds(pl.multiple_of(cols_ref[row, k] * blk, blk), blk), :]
-                for k in range(cols_ref.shape[1])
+                rows_ref[pl.ds(pl.multiple_of(cols_ref[k, row] * blk, blk), blk), :]
+                for k in range(cols_ref.shape[0])
             ],
             axis=0,
         )
@@ -136,28 +142,27 @@
     )(pick, in_hbm(array))
 
 
-def rims_body(*refs):
-    edges, (last_ref, first_ref) = refs[:-2], refs[-2:]
-    rim = last_ref.shape[0]
-    lane = 0
-    for edge in edges:
-        place = span(lane, edge.shape[1])
-        first_ref[:, place] = edge[:rim, :]
-        last_ref[:, place] = edge[rim:, :]
-        lane += edge.shape[1]
-
-
-def rims_of(*edges):
+def rims_body(pick_ref, *refs):
+    edges, targets = refs[:-2], refs[-2:]
+    rim = targets[0].shape[0]
+    for target, side in zip(targets, (1 - pick_ref[0], pick_ref[0])):
+        rows = pl.ds(pl.multiple_of(side * rim, rim), rim)
+        for i, edge in enumerate(edges):
+            target[:, span(i * edge.shape[1], edge.shape[1])] = edge[rows, :]
+
+
+def rims_of(pick, *edges):
     vmem = pl.BlockSpec(memory_space=pltpu.VMEM)
     shape = (edges[0].shape[0] // 2, sum(edge.shape[1] for edge in edges))
     return pl.pallas_call(
         rims_body,
-        in_specs=[vmem] * len(edges),
-        out_specs=[vmem] * 2,
+        grid_spec=pltpu.PrefetchScalarGridSpec(
+            num_scalar_prefetch=1, grid=(), in_specs=[vmem] * len(edges), out_specs=[vmem] * 2
+        ),
         out_shape=[pltpu.VMEM(shape, edges[0].dtype)] * 2,
         compiler_params=pltpu.CompilerParams(vmem_limit_bytes=4 << 20),
         name="rims",
-    )(*(in_vmem(edge) for edge in edges))
+    )(pick, *(in_vmem(edge) for edge in edges))
 
 
 def in_vmem(array):
@@ -170,7 +175,7 @@
     nodes = block_rows * blk
     width = max(lane + w for _, _, (_, w), _, lane in places)
     half = width // 2
-    row_count = max(to + n for _, (_, n), _, to, _ in places)
+    row_count = max(n + (to if isinstance(to, int) else max(to)) for _, (_, n), _, to, _ in places)
     parts = 4 if block_rows % 4 == 0 else 1
     plan = dict(
         blk=blk, rim=rim, half=half, multiplies=multiplies, places=places, count=len(pieces),
@@ -202,7 +207,7 @@
         out_shape=outs,
         cost_estimate=pl.CostEstimate(flops=flops, bytes_accessed=8 << 20, transcendentals=0),
         compiler_params=pltpu.CompilerParams(vmem_limit_bytes=24 << 20),
-    )(local_cols, pick, *operands)
+    )(local_cols.T, pick, *operands)
 
 
 def products_of_rows_body(rim, pick_ref, rows_ref, w_ref, x_ref, keep_ref, send_ref):
@@ -450,7 +455,7 @@
         return lax.ppermute(v, "run", across(Y))
 
     pick = core[None].astype(jnp.int32)
-    shards = 2 * chips
+    facing = [(m, m + (1 if m % 2 else -1)) for m in range(1, 2 * chips - 1)]
     west, east = (0, half), (half, half)
     middle = (rim, node_count - 2 * rim)
     ends = (0, rim), (node_count - rim, rim)
@@ -462,9 +467,9 @@
     left_middle, right_middle = parts_of(snapshots, ((middle, west),), ((middle, east),))
     a1 = over_x(left_middle)
     b2 = over_y(right_middle)
-    last_rows, first_rows = rims_of(left_edge, right_edge, a_edge, b_edge)
-    low = lax.ppermute(last_rows, "mesh", [(i, i + 1) for i in range(shards - 1)])
-    high = lax.ppermute(first_rows, "mesh", [(i + 1, i) for i in range(shards - 1)])
+    inner_rows, outer_rows = rims_of(pick, left_edge, right_edge, a_edge, b_edge)
+    outer = lax.ppermute(outer_rows, "mesh", facing)
+    inner = lax.ppermute(inner_rows, "mesh", cores)
     mine, others = sides_of(pick, snapshots)
     got = lax.ppermute(mine, both, straight)
     got_too = lax.ppermute(others, both, crosswise)
@@ -479,10 +484,10 @@
         return lambda c: (Y, X)[c != core_a]
 
     w, keep0, send0 = fused(
-        local_cols, pick, mass_blocks, [low, in_hbm(snapshots), high],
+        local_cols, pick, mass_blocks, [inner, in_hbm(snapshots), outer],
         [
-            (0, all_rows, every, 0, 0), (1, (0, node_count), every, rim, 0),
-            (2, all_rows, every, top, 0),
+            (0, all_rows, every, (top, 0), 0), (1, (0, node_count), every, rim, 0),
+            (2, all_rows, every, (0, top), 0),
         ],
     )
     beyond = (column_count, column_count)
@@ -496,8 +501,8 @@
         )
     ]
     wx, wx_side, rows = fused(
-        local_cols, pick, mass_blocks, [low, high, a_edge, a1, b_edge, b2],
-        [(0, all_rows, beyond, 0, 0), (1, all_rows, beyond, top, 0), *near_rows],
+        local_cols, pick, mass_blocks, [inner, outer, a_edge, a1, b_edge, b2],
+        [(0, all_rows, beyond, (top, 0), 0), (1, all_rows, beyond, (0, top), 0), *near_rows],
         multiplies=False, hands_out=True,
     )
     keep1, send1 = products_of_rows(pick, rows, rim, w, wx)

time: 108 us -> 107 us (level)
  starting transfers between devices: 42 us -> 39.6 us
  waiting for transfers between devices: 27.6 us -> 29.2 us
    ppermute x2, starting transfers between devices: 2.6 us -> 0.75 us  [the longest x1 0.68 us: on_square(): outer = lax.ppermute(outer_rows, 'mesh', facing)]
    ppermute x2, waiting for transfers between devices: 3.84 us -> 5.17 us  [over_x(): return lax.ppermute(v, 'run', across(X))]
    ppermute x1, starting transfers between devices: 4.19 us -> 3.07 us  [on_square(): w_too = lax.ppermute(w, 'mesh', cores)]
where the time goes in v6:
time: 107 us; the launch traced here: 106 us
  starting transfers between devices  39.6 us (37%)
  Pallas kernels  35.3 us (33%)
  waiting for transfers between devices  29.2 us (27%)
  local copies, waits for them, and re-layouts  1.69 us (2%)
    pallas_call x2, Pallas kernels, fused(): pl.pallas_call(functools.partial(fused_body, plan), grid_spec=pltpu.Prefe...  18.9 us
    ppermute x1, waiting for transfers between devices, on_square(): came = lax.ppermute(coded, both, line(own_target, 0))  12.6 us
    ppermute x2, starting transfers between devices, finished(): came = lax.ppermute(coded, both, line(target, 0))  8.5 us
    ppermute x2, starting transfers between devices, finished(): leg = lax.ppermute(leg, both, line(target, 1) + corner(target, bit))  6.83 us
    ppermute x2, starting transfers between devices, finished(): far = lax.ppermute(far, both, around(target, bit))  5.59 us
    ppermute x2, waiting for transfers between devices, over_x(): return lax.ppermute(v, 'run', across(X))  5.17 us
    ppermute x1, waiting for transfers between devices, on_square(): got = lax.ppermute(mine, both, straight)  4.39 us
    ppermute x1, starting transfers between devices, on_square(): wx_too = lax.ppermute(wx_side, 'mesh', cores)  3.8 us
  transfers between devices with their start and end apart: 20, of which 8 were waited for; matrix products, arithmetic and copies ran while one was open for 0% of the time, Pallas kernels for 31%

profile of v6, /device:TPU:0, one launch (start us, length us, event | category | flops | bytes accessed | tf_op | source)
XLA Modules:
  0.0 106.1 jit_solution(7205274547315085537)
XLA Ops:
  1.0 3.0 %collective-permute-start = (bf16[256,256]{1,0:T(8,128)(2,1)S(1)}, bf16[256,256]{1,0:T(8,128)(2,1)S(1)}, u32[]{:S(2)}, u32[]{:S(2)}) collective-permute-start(bf16[256,256]{1,0:T(8,128)(2,1)S(1)} %get-tuple-element.35.refs_0_), channel_id=1, source_target_pairs={{0,1},{1,0},{2,3},{3,2},{4,5},{5,4},{6,7},{7,6},{8,9},{9,8},{10,11... | collective-permute-start | bytes 393224 | tf_op jit(solution)/shard_map/ppermute | solution.py:452
  4.0 1.5 %collective-permute-start.1 = (bf16[256,256]{1,0:T(8,128)(2,1)S(1)}, bf16[256,256]{1,0:T(8,128)(2,1)S(1)}, u32[]{:S(2)}, u32[]{:S(2)}) collective-permute-start(bf16[256,256]{1,0:T(8,128)(2,1)S(1)} %get-tuple-element.36.refs_1_), channel_id=1, source_target_pairs={{0,2},{1,3},{2,0},{3,1},{4,6},{5,7},{6,4},{7,5},{8,10},{9,11},{10,... | collective-permute-start | bytes 393224 | tf_op jit(solution)/shard_map/ppermute | solution.py:455
  5.5 2.0 %collective-permute-done.refs_2_.refs_5_ = bf16[256,256]{1,0:T(8,128)(2,1)S(1)} collective-permute-done((bf16[256,256]{1,0:T(8,128)(2,1)S(1)}, bf16[256,256]{1,0:T(8,128)(2,1)S(1)}, u32[]{:S(2)}, u32[]{:S(2)}) %collective-permute-start) | collective-permute-done | bytes 131104 | tf_op jit(solution)/shard_map/ppermute | solution.py:452
  7.5 1.5 %collective-permute-done.1.refs_3_.refs_7_ = bf16[256,256]{1,0:T(8,128)(2,1)S(1)} collective-permute-done((bf16[256,256]{1,0:T(8,128)(2,1)S(1)}, bf16[256,256]{1,0:T(8,128)(2,1)S(1)}, u32[]{:S(2)}, u32[]{:S(2)}) %collective-permute-start.1) | collective-permute-done | bytes 131104 | tf_op jit(solution)/shard_map/ppermute | solution.py:455
  9.8 2.7 %shard_map.41 = (bf16[1792,256]{1,0:T(8,128)(2,1)}, bf16[1792,256]{1,0:T(8,128)(2,1)}) custom-call(bf16[2048,512]{1,0:T(8,128)(2,1)} %source.5), custom_call_target="tpu_custom_call" | custom-call | tf_op jit(solution)/shard_map/pallas_call | solution.py:107
  13.0 1.7 %collective-permute-start.8 = (bf16[1792,256]{1,0:T(8,128)(2,1)}, bf16[1792,256]{1,0:T(8,128)(2,1)}, u32[]{:S(2)}, u32[]{:S(2)}) collective-permute-start(bf16[1792,256]{1,0:T(8,128)(2,1)} %get-tuple-element.46), channel_id=1, source_target_pairs={{0,2},{1,3},{2,0},{3,1},{4,6},{5,7},{6,4},{7,5},{8,10},{9,11},{10,... | collective-permute-start | bytes 2752520 | tf_op jit(solution)/shard_map/ppermute | solution.py:455
  14.7 10.0 %shard_map.38 = (bf16[2048,512]{1,0:T(8,128)(2,1)S(1)}, f32[256,512]{1,0:T(8,128)S(1)}, f32[256,512]{1,0:T(8,128)S(1)}) custom-call(s32[16,32]{1,0:T(8,128)S(1)} %subtract_bitcast_fusion.refs_0_, s32[1]{0:T(128)} %bitcast.2.pick_ref.refs_1_, bf16[32,64,1024]{2,1,0:T(8,128)(2,1)} %refs_2_.3, bf16[128,1024]{1,0:T(8,128)(2,1)S(1)} %collective-permute-done.2.refs_3_, ...), custom_call_target="tpu_custom_call" | custom-call | flops 9663676416 | bytes 8388608 | tf_op jit(solution)/shard_map/pallas_call | solution.py:194
  24.7 3.1 %collective-permute-start.15 = (bf16[2048,512]{1,0:T(8,128)(2,1)S(1)}, bf16[2048,512]{1,0:T(8,128)(2,1)S(1)}, u32[]{:S(2)}, u32[]{:S(2)}) collective-permute-start(bf16[2048,512]{1,0:T(8,128)(2,1)S(1)} %get-tuple-element.48.w_ref.w), channel_id=1, source_target_pairs={{0,4},{4,0},{8,12},{12,8},{16,20},{20,16},{24,28},{28,24},{1,5},{5... | collective-permute-start | bytes 6291464 | tf_op jit(solution)/shard_map/ppermute | solution.py:509
  27.8 1.6 %shard_map.46 = (bf16[2048,256]{1,0:T(8,128)(2,1)S(1)}, bf16[2048,256]{1,0:T(8,128)(2,1)S(1)}) custom-call(s32[1]{0:T(128)} %bitcast.2.pick_ref.refs_1_, bf16[2048,512]{1,0:T(8,128)(2,1)} %source.5), custom_call_target="tpu_custom_call" | custom-call | tf_op jit(solution)/shard_map/pallas_call | solution.py:131
  29.3 1.6 %collective-permute-start.13 = (bf16[2048,256]{1,0:T(8,128)(2,1)S(1)}, bf16[2048,256]{1,0:T(8,128)(2,1)S(1)}, u32[]{:S(2)}, u32[]{:S(2)}) collective-permute-start(bf16[2048,256]{1,0:T(8,128)(2,1)S(1)} %get-tuple-element.57), channel_id=1, source_target_pairs={{0,2},{1,3},{2,0},{3,1},{4,5},{5,4},{6,7},{7,6},{8,10},{9,11},{10,... | collective-permute-start | bytes 3145736 | tf_op jit(solution)/shard_map/ppermute | solution.py:474
  30.9 3.2 %collective-permute-done.7.refs_6_ = bf16[1792,256]{1,0:T(8,128)(2,1)S(1)} collective-permute-done((bf16[1792,256]{1,0:T(8,128)(2,1)}, bf16[1792,256]{1,0:T(8,128)(2,1)S(1)}, u32[]{:S(2)}, u32[]{:S(2)}) %collective-permute-start.7) | collective-permute-done | bytes 917536 | tf_op jit(solution)/shard_map/ppermute | solution.py:452
  34.6 8.9 %shard_map.42 = (bf16[2048,512]{1,0:T(8,128)(2,1)S(1)}, bf16[2048,256]{1,0:T(8,128)(2,1)S(1)}, bf16[2304,512]{1,0:T(8,128)(2,1)S(1)}) custom-call(s32[16,32]{1,0:T(8,128)S(1)} %subtract_bitcast_fusion.refs_0_, s32[1]{0:T(128)} %bitcast.2.pick_ref.refs_1_, bf16[32,64,1024]{2,1,0:T(8,128)(2,1)} %refs_2_.3, ...), custom_call_target="tpu_custom_call" | custom-call | flops 8589934592 | bytes 8388608 | tf_op jit(solution)/shard_map/pallas_call | solution.py:194
  43.5 3.8 %collective-permute-start.16 = (bf16[2048,256]{1,0:T(8,128)(2,1)S(1)}, bf16[2048,256]{1,0:T(8,128)(2,1)S(1)}, u32[]{:S(2)}, u32[]{:S(2)}) collective-permute-start(bf16[2048,256]{1,0:T(8,128)(2,1)S(1)} %get-tuple-element.59), channel_id=1, source_target_pairs={{0,4},{4,0},{8,12},{12,8},{16,20},{20,16},{24,28},{28,24},{1,5},{5... | collective-permute-start | bytes 3145736 | tf_op jit(solution)/shard_map/ppermute | solution.py:510
  47.3 1.8 %shard_map.43 = (f32[256,768]{1,0:T(8,128)S(1)}, f32[256,768]{1,0:T(8,128)S(1)}) custom-call(s32[1]{0:T(128)} %bitcast.2.pick_ref.refs_1_, bf16[2304,512]{1,0:T(8,128)(2,1)S(1)} %get-tuple-element.47.rows_ref, bf16[2048,512]{1,0:T(8,128)(2,1)S(1)} %get-tuple-element.48.w_ref.w, bf16[2048,512]{1,0:T(8,128)(2,1)S(1)} %get-tuple-element.49.x_ref.x), custom_call_target="tpu_custom_call" | custom-call | flops 1610612736 | bytes 8388608 | tf_op jit(solution)/shard_map/pallas_call | solution.py:226
  49.3 2.2 %collective-permute-done.9.came_ref = f32[256,768]{1,0:T(8,128)S(1)} collective-permute-done((f32[256,768]{1,0:T(8,128)S(1)}, f32[256,768]{1,0:T(8,128)S(1)}, u32[]{:S(2)}, u32[]{:S(2)}) %collective-permute-start.9) | collective-permute-done | bytes 786464 | tf_op jit(solution)/shard_map/ppermute | solution.py:520
  52.6 4.4 %collective-permute-done.13.left = bf16[2048,256]{1,0:T(8,128)(2,1)S(1)} collective-permute-done((bf16[2048,256]{1,0:T(8,128)(2,1)S(1)}, bf16[2048,256]{1,0:T(8,128)(2,1)S(1)}, u32[]{:S(2)}, u32[]{:S(2)}) %collective-permute-start.13) | collective-permute-done | bytes 1048608 | tf_op jit(solution)/shard_map/ppermute | solution.py:474
  57.0 7.2 %collective-permute-start.10 = (s16[272,768]{1,0:T(8,128)(2,1)}, s16[272,768]{1,0:T(8,128)(2,1)S(1)}, u32[]{:S(2)}, u32[]{:S(2)}) collective-permute-start(s16[272,768]{1,0:T(8,128)(2,1)} %get-tuple-element.53), channel_id=1, source_target_pairs={{0,8},{16,24},{9,1},{25,17},{18,26},{2,10},{27,19},{11,3},{28,20},... | collective-permute-start | bytes 1253384 | tf_op jit(solution)/shard_map/ppermute | solution.py:525
  64.3 2.7 %shard_map.47 = (f32[256,768]{1,0:T(8,128)S(1)}, s16[272,768]{1,0:T(8,128)(2,1)}) custom-call(s32[1]{0:T(128)} %bitcast.2.pick_ref.refs_1_, bf16[2048,256]{1,0:T(8,128)(2,1)S(1)} %collective-permute-done.13.left, bf16[2048,256]{1,0:T(8,128)(2,1)S(1)} %collective-permute-done.14.left_too, bf16[2048,512]{1,0:T(8,128)(2,1)S(1)} %get-tuple-element.48.w_ref.w, ...), custom_call_target="tpu_custom_call" | custom-call | flops 1610612736 | bytes 8388608 | tf_op jit(solution)/shard_map/pallas_call | solution.py:308
  67.0 1.3 %collective-permute-start.17 = (s16[272,768]{1,0:T(8,128)(2,1)}, s16[272,768]{1,0:T(8,128)(2,1)S(1)}, u32[]{:S(2)}, u32[]{:S(2)}) collective-permute-start(s16[272,768]{1,0:T(8,128)(2,1)} %get-tuple-element.61), channel_id=1, source_target_pairs={{24,16},{8,0},{17,25},{1,9},{10,2},{26,18},{3,11},{19,27},{4,12},{... | collective-permute-start | bytes 1253384 | tf_op jit(solution)/shard_map/ppermute | solution.py:525
  70.5 12.6 %collective-permute-done.5.came_ref = s16[272,512]{1,0:T(8,128)(2,1)S(1)} collective-permute-done((s16[272,512]{1,0:T(8,128)(2,1)}, s16[272,512]{1,0:T(8,128)(2,1)S(1)}, u32[]{:S(2)}, u32[]{:S(2)}) %collective-permute-start.5) | collective-permute-done | bytes 278560 | tf_op jit(solution)/shard_map/ppermute | solution.py:515
  89.6 6.2 %collective-permute-start.18 = (s16[272,512]{1,0:T(8,128)(2,1)}, s16[272,512]{1,0:T(8,128)(2,1)S(1)}, u32[]{:S(2)}, u32[]{:S(2)}) collective-permute-start(s16[272,512]{1,0:T(8,128)(2,1)} %get-tuple-element.63), channel_id=1, source_target_pairs={{0,16},{9,25},{18,2},{27,11},{28,12},{21,5},{14,30},{7,23},{16,17}... | collective-permute-start | bytes 835592 | tf_op jit(solution)/shard_map/ppermute | solution.py:528
  96.5 4.9 %collective-permute-start.19 = (s16[272,256]{1,0:T(8,128)(2,1)S(1)}, s16[272,256]{1,0:T(8,128)(2,1)S(1)}, u32[]{:S(2)}, u32[]{:S(2)}) collective-permute-start(s16[272,256]{1,0:T(8,128)(2,1)S(1)} %get-tuple-element.64), channel_id=1, source_target_pairs={{0,17},{9,24},{18,3},{27,10},{28,14},{21,7},{14,28},{7,21}} | collective-permute-start | bytes 417800 | tf_op jit(solution)/shard_map/ppermute | solution.py:529
  101.4 2.8 %collective-permute-done.6.own_came = s16[272,512]{1,0:T(8,128)(2,1)} collective-permute-done((s16[272,512]{1,0:T(8,128)(2,1)}, s16[272,512]{1,0:T(8,128)(2,1)}, u32[]{:S(2)}, u32[]{:S(2)}) %collective-permute-start.6) | collective-permute-done | bytes 278560 | tf_op jit(solution)/shard_map/ppermute | solution.py:517
  104.3 1.8 %close.1 = f32[256,512]{1,0:T(8,128)} custom-call(s32[1]{0:T(128)} %bitcast.case_ref, f32[256,512]{1,0:T(8,128)S(1)} %get-tuple-element.43.own, s16[272,512]{1,0:T(8,128)(2,1)} %collective-permute-done.6.own_came, f32[256,512]{1,0:T(8,128)S(1)} %get-tuple-element.54.near1, s16[272,512]{1,0:T(8,128)(2,1)S(1)} %collective-permute-done.11.leg1, ...), custom_call_target="tpu_custom_call" | custom-call | tf_op jit(solution)/shard_map/close/pallas_call | solution.py:382
  (37 shorter events, 13.4 us)
Async XLA Ops:
  0.0 14.7 %copy-start.2 = (s32[32,16]{0,1:T(8,128)S(1)}, s32[32,16]{0,1:T(8,128)}, u32[]{:S(2)}) copy-start(s32[32,16]{0,1:T(8,128)} %param.4) | copy-start | bytes 6148
  1.0 6.5 %collective-permute-start = (bf16[256,256]{1,0:T(8,128)(2,1)S(1)}, bf16[256,256]{1,0:T(8,128)(2,1)S(1)}, u32[]{:S(2)}, u32[]{:S(2)}) collective-permute-start(bf16[256,256]{1,0:T(8,128)(2,1)S(1)} %get-tuple-element.35.refs_0_), channel_id=1, source_target_pairs={{0,1},{1,0},{2,3},{3,2},{4,5},{5,4},{6,7},{7,6},{8,9},{9,8},{10,11... | collective-permute-start | bytes 393224 | tf_op jit(solution)/shard_map/ppermute | solution.py:452
  4.0 5.0 %collective-permute-start.1 = (bf16[256,256]{1,0:T(8,128)(2,1)S(1)}, bf16[256,256]{1,0:T(8,128)(2,1)S(1)}, u32[]{:S(2)}, u32[]{:S(2)}) collective-permute-start(bf16[256,256]{1,0:T(8,128)(2,1)S(1)} %get-tuple-element.36.refs_1_), channel_id=1, source_target_pairs={{0,2},{1,3},{2,0},{3,1},{4,6},{5,7},{6,4},{7,5},{8,10},{9,11},{10,... | collective-permute-start | bytes 393224 | tf_op jit(solution)/shard_map/ppermute | solution.py:455
  9.0 5.6 %collective-permute-start.2 = (bf16[128,1024]{1,0:T(8,128)(2,1)S(1)}, bf16[128,1024]{1,0:T(8,128)(2,1)S(1)}, u32[]{:S(2)}, u32[]{:S(2)}) collective-permute-start(bf16[128,1024]{1,0:T(8,128)(2,1)S(1)} %get-tuple-element.37), channel_id=1, source_target_pairs={{0,4},{4,0},{8,12},{12,8},{16,20},{20,16},{24,28},{28,24},{1,5},{5... | collective-permute-start | bytes 786440 | tf_op jit(solution)/shard_map/ppermute | solution.py:472
  9.1 5.6 %collective-permute-start.3 = (bf16[128,1024]{1,0:T(8,128)(2,1)S(1)}, bf16[128,1024]{1,0:T(8,128)(2,1)S(1)}, u32[]{:S(2)}, u32[]{:S(2)}) collective-permute-start(bf16[128,1024]{1,0:T(8,128)(2,1)S(1)} %get-tuple-element.38), channel_id=1, source_target_pairs={{4,8},{8,4},{12,16},{16,12},{20,24},{24,20},{5,9},{9,5},{13,17},{1... | collective-permute-start | bytes 786440 | tf_op jit(solution)/shard_map/ppermute | solution.py:471
  12.5 21.5 %collective-permute-start.7 = (bf16[1792,256]{1,0:T(8,128)(2,1)}, bf16[1792,256]{1,0:T(8,128)(2,1)S(1)}, u32[]{:S(2)}, u32[]{:S(2)}) collective-permute-start(bf16[1792,256]{1,0:T(8,128)(2,1)} %get-tuple-element.45), channel_id=1, source_target_pairs={{0,1},{1,0},{2,3},{3,2},{4,5},{5,4},{6,7},{7,6},{8,9},{9,8},{10,11... | collective-permute-start | bytes 2752520 | tf_op jit(solution)/shard_map/ppermute | solution.py:452
  13.0 21.7 %collective-permute-start.8 = (bf16[1792,256]{1,0:T(8,128)(2,1)}, bf16[1792,256]{1,0:T(8,128)(2,1)}, u32[]{:S(2)}, u32[]{:S(2)}) collective-permute-start(bf16[1792,256]{1,0:T(8,128)(2,1)} %get-tuple-element.46), channel_id=1, source_target_pairs={{0,2},{1,3},{2,0},{3,1},{4,6},{5,7},{6,4},{7,5},{8,10},{9,11},{10,... | collective-permute-start | bytes 2752520 | tf_op jit(solution)/shard_map/ppermute | solution.py:455
  24.7 39.6 %collective-permute-start.15 = (bf16[2048,512]{1,0:T(8,128)(2,1)S(1)}, bf16[2048,512]{1,0:T(8,128)(2,1)S(1)}, u32[]{:S(2)}, u32[]{:S(2)}) collective-permute-start(bf16[2048,512]{1,0:T(8,128)(2,1)S(1)} %get-tuple-element.48.w_ref.w), channel_id=1, source_target_pairs={{0,4},{4,0},{8,12},{12,8},{16,20},{20,16},{24,28},{28,24},{1,5},{5... | collective-permute-start | bytes 6291464 | tf_op jit(solution)/shard_map/ppermute | solution.py:509
  29.3 27.7 %collective-permute-start.13 = (bf16[2048,256]{1,0:T(8,128)(2,1)S(1)}, bf16[2048,256]{1,0:T(8,128)(2,1)S(1)}, u32[]{:S(2)}, u32[]{:S(2)}) collective-permute-start(bf16[2048,256]{1,0:T(8,128)(2,1)S(1)} %get-tuple-element.57), channel_id=1, source_target_pairs={{0,2},{1,3},{2,0},{3,1},{4,5},{5,4},{6,7},{7,6},{8,10},{9,11},{10,... | collective-permute-start | bytes 3145736 | tf_op jit(solution)/shard_map/ppermute | solution.py:474
  30.9 33.3 %collective-permute-start.14 = (bf16[2048,256]{1,0:T(8,128)(2,1)S(1)}, bf16[2048,256]{1,0:T(8,128)(2,1)S(1)}, u32[]{:S(2)}, u32[]{:S(2)}) collective-permute-start(bf16[2048,256]{1,0:T(8,128)(2,1)S(1)} %get-tuple-element.58), channel_id=1, source_target_pairs={{0,5},{1,4},{2,7},{3,6},{4,2},{5,3},{6,0},{7,1},{8,13},{9,12},{10,... | collective-permute-start | bytes 3145736 | tf_op jit(solution)/shard_map/ppermute | solution.py:475
  43.5 20.7 %collective-permute-start.16 = (bf16[2048,256]{1,0:T(8,128)(2,1)S(1)}, bf16[2048,256]{1,0:T(8,128)(2,1)S(1)}, u32[]{:S(2)}, u32[]{:S(2)}) collective-permute-start(bf16[2048,256]{1,0:T(8,128)(2,1)S(1)} %get-tuple-element.59), channel_id=1, source_target_pairs={{0,4},{4,0},{8,12},{12,8},{16,20},{20,16},{24,28},{28,24},{1,5},{5... | collective-permute-start | bytes 3145736 | tf_op jit(solution)/shard_map/ppermute | solution.py:510
  49.2 2.4 %collective-permute-start.9 = (f32[256,768]{1,0:T(8,128)S(1)}, f32[256,768]{1,0:T(8,128)S(1)}, u32[]{:S(2)}, u32[]{:S(2)}) collective-permute-start(f32[256,768]{1,0:T(8,128)S(1)} %get-tuple-element.51), channel_id=1, source_target_pairs={{0,4},{4,0},{8,12},{12,8},{16,20},{20,16},{24,28},{28,24},{1,5},{5... | collective-permute-start | bytes 2359304 | tf_op jit(solution)/shard_map/ppermute | solution.py:520
  51.5 16.8 %collective-permute-start.4 = (f32[256,512]{1,0:T(8,128)S(1)}, f32[256,512]{1,0:T(8,128)S(1)}, u32[]{:S(2)}, u32[]{:S(2)}) collective-permute-start(f32[256,512]{1,0:T(8,128)S(1)} %get-tuple-element.40), channel_id=1, source_target_pairs={{0,4},{4,0},{8,12},{12,8},{16,20},{20,16},{24,28},{28,24},{1,5},{5... | collective-permute-start | bytes 1572872 | tf_op jit(solution)/shard_map/ppermute | solution.py:513
  57.0 30.0 %collective-permute-start.10 = (s16[272,768]{1,0:T(8,128)(2,1)}, s16[272,768]{1,0:T(8,128)(2,1)S(1)}, u32[]{:S(2)}, u32[]{:S(2)}) collective-permute-start(s16[272,768]{1,0:T(8,128)(2,1)} %get-tuple-element.53), channel_id=1, source_target_pairs={{0,8},{16,24},{9,1},{25,17},{18,26},{2,10},{27,19},{11,3},{28,20},... | collective-permute-start | bytes 1253384 | tf_op jit(solution)/shard_map/ppermute | solution.py:525
  67.0 21.7 %collective-permute-start.17 = (s16[272,768]{1,0:T(8,128)(2,1)}, s16[272,768]{1,0:T(8,128)(2,1)S(1)}, u32[]{:S(2)}, u32[]{:S(2)}) collective-permute-start(s16[272,768]{1,0:T(8,128)(2,1)} %get-tuple-element.61), channel_id=1, source_target_pairs={{24,16},{8,0},{17,25},{1,9},{10,2},{26,18},{3,11},{19,27},{4,12},{... | collective-permute-start | bytes 1253384 | tf_op jit(solution)/shard_map/ppermute | solution.py:525
  69.2 13.9 %collective-permute-start.5 = (s16[272,512]{1,0:T(8,128)(2,1)}, s16[272,512]{1,0:T(8,128)(2,1)S(1)}, u32[]{:S(2)}, u32[]{:S(2)}) collective-permute-start(s16[272,512]{1,0:T(8,128)(2,1)} %get-tuple-element.42), channel_id=1, source_target_pairs={{8,0},{24,16},{1,9},{17,25},{26,18},{10,2},{19,27},{3,11},{12,4},{... | collective-permute-start | bytes 835592 | tf_op jit(solution)/shard_map/ppermute | solution.py:515
  83.1 0.7 copy-start
  83.8 1.0 copy-start.1
  85.7 18.6 %collective-permute-start.6 = (s16[272,512]{1,0:T(8,128)(2,1)}, s16[272,512]{1,0:T(8,128)(2,1)}, u32[]{:S(2)}, u32[]{:S(2)}) collective-permute-start(s16[272,512]{1,0:T(8,128)(2,1)} %get-tuple-element.44), channel_id=1, source_target_pairs={{16,0},{25,9},{2,18},{11,27},{20,4},{29,13},{6,22},{15,31}} | collective-permute-start | bytes 835592 | tf_op jit(solution)/shard_map/ppermute | solution.py:517
  88.0 16.3 %collective-permute-start.11 = (s16[272,512]{1,0:T(8,128)(2,1)}, s16[272,512]{1,0:T(8,128)(2,1)S(1)}, u32[]{:S(2)}, u32[]{:S(2)}) collective-permute-start(s16[272,512]{1,0:T(8,128)(2,1)} %get-tuple-element.55), channel_id=1, source_target_pairs={{24,8},{17,1},{10,26},{3,19},{4,20},{13,29},{22,6},{31,15},{8,10},... | collective-permute-start | bytes 835592 | tf_op jit(solution)/shard_map/ppermute | solution.py:528
  89.6 14.6 %collective-permute-start.18 = (s16[272,512]{1,0:T(8,128)(2,1)}, s16[272,512]{1,0:T(8,128)(2,1)S(1)}, u32[]{:S(2)}, u32[]{:S(2)}) collective-permute-start(s16[272,512]{1,0:T(8,128)(2,1)} %get-tuple-element.63), channel_id=1, source_target_pairs={{0,16},{9,25},{18,2},{27,11},{28,12},{21,5},{14,30},{7,23},{16,17}... | collective-permute-start | bytes 835592 | tf_op jit(solution)/shard_map/ppermute | solution.py:528
  95.8 8.4 %collective-permute-start.12 = (s16[272,256]{1,0:T(8,128)(2,1)}, s16[272,256]{1,0:T(8,128)(2,1)S(1)}, u32[]{:S(2)}, u32[]{:S(2)}) collective-permute-start(s16[272,256]{1,0:T(8,128)(2,1)} %get-tuple-element.56), channel_id=1, source_target_pairs={{24,10},{17,3},{10,24},{3,17},{4,21},{13,28},{22,7},{31,14}} | collective-permute-start | bytes 417800 | tf_op jit(solution)/shard_map/ppermute | solution.py:529
  96.5 7.8 %collective-permute-start.19 = (s16[272,256]{1,0:T(8,128)(2,1)S(1)}, s16[272,256]{1,0:T(8,128)(2,1)S(1)}, u32[]{:S(2)}, u32[]{:S(2)}) collective-permute-start(s16[272,256]{1,0:T(8,128)(2,1)S(1)} %get-tuple-element.64), channel_id=1, source_target_pairs={{0,17},{9,24},{18,3},{27,10},{28,14},{21,7},{14,28},{7,21}} | collective-permute-start | bytes 417800 | tf_op jit(solution)/shard_map/ppermute | solution.py:529
